TPU v7x, 32 devices: a whole 2x2x4 slice. The times are simulated.
32 devices in a mesh: leaf: 16 (over z, y, x), head: 2 (over core).
Axes of the slice: x: 2, y: 2, z: 4, core: 2. Of those that a mesh axis runs over, the one named last changes fastest.
Arguments:
- queries: bfloat16 [2048, 16, 576], P('leaf', 'head'), may hold values from -40 to 40
- leaf_latent: bfloat16 [2048, 576], P('leaf'), may hold values from -4 to 4
- node_latent: bfloat16 [16, 96, 576], P('leaf', 'head'), may hold values from -4 to 4
- grad_out: bfloat16 [2048, 16, 512], P('leaf', 'head'), may hold values from -6 to 6
- leaf_nodes: int32 [32, 3], P('leaf'), may hold values from 0 to 15, as said below
- leaf_lengths: int32 [32], P('leaf'), may hold values from 1 to 64, 1280 in all
Outputs:
- attention: bfloat16 [2048, 16, 512], P('leaf', 'head')
- node_grad: bfloat16 [16, 96, 576], P('leaf', 'head')
- leaf_grad: bfloat16 [2048, 576], P('leaf')
Inputs may be any that keep to these rules, and one draw needn't show every extreme that they name: `leaf_nodes`: each row lists three different nodes: a root, one of its children and one of that child's children. Every node has one level and one parent; which nodes are used and how often varies.
All inputs are finite; a program needn't handle non-finite values. No bound on the sum of `leaf_lengths` on one device may be relied on, other than what follows from the above.
Results may differ from a plain program's by a relative error of at most 0.0095.
Values may be sent and summed in bfloat16 or wider, within the bound.
No kernel may reach another device: no remote copies, remote signals or barrier semaphores. Data moves between devices by JAX's collectives and lax.ppermute only.
A program may use at most 64 MiB of HBM per device.

v0:
```python
import jax
import jax.numpy as jnp
from jax import lax
from jax.sharding import PartitionSpec as P

LAT = 512
NODE_ROWS = 96


score_scale = 192.0 ** (-0.5)


def body(queries, leaf_latent, node_latent, grad_out, leaf_nodes, leaf_lengths):
    rows, heads, width = queries.shape
    leaves = leaf_nodes.shape[0]
    leaf_rows = rows // leaves
    slices = lax.all_gather(node_latent, "leaf", axis=0, tiled=True)
    total_nodes = slices.shape[0]
    node_ids = leaf_nodes.reshape(-1)
    picker = (node_ids[:, None] == jnp.arange(total_nodes, dtype=jnp.int32)[None, :]).astype(
        jnp.bfloat16
    )
    chosen = jnp.dot(picker, slices.reshape(total_nodes, -1), preferred_element_type=jnp.float32)
    chosen = chosen.astype(jnp.bfloat16).reshape(leaves * 3, -1, width)
    whole_nodes = lax.all_gather(chosen, "head", axis=1, tiled=True)
    node_keys = whole_nodes.reshape(leaves, 3 * NODE_ROWS, width)
    keys = jnp.concatenate([node_keys, leaf_latent.reshape(leaves, leaf_rows, width)], axis=1)
    values = keys[:, :, :LAT]
    total_keys = keys.shape[1]
    query = queries.reshape(leaves, leaf_rows * heads, width)
    row_of = jnp.arange(leaf_rows * heads, dtype=jnp.int32) // heads
    key_index = jnp.arange(total_keys, dtype=jnp.int32)
    visible = (key_index[None, :] < 3 * NODE_ROWS) | (
        key_index[None, :] - 3 * NODE_ROWS <= row_of[:, None]
    )
    live = (row_of[None, :] < leaf_lengths[:, None]).astype(jnp.float32)[..., None]
    scores = (
        jnp.einsum("lqc,lkc->lqk", query, keys, preferred_element_type=jnp.float32) * score_scale
    )
    scores = jnp.where(visible[None], scores, -jnp.inf)
    top = jnp.max(scores, axis=-1, keepdims=True)
    expo = jnp.exp(scores - top)
    probs = expo / jnp.sum(expo, axis=-1, keepdims=True)
    probs_b = probs.astype(jnp.bfloat16)
    outputs = jnp.einsum("lqk,lkc->lqc", probs_b, values, preferred_element_type=jnp.float32)
    attention = (outputs * live).astype(jnp.bfloat16).reshape(rows, heads, LAT)
    masked_f = grad_out.reshape(leaves, leaf_rows * heads, LAT).astype(jnp.float32) * live
    masked = masked_f.astype(jnp.bfloat16)
    dprobs = jnp.einsum("lqc,lkc->lqk", masked, values, preferred_element_type=jnp.float32)
    delta = jnp.sum(masked_f * outputs, axis=-1)
    dscores = (score_scale * probs * (dprobs - delta[..., None])).astype(jnp.bfloat16)
    grad_keys = jnp.einsum("lqk,lqc->lkc", dscores, query, preferred_element_type=jnp.float32)
    grad_values = jnp.einsum("lqk,lqc->lkc", probs_b, masked, preferred_element_type=jnp.float32)
    grad_keys = jnp.concatenate(
        [grad_keys[:, :, :LAT] + grad_values, grad_keys[:, :, LAT:]], axis=2
    )
    node_terms = grad_keys[:, : 3 * NODE_ROWS].reshape(leaves * 3, NODE_ROWS, width)
    own_terms = grad_keys[:, 3 * NODE_ROWS :].reshape(rows, width)
    head_shares = lax.psum_scatter(node_terms, "head", scatter_dimension=1, tiled=True)
    owned = node_latent.shape[0]
    spread = jnp.dot(
        picker.T.astype(jnp.float32),
        head_shares.reshape(leaves * 3, -1),
        precision=lax.Precision.HIGHEST,
    )
    arrived = lax.all_to_all(spread, "leaf", split_axis=0, concat_axis=0, tiled=True)
    mine = jnp.sum(arrived.reshape(-1, owned, arrived.shape[1]), axis=0)
    node_grad = mine.reshape(node_latent.shape).astype(jnp.bfloat16)
    leaf_grad = lax.psum(own_terms, "head").astype(jnp.bfloat16)
    return (attention, node_grad, leaf_grad)


def solution(mesh):
    return jax.shard_map(
        body,
        mesh=mesh,
        in_specs=(
            P("leaf", "head", None),
            P("leaf", None),
            P("leaf", "head", None),
            P("leaf", "head", None),
            P("leaf", None),
            P("leaf"),
        ),
        out_specs=(P("leaf", "head", None), P("leaf", "head", None), P("leaf", None)),
        check_vma=False,
    )
```

profile of v0, /device:TPU:12, one launch (start us, length us, event | category | flops | bytes accessed | tf_op | source)
XLA Modules:
  0.0 151.8 jit_solution(2849219030837386049)
XLA Ops:
  7.2 0.8 eq.15
  8.0 1.1 copy.22
  9.1 0.9 copy.24
  9.9 38.9 %all_gather.6 = bf16[16,48,576]{2,1,0:T(8,128)(2,1)S(1)} all-gather(bf16[1,48,576]{2,1,0:T(8,128)(2,1)} %param.8), channel_id=1, replica_groups=mesh['leaf'=16,'head'=2] {'leaf'}, dimensions={0}, use_global_device_ids=true | all-gather | bytes 940032 | tf_op jit(solution)/shard_map/all_gather | solution.py:17
  48.9 0.9 reshape.166
  49.8 0.3 convolution_convert_fusion
  50.1 0.3 reshape.167
  50.5 2.5 %all_gather.7 = bf16[6,96,576]{2,1,0:T(8,128)(2,1)S(1)} all-gather(bf16[6,48,576]{2,1,0:T(8,128)(2,1)S(1)} %reshape.167), channel_id=1, replica_groups=mesh['leaf'=16,'head'=2] {'head'}, dimensions={1}, use_global_device_ids=true | all-gather | bytes 995328 | tf_op jit(solution)/shard_map/all_gather | solution.py:25
  52.9 1.2 copy.23
  54.2 1.3 copy.25
  55.6 0.2 compare_or_fusion
  55.8 2.6 %fusion.8 = f32[2,512,352]{1,2,0:T(8,128)S(1)} fusion(bf16[2,512,576]{2,1,0:T(8,128)(2,1)S(1)} %bitcast.28, bf16[2,64,576]{1,2,0:T(8,128)(2,1)} %copy.24, bf16[2,288,576]{1,2,0:T(8,128)(2,1)} %copy.23, pred[512,352]{0,1:T(8,128)(4,1)S(1)} %compare_or_fusion), kind=kOutput, calls=%fused_computation.16 | convolution fusion | flops 417579008 | bytes 3612672 | tf_op jit(solution)/shard_map/lqc,lkc->lqk/dot_general | solution.py:38
  58.4 1.4 fusion.30
  59.8 2.2 %fusion.17 = f32[2,512,512]{2,1,0:T(8,128)S(1)} fusion(bf16[2,64,576]{1,2,0:T(8,128)(2,1)} %copy.24, bf16[2,288,576]{1,2,0:T(8,128)(2,1)} %copy.23, f32[2,512]{1,0:T(2,128)S(1)} %get-tuple-element.12, f32[2,512,352]{1,2,0:T(8,128)S(1)} %fusion.8), kind=kOutput, calls=%fused_computation.29 | convolution fusion | flops 371623264 | bytes 4354048 | tf_op jit(solution)/shard_map/lqk,lkc->lqc/dot_general | solution.py:45
  62.0 3.0 %fusion.3 = (f32[2,512]{1,0:T(2,128)S(1)}, bf16[2,512,512]{2,1,0:T(8,128)(2,1)}, bf16[2,512,512]{2,1,0:T(8,128)(2,1)}) fusion(f32[2,512,512]{2,1,0:T(8,128)S(1)} %fusion.17, f32[2,512]{1,0:T(2,128)S(1)} %compare_convert_fusion, bf16[2,512,512]{2,1,0:T(8,128)(2,1)} %bitcast.31), kind=kLoop, calls=%fused_computation.6 | loop fusion | flops 3668992 | bytes 5251072 | tf_op jit(solution)/shard_map/reduce_sum | solution.py:50
  65.0 5.2 %fusion.10 = f32[2,352,576]{1,2,0:T(8,128)} fusion(bf16[2,512,576]{2,1,0:T(8,128)(2,1)} %bitcast.29, bf16[2,512,512]{2,1,0:T(8,128)(2,1)} %get-tuple-element.11, f32[2,512]{1,0:T(2,128)S(1)} %get-tuple-element.9, f32[2,512,352]{1,2,0:T(8,128)} %get-tuple-element.13, f32[2,512]{1,0:T(2,128)S(1)} %get-tuple-element.12, bf16[2,64,576]{1,2,0:T(8,128)(2,1)} %copy.24, ...), kind=kOutput, calls=%fused_computation.18 | convolution fusion | flops 787578880 | bytes 6111232 | tf_op jit(solution)/shard_map/lqk,lqc->lkc/dot_general | solution.py:52
  70.2 2.5 %slice_add_fusion = f32[2,352,512]{1,2,0:T(8,128)S(1)} fusion(f32[2,352,576]{1,2,0:T(8,128)} %fusion.10, bf16[2,512,512]{2,1,0:T(8,128)(2,1)} %get-tuple-element.11, f32[2,512]{1,0:T(2,128)S(1)} %get-tuple-element.12, f32[2,512,352]{1,2,0:T(8,128)S(1)} %fusion.8), kind=kOutput, calls=%fused_computation.10 | convolution fusion | flops 370541920 | bytes 6819840 | tf_op jit(solution)/shard_map/lqk,lqc->lkc/dot_general | solution.py:53
  72.7 0.9 slice.21
  73.7 0.1 slice_maximum_fusion
  73.8 1.6 %copy.31 = f32[2,288,576]{2,1,0:T(8,128)} copy(f32[2,288,576]{1,2,0:T(8,128)S(1)} %slice_maximum_fusion) | data formatting | bytes 2654208 | tf_op jit(solution)/shard_map/slice | solution.py:57
  75.5 13.4 %reduce-scatter.2.cloned.1.call-done = f32[6,48,576]{2,1,0:T(8,128)} async-done(((f32[6,96,576]{2,1,0:T(8,128)}), f32[6,48,576]{2,1,0:T(8,128)}) %reduce-scatter.2.cloned.1.call-update) | async-done | bytes 663568 | tf_op jit(solution)/shard_map/reduce_scatter | solution.py:59
  88.9 1.5 reshape.173
  90.4 1.0 convolution_bitcast_fusion
  91.4 3.0 %copy.32 = f32[16,1,27648]{2,1,0:T(1,128)} copy(f32[16,1,27648]{2,0,1:T(8,128)S(1)} %convolution_bitcast_fusion) | data formatting | bytes 3538944 | tf_op jit(solution)/shard_map/all_to_all | solution.py:66
  94.5 7.0 %all-to-all-start = ((f32[16,1,27648]{2,1,0:T(1,128)}), f32[16,1,27648]{2,1,0:T(1,128)S(1)}, u32[]{:S(2)}, u32[]{:S(2)}) async-start(f32[16,1,27648]{2,1,0:T(1,128)} %copy.32), calls=%async_computation.1 | async-start | bytes 3538944 | tf_op jit(solution)/shard_map/all_to_all | solution.py:66
  101.4 1.1 pad_maximum_fusion.1
  102.5 1.3 copy.33
  103.8 4.3 %all-reduce.1 = bf16[128,576]{1,0:T(8,128)(2,1)S(1)} all-reduce(f32[128,576]{1,0:T(8,128)S(1)} %bitcast.30), channel_id=1, replica_groups=mesh['leaf'=16,'head'=2] {'head'}, use_global_device_ids=true, to_apply=%region_5.6 | all-reduce | flops 73728 | bytes 442368 | tf_op jit(solution)/shard_map/psum | solution.py:69
  108.0 0.8 copy.34
  108.8 34.0 %all-to-all-done = f32[16,1,27648]{2,1,0:T(1,128)S(1)} async-done(((f32[16,1,27648]{2,1,0:T(1,128)}), f32[16,1,27648]{2,1,0:T(1,128)S(1)}, u32[]{:S(2)}, u32[]{:S(2)}) %all-to-all-start) | async-done | bytes 1769504 | tf_op jit(solution)/shard_map/all_to_all | solution.py:66
  142.8 1.3 reduce_sum.29
  144.2 0.7 convert_element_type.56
  (12 shorter events, 0.2 us)
Async XLA Ops:
  7.2 81.8 %reduce-scatter.2.cloned.1.call-start = ((), (), s32[]{:S(2)}) async-start(), calls=%async_computation.2 | async-start | bytes 2211840 | tf_op jit(solution)/shard_map/reduce_scatter | solution.py:59
  50.4 3.7 %copy-start.1 = (bf16[128,8,576]{0,2,1:T(8,128)(2,1)S(1)}, bf16[128,8,576]{0,2,1:T(8,128)(2,1)}, u32[]{:S(2)}) copy-start(bf16[128,8,576]{0,2,1:T(8,128)(2,1)} %param.6) | copy-start | bytes 3538948
  54.1 1.4 copy-start.2
  55.5 4.3 %copy-start = (bf16[128,8,576]{2,1,0:T(8,128)(2,1)}, bf16[128,8,576]{2,1,0:T(8,128)(2,1)S(1)}, u32[]{:S(2)}) copy-start(bf16[128,8,576]{2,1,0:T(8,128)(2,1)S(1)} %copy.25) | copy-start | bytes 3538948
  94.5 48.4 %all-to-all-start = ((f32[16,1,27648]{2,1,0:T(1,128)}), f32[16,1,27648]{2,1,0:T(1,128)S(1)}, u32[]{:S(2)}, u32[]{:S(2)}) async-start(f32[16,1,27648]{2,1,0:T(1,128)} %copy.32), calls=%async_computation.1 | async-start | bytes 3538944 | tf_op jit(solution)/shard_map/all_to_all | solution.py:66
Sparse Core Ops, SparseCore 0:
  75.6 13.2 reduce-scatter.1
where the time goes:
time: 152 us
  waiting for transfers between devices  47.4 us (31%)
  blocking collectives  45.7 us (30%)
  local copies, waits for them, and re-layouts  16.4 us (11%)
  between operations  14.2 us (9%)
  matrix products  13.9 us (9%)
  other arithmetic  7.23 us (5%)
  starting transfers between devices  6.99 us (5%)
    all_gather x1, blocking collectives, body(): slices = lax.all_gather(node_latent, 'leaf', axis=0, tiled=True)  38.9 us
    all_to_all x1, waiting for transfers between devices, body(): lax.all_to_all(spread, 'leaf', split_axis=0, concat_axis=0, tiled=True)  34 us
    reduce_scatter x1, waiting for transfers between devices, body(): lax.psum_scatter(node_terms, 'head', scatter_dimension=1, tiled=True)  13.4 us
    all_to_all x1, starting transfers between devices, body(): lax.all_to_all(spread, 'leaf', split_axis=0, concat_axis=0, tiled=True)  6.95 us
    dot_general x1, matrix products, body(): jnp.einsum('lqk,lqc->lkc', dscores, query, preferred_element_type=jnp.flo...  5.17 us
    psum x1, blocking collectives, body(): leaf_grad = lax.psum(own_terms, 'head').astype(jnp.bfloat16)  4.29 us
    unnamed x9, local copies, waits for them, and re-layouts  3.2 us
  transfers between devices with their start and end apart: 2, of which 2 were waited for; matrix products, arithmetic and copies ran while one was open for 2% of the time, Pallas kernels for 0%

commit v1 on v0

v1 whole, which is shorter than its diff:
```python
import functools

import jax
import jax.numpy as jnp
from jax import lax
from jax.experimental import pallas as pl
from jax.experimental.pallas import tpu as pltpu
from jax.sharding import PartitionSpec as P

LAT = 512
LEVELS = 3

score_scale = 192.0 ** (-0.5)

NT = (((1,), (1,)), ((), ()))
NN = (((1,), (0,)), ((), ()))
TN = (((0,), (0,)), ((), ()))


def dot(a, b, dims):
    return lax.dot_general(a, b, dims, preferred_element_type=jnp.float32)


def vmem(count):
    return [pl.BlockSpec(memory_space=pltpu.VMEM)] * count


def cost(flops, moved):
    return pl.CostEstimate(flops=flops, bytes_accessed=moved, transcendentals=0)


def select_kernel(where_ref, table_ref, out_ref):
    for slot in range(out_ref.shape[0]):
        out_ref[slot] = table_ref[where_ref[slot]]


def select(where, table):
    slots = where.shape[0]
    shape = (slots,) + table.shape[1:]
    return pl.pallas_call(
        select_kernel,
        out_shape=jax.ShapeDtypeStruct(shape, table.dtype),
        in_specs=[pl.BlockSpec(memory_space=pltpu.SMEM)] + vmem(1),
        out_specs=vmem(1)[0],
        name="select_nodes",
    )(where, table)


def grads_kernel(parts, leaves, heads, len_ref, own_ref, query_ref, grad_ref, *refs):
    part_refs, refs = refs[:parts], refs[parts:]
    term_refs, refs = refs[:parts], refs[parts:]
    own_grad_ref, probs_ref, keys_ref, key_ref, dscore_ref = refs
    slice_rows, width = part_refs[0].shape[1:]
    leaf_rows = own_ref.shape[0] // leaves
    lines = leaf_rows * heads
    node_rows = LEVELS * parts * slice_rows
    total_keys = node_rows + leaf_rows
    for leaf in range(leaves):
        for part in range(parts):
            for level in range(LEVELS):
                row = (part * LEVELS + level) * slice_rows
                key_ref[row : row + slice_rows, :] = part_refs[part][leaf * LEVELS + level]
        key_ref[node_rows:, :] = own_ref[leaf * leaf_rows : (leaf + 1) * leaf_rows, :]
        keys = key_ref[...]
        keys_ref[leaf] = keys
        query = query_ref[leaf * lines : (leaf + 1) * lines, :]
        grad = grad_ref[leaf * lines : (leaf + 1) * lines, :]
        scores = dot(keys, query, NT) * score_scale
        row_of = lax.broadcasted_iota(jnp.int32, (leaf_rows, lines), 1) // heads
        own_key = lax.broadcasted_iota(jnp.int32, (leaf_rows, lines), 0)
        own_scores = jnp.where(own_key <= row_of, scores[node_rows:], -jnp.inf)
        scores = jnp.concatenate([scores[:node_rows], own_scores], axis=0)
        top = jnp.max(scores, axis=0, keepdims=True)
        expo = jnp.exp(scores - top)
        live = lax.broadcasted_iota(jnp.int32, (1, lines), 1) // heads < len_ref[leaf]
        scale = jnp.where(live, 1.0, 0.0) / jnp.sum(expo, axis=0, keepdims=True)
        probs = expo * scale
        probs_b = probs.astype(jnp.bfloat16)
        probs_ref[leaf] = probs_b
        dprobs = dot(keys[:, :LAT], grad, NT)
        delta = jnp.sum(probs_b.astype(jnp.float32) * dprobs, axis=0, keepdims=True)
        dscore_ref[...] = (score_scale * probs * (dprobs - delta)).astype(jnp.bfloat16)
        dscores = dscore_ref[...]
        head_part = dot(dscores, query[:, :LAT], NN) + dot(probs_ref[leaf], grad, NN)
        tail_part = dot(dscores, query[:, LAT:], NN)
        for part in range(parts):
            for level in range(LEVELS):
                row = (part * LEVELS + level) * slice_rows
                ref = term_refs[part]
                ref[leaf * LEVELS + level, :, :LAT] = head_part[row : row + slice_rows].astype(ref.dtype)
                ref[leaf * LEVELS + level, :, LAT:] = tail_part[row : row + slice_rows].astype(ref.dtype)
        first = leaf * leaf_rows
        own_grad_ref[first : first + leaf_rows, :LAT] = head_part[node_rows:].astype(jnp.bfloat16)
        own_grad_ref[first : first + leaf_rows, LAT:] = tail_part[node_rows:].astype(jnp.bfloat16)


def grads(lengths, own, query, grad, parts, leaves, heads):
    slots, slice_rows, width = parts[0].shape
    rows = own.shape[0]
    lines = rows * heads // leaves
    total_keys = LEVELS * len(parts) * slice_rows + rows // leaves
    outs = [
        jax.ShapeDtypeStruct((slots, slice_rows, width), jnp.float32 if i == 0 else jnp.bfloat16)
        for i in range(len(parts))
    ] + [
        jax.ShapeDtypeStruct((rows, width), jnp.bfloat16),
        jax.ShapeDtypeStruct((leaves, total_keys, lines), jnp.bfloat16),
        jax.ShapeDtypeStruct((leaves, total_keys, width), jnp.bfloat16),
    ]
    return pl.pallas_call(
        functools.partial(grads_kernel, len(parts), leaves, heads),
        out_shape=outs,
        in_specs=[pl.BlockSpec(memory_space=pltpu.SMEM)] + vmem(3 + len(parts)),
        out_specs=vmem(len(outs)),
        scratch_shapes=[
            pltpu.VMEM((total_keys, width), jnp.bfloat16),
            pltpu.VMEM((total_keys, lines), jnp.bfloat16),
        ],
        compiler_params=pltpu.CompilerParams(vmem_limit_bytes=40 << 20),
        cost_estimate=cost(2 * rows * heads * total_keys * 4 * width, 8 << 20),
        name="attend_grads",
    )(lengths, own, query, grad, *parts)


def outputs_kernel(leaves, probs_ref, keys_ref, out_ref):
    lines = probs_ref.shape[2]
    for leaf in range(leaves):
        out = dot(probs_ref[leaf], keys_ref[leaf, :, :LAT], TN)
        out_ref[leaf * lines : (leaf + 1) * lines, :] = out.astype(jnp.bfloat16)


def outputs(probs, keys):
    leaves, total_keys, lines = probs.shape
    return pl.pallas_call(
        functools.partial(outputs_kernel, leaves),
        out_shape=jax.ShapeDtypeStruct((leaves * lines, LAT), jnp.bfloat16),
        in_specs=vmem(2),
        out_specs=vmem(1)[0],
        compiler_params=pltpu.CompilerParams(vmem_limit_bytes=24 << 20),
        cost_estimate=cost(2 * leaves * total_keys * lines * LAT, 4 << 20),
        name="attend_outputs",
    )(probs, keys)


def spread_kernel(shares, where_ref, *refs):
    share_refs, rest = refs[:shares], refs[shares:]
    keep_ref, send_refs, table_ref = rest[0], rest[1:-1], rest[-1]
    inner = keep_ref.shape[0]
    table_ref[...] = jnp.zeros_like(table_ref)
    for slot in range(share_refs[0].shape[0]):
        total = share_refs[0][slot]
        for ref in share_refs[1:]:
            total = total + ref[slot].astype(jnp.float32)
        table_ref[where_ref[slot]] += total
    keep_ref[...] = table_ref[:inner]
    for i, ref in enumerate(send_refs):
        ref[...] = table_ref[(i + 1) * inner : (i + 2) * inner].astype(jnp.bfloat16)


def spread(where, shares, outer, inner):
    block = shares[0].shape[1:]
    outs = [jax.ShapeDtypeStruct((inner,) + block, jnp.float32)] + [
        jax.ShapeDtypeStruct((inner,) + block, jnp.bfloat16)
    ] * (outer - 1)
    return pl.pallas_call(
        functools.partial(spread_kernel, len(shares)),
        out_shape=outs,
        in_specs=[pl.BlockSpec(memory_space=pltpu.SMEM)] + vmem(len(shares)),
        out_specs=vmem(len(outs)),
        scratch_shapes=[pltpu.VMEM((outer * inner,) + block, jnp.float32)],
        compiler_params=pltpu.CompilerParams(vmem_limit_bytes=40 << 20),
        name="spread_terms",
    )(where, *shares)


def merge_kernel(count, *refs):
    keep_ref, got_refs, out_refs = refs[0], refs[1:count], refs[count:]
    for i, ref in enumerate(out_refs):
        total = keep_ref[i]
        for got in got_refs:
            total = total + got[i].astype(jnp.float32)
        ref[0] = total.astype(ref.dtype)


def merge(keep, got):
    inner = keep.shape[0]
    block = (1,) + keep.shape[1:]
    outs = [jax.ShapeDtypeStruct(block, jnp.float32)] + [
        jax.ShapeDtypeStruct(block, jnp.bfloat16)
    ] * (inner - 1)
    return pl.pallas_call(
        functools.partial(merge_kernel, 1 + len(got)),
        out_shape=outs,
        in_specs=vmem(1 + len(got)),
        out_specs=vmem(len(outs)),
        compiler_params=pltpu.CompilerParams(vmem_limit_bytes=40 << 20),
        name="merge_terms",
    )(keep, *got)


def body(leaf_size, head_size, queries, leaf_latent, node_latent, grad_out, leaf_nodes, leaf_lengths):
    rows, heads, width = queries.shape
    leaves = leaf_nodes.shape[0]
    side = 1
    while side * side < leaf_size:
        side *= 2
    axes = ("leaf", "head")

    def step(value, which, distance):
        pairs = []
        for leaf in range(leaf_size):
            for head in range(head_size):
                far = (which + head) % 2 == 0
                target = leaf ^ (distance * side if far else distance)
                pairs.append((leaf * head_size + head, target * head_size + head))
        return lax.ppermute(value, axes, pairs)

    def swap(value, distance):
        return lax.ppermute(value, "head", [(i, i ^ distance) for i in range(head_size)])

    relative = leaf_nodes.reshape(-1) ^ lax.axis_index("leaf")
    far, near = relative // side, relative % side
    even = lax.axis_index("head") % 2 == 0
    where = jnp.where(even, near * side + far, far * side + near)

    inner = jnp.concatenate([node_latent] + [step(node_latent, 0, d) for d in range(1, side)], axis=0)
    table = jnp.concatenate([inner] + [step(inner, 1, d) for d in range(1, side)], axis=0)
    mine = select(where, table)
    parts = [mine] + [swap(mine, d) for d in range(1, head_size)]

    query = queries.reshape(rows * heads, width)
    grad = grad_out.reshape(rows * heads, LAT)
    results = grads(leaf_lengths, leaf_latent, query, grad, parts, leaves, heads)
    terms, (own_grad, probs, keys) = results[:head_size], results[head_size:]

    shares = [terms[0]] + [swap(terms[d], d) for d in range(1, head_size)]
    keep, *sends = spread(where, shares, side, side)
    got = [step(send, 1, d + 1) for d, send in enumerate(sends)]
    attention = outputs(probs, keys).reshape(rows, heads, LAT)
    keep, *sends = merge(keep, got)
    total = keep
    for d, send in enumerate(sends):
        total = total + step(send, 0, d + 1).astype(jnp.float32)
    node_grad = total.astype(jnp.bfloat16)

    leaf_grad = own_grad
    distance = 1
    while distance < head_size:
        leaf_grad = leaf_grad + swap(leaf_grad, distance)
        distance *= 2
    return (attention, node_grad, leaf_grad)


def solution(mesh):
    return jax.shard_map(
        functools.partial(body, mesh.shape["leaf"], mesh.shape["head"]),
        mesh=mesh,
        in_specs=(
            P("leaf", "head", None),
            P("leaf", None),
            P("leaf", "head", None),
            P("leaf", "head", None),
            P("leaf", None),
            P("leaf"),
        ),
        out_specs=(P("leaf", "head", None), P("leaf", "head", None), P("leaf", None)),
        check_vma=False,
    )
```

time: 152 us -> 57.1 us (0.38)
  the two profiles are of different devices: /device:TPU:12 before, /device:TPU:9 now
where the time goes in v1:
time: 57.1 us; the launch traced here: 56.9 us
  waiting for transfers between devices  26.5 us (46%)
  starting transfers between devices  14.6 us (26%)
  Pallas kernels  7.82 us (14%)
  local copies, waits for them, and re-layouts  5.31 us (9%)
  other arithmetic  1.91 us (3%)
  between operations  0.81 us (1%)
    ppermute x12, waiting for transfers between devices, step(): return lax.ppermute(value, axes, pairs)  25.2 us
    ppermute x12, starting transfers between devices, step(): return lax.ppermute(value, axes, pairs)  13.9 us
    unnamed x20, local copies, waits for them, and re-layouts  5.18 us
    pallas_call x1, Pallas kernels, grads(): pl.pallas_call(functools.partial(grads_kernel, len(parts), leaves, heads)...  3.14 us
    pallas_call x1, Pallas kernels, select(): pl.pallas_call(select_kernel, out_shape=jax.ShapeDtypeStruct(shape, table...  1.99 us
    pallas_call x1, Pallas kernels, outputs(): pl.pallas_call(functools.partial(outputs_kernel, leaves), out_shape=jax.S...  1.72 us
    ppermute x3, waiting for transfers between devices, swap(): lax.ppermute(value, 'head', [(i, i ^ distance) for i in range(head_size)])  1.32 us
  transfers between devices with their start and end apart: 15, of which 9 were waited for; matrix products, arithmetic and copies ran while one was open for 10% of the time, Pallas kernels for 3%

profile of v1, /device:TPU:9, one launch (start us, length us, event | category | flops | bytes accessed | tf_op | source)
XLA Modules:
  0.0 56.9 jit_solution(2147509149199835601)
XLA Ops:
  0.6 1.3 %collective-permute-start.1 = (bf16[1,48,576]{2,1,0:T(8,128)(2,1)}, bf16[1,48,576]{2,1,0:T(8,128)(2,1)S(1)}, u32[]{:S(2)}, u32[]{:S(2)}) collective-permute-start(bf16[1,48,576]{2,1,0:T(8,128)(2,1)} %param.8), channel_id=1, source_target_pairs={{0,16},{1,5},{2,18},{3,7},{4,20},{5,1},{6,22},{7,3},{8,24},{9,13},... | collective-permute-start | bytes 165896 | tf_op jit(solution)/shard_map/ppermute | solution.py:216
  1.9 1.2 %collective-permute-start = (bf16[1,48,576]{2,1,0:T(8,128)(2,1)}, bf16[1,48,576]{2,1,0:T(8,128)(2,1)S(1)}, u32[]{:S(2)}, u32[]{:S(2)}) collective-permute-start(bf16[1,48,576]{2,1,0:T(8,128)(2,1)} %param.8), channel_id=1, source_target_pairs={{0,8},{1,3},{2,10},{3,1},{4,12},{5,7},{6,14},{7,5},{8,0},{9,11},{1... | collective-permute-start | bytes 165896 | tf_op jit(solution)/shard_map/ppermute | solution.py:216
  3.1 0.2 collective-permute-start.2
  3.3 0.7 %broadcast_xor_fusion = s32[2,3]{1,0:T(2,128)S(1)} fusion(s32[2,3]{1,0:T(2,128)} %param.10, s32[]{:T(128)S(6)} %axis_index.25), kind=kLoop, calls=%fused_computation.18 | loop fusion | flops 6 | bytes 52 | tf_op jit(solution)/shard_map/xor | solution.py:221
  4.0 0.8 %constant_dynamic-update-slice_fusion.3 = (bf16[4,48,576]{2,1,0:T(8,128)(2,1)S(1)}, bf16[16,48,576]{2,1,0:T(8,128)(2,1)S(1)}) fusion(bf16[1,48,576]{2,1,0:T(8,128)(2,1)} %param.8), kind=kLoop, calls=%fused_computation.4 | loop fusion | bytes 178176
  5.0 0.3 collective-permute-done
  5.3 2.1 %collective-permute-done.2 = bf16[1,48,576]{2,1,0:T(8,128)(2,1)S(1)} collective-permute-done((bf16[1,48,576]{2,1,0:T(8,128)(2,1)}, bf16[1,48,576]{2,1,0:T(8,128)(2,1)S(1)}, u32[]{:S(2)}, u32[]{:S(2)}) %collective-permute-start.2) | collective-permute-done | bytes 55328 | tf_op jit(solution)/shard_map/ppermute | solution.py:216
  7.3 2.4 %collective-permute-start.4 = (bf16[4,48,576]{2,1,0:T(8,128)(2,1)S(1)}, bf16[4,48,576]{2,1,0:T(8,128)(2,1)S(1)}, u32[]{:S(2)}, u32[]{:S(2)}) collective-permute-start(bf16[4,48,576]{2,1,0:T(8,128)(2,1)S(1)} %get-tuple-element.32), channel_id=1, source_target_pairs={{0,4},{1,17},{2,6},{3,19},{4,0},{5,21},{6,2},{7,23},{8,12},{9,25},... | collective-permute-start | bytes 663560 | tf_op jit(solution)/shard_map/ppermute | solution.py:216
  9.7 0.2 collective-permute-start.3
  9.9 0.5 broadcast_select_fusion.where_ref
  10.4 0.2 collective-permute-start.5
  10.6 5.6 %collective-permute-done.3 = bf16[4,48,576]{2,1,0:T(8,128)(2,1)S(1)} collective-permute-done((bf16[4,48,576]{2,1,0:T(8,128)(2,1)S(1)}, bf16[4,48,576]{2,1,0:T(8,128)(2,1)S(1)}, u32[]{:S(2)}, u32[]{:S(2)}) %collective-permute-start.3) | collective-permute-done | bytes 221216 | tf_op jit(solution)/shard_map/ppermute | solution.py:216
  16.3 4.3 %collective-permute-done.5 = bf16[4,48,576]{2,1,0:T(8,128)(2,1)S(1)} collective-permute-done((bf16[4,48,576]{2,1,0:T(8,128)(2,1)S(1)}, bf16[4,48,576]{2,1,0:T(8,128)(2,1)S(1)}, u32[]{:S(2)}, u32[]{:S(2)}) %collective-permute-start.5) | collective-permute-done | bytes 221216 | tf_op jit(solution)/shard_map/ppermute | solution.py:216
  20.7 0.9 %copy-done.4 = bf16[16,48,576]{2,1,0:T(8,128)(2,1)} copy-done((bf16[16,48,576]{2,1,0:T(8,128)(2,1)}, bf16[16,48,576]{2,1,0:T(8,128)(2,1)S(1)}, u32[]{:S(2)}) %copy-start.4) | copy-done | bytes 884760
  21.6 2.0 %select_nodes.1.refs_0_ = bf16[6,48,576]{2,1,0:T(8,128)(2,1)} custom-call(s32[6]{0:T(128)} %broadcast_select_fusion.where_ref, bf16[16,48,576]{2,1,0:T(8,128)(2,1)} %copy-done.4), custom_call_target="tpu_custom_call" | custom-call | tf_op jit(solution)/shard_map/select_nodes/pallas_call | solution.py:40
  23.8 2.3 %copy.9 = bf16[128,8,576]{2,1,0:T(8,128)(2,1)S(1)} copy(bf16[128,8,576]{0,2,1:T(8,128)(2,1)} %param.6) | data formatting | bytes 2359296 | tf_op args[0]
  26.2 3.1 %attend_grads.1 = (f32[6,48,576]{2,1,0:T(8,128)S(1)}, bf16[6,48,576]{2,1,0:T(8,128)(2,1)S(1)}, bf16[128,576]{1,0:T(8,128)(2,1)S(1)}, bf16[2,352,512]{2,1,0:T(8,128)(2,1)S(1)}, bf16[2,352,576]{2,1,0:T(8,128)(2,1)S(1)}) custom-call(s32[2]{0:T(128)S(1)} %copy-done.3, bf16[128,576]{1,0:T(8,128)(2,1)S(1)} %copy.10.own_ref, bf16[1024,576]{1,0:T(8,128)(2,1)S(1)} %bitcast.3, ...), custom_call_target="tpu_custom_call" | custom-call | flops 1660944384 | bytes 8388608 | tf_op jit(solution)/shard_map/attend_grads/pallas_call | solution.py:110
  29.4 0.6 collective-permute-start.7
  29.9 1.3 %collective-permute-done.7.refs_1_ = bf16[6,48,576]{2,1,0:T(8,128)(2,1)S(1)} collective-permute-done((bf16[6,48,576]{2,1,0:T(8,128)(2,1)S(1)}, bf16[6,48,576]{2,1,0:T(8,128)(2,1)S(1)}, u32[]{:S(2)}, u32[]{:S(2)}) %collective-permute-start.7) | collective-permute-done | bytes 331808 | tf_op jit(solution)/shard_map/ppermute | solution.py:219
  31.2 0.9 %spread_terms.1 = (f32[4,48,576]{2,1,0:T(8,128)S(1)}, bf16[4,48,576]{2,1,0:T(8,128)(2,1)S(1)}, bf16[4,48,576]{2,1,0:T(8,128)(2,1)S(1)}, bf16[4,48,576]{2,1,0:T(8,128)(2,1)S(1)}) custom-call(s32[6]{0:T(128)S(1)} %copy-done.1, f32[6,48,576]{2,1,0:T(8,128)S(1)} %get-tuple-element.18.refs_0_, bf16[6,48,576]{2,1,0:T(8,128)(2,1)S(1)} %collective-permute-done.7.refs_1_), custom_call_target="tpu_custom_call" | custom-call | tf_op jit(solution)/shard_map/spread_terms/pallas_call | solution.py:165
  32.1 2.6 %collective-permute-start.8 = (bf16[4,48,576]{2,1,0:T(8,128)(2,1)S(1)}, bf16[4,48,576]{2,1,0:T(8,128)(2,1)S(1)}, u32[]{:S(2)}, u32[]{:S(2)}) collective-permute-start(bf16[4,48,576]{2,1,0:T(8,128)(2,1)S(1)} %get-tuple-element.21), channel_id=1, source_target_pairs={{0,2},{1,9},{2,0},{3,11},{4,6},{5,13},{6,4},{7,15},{8,10},{9,1},{1... | collective-permute-start | bytes 663560 | tf_op jit(solution)/shard_map/ppermute | solution.py:216
  34.7 0.6 %collective-permute-start.9 = (bf16[4,48,576]{2,1,0:T(8,128)(2,1)S(1)}, bf16[4,48,576]{2,1,0:T(8,128)(2,1)S(1)}, u32[]{:S(2)}, u32[]{:S(2)}) collective-permute-start(bf16[4,48,576]{2,1,0:T(8,128)(2,1)S(1)} %get-tuple-element.22), channel_id=1, source_target_pairs={{0,4},{1,17},{2,6},{3,19},{4,0},{5,21},{6,2},{7,23},{8,12},{9,25},... | collective-permute-start | bytes 663560 | tf_op jit(solution)/shard_map/ppermute | solution.py:216
  35.3 0.7 %collective-permute-start.10 = (bf16[4,48,576]{2,1,0:T(8,128)(2,1)S(1)}, bf16[4,48,576]{2,1,0:T(8,128)(2,1)S(1)}, u32[]{:S(2)}, u32[]{:S(2)}) collective-permute-start(bf16[4,48,576]{2,1,0:T(8,128)(2,1)S(1)} %get-tuple-element.23), channel_id=1, source_target_pairs={{0,6},{1,25},{2,4},{3,27},{4,2},{5,29},{6,0},{7,31},{8,14},{9,17},... | collective-permute-start | bytes 663560 | tf_op jit(solution)/shard_map/ppermute | solution.py:216
  36.0 3.8 %collective-permute-done.8.refs_1_ = bf16[4,48,576]{2,1,0:T(8,128)(2,1)S(1)} collective-permute-done((bf16[4,48,576]{2,1,0:T(8,128)(2,1)S(1)}, bf16[4,48,576]{2,1,0:T(8,128)(2,1)S(1)}, u32[]{:S(2)}, u32[]{:S(2)}) %collective-permute-start.8) | collective-permute-done | bytes 221216 | tf_op jit(solution)/shard_map/ppermute | solution.py:216
  39.8 3.9 %collective-permute-done.9.refs_2_ = bf16[4,48,576]{2,1,0:T(8,128)(2,1)S(1)} collective-permute-done((bf16[4,48,576]{2,1,0:T(8,128)(2,1)S(1)}, bf16[4,48,576]{2,1,0:T(8,128)(2,1)S(1)}, u32[]{:S(2)}, u32[]{:S(2)}) %collective-permute-start.9) | collective-permute-done | bytes 221216 | tf_op jit(solution)/shard_map/ppermute | solution.py:216
  43.7 3.8 %collective-permute-done.10.refs_3_ = bf16[4,48,576]{2,1,0:T(8,128)(2,1)S(1)} collective-permute-done((bf16[4,48,576]{2,1,0:T(8,128)(2,1)S(1)}, bf16[4,48,576]{2,1,0:T(8,128)(2,1)S(1)}, u32[]{:S(2)}, u32[]{:S(2)}) %collective-permute-start.10) | collective-permute-done | bytes 221216 | tf_op jit(solution)/shard_map/ppermute | solution.py:216
  47.6 0.5 collective-permute-start.11
  48.1 4.1 %collective-permute-start.12 = (bf16[1,48,576]{2,1,0:T(8,128)(2,1)S(1)}, bf16[1,48,576]{2,1,0:T(8,128)(2,1)S(1)}, u32[]{:S(2)}, u32[]{:S(2)}) collective-permute-start(bf16[1,48,576]{2,1,0:T(8,128)(2,1)S(1)} %get-tuple-element.26), channel_id=1, source_target_pairs={{0,16},{1,5},{2,18},{3,7},{4,20},{5,1},{6,22},{7,3},{8,24},{9,13},... | collective-permute-start | bytes 165896 | tf_op jit(solution)/shard_map/ppermute | solution.py:216
  52.2 1.7 %attend_outputs.1 = bf16[1024,512]{1,0:T(8,128)(2,1)} custom-call(bf16[2,352,512]{2,1,0:T(8,128)(2,1)S(1)} %get-tuple-element.16.probs_ref, bf16[2,352,576]{2,1,0:T(8,128)(2,1)S(1)} %get-tuple-element.17.keys_ref), custom_call_target="tpu_custom_call" | custom-call | flops 369098752 | bytes 4194304 | tf_op jit(solution)/shard_map/attend_outputs/pallas_call | solution.py:134
  54.0 0.8 %copy.11 = bf16[128,576]{0,1:T(8,128)(2,1)} copy(bf16[128,576]{1,0:T(8,128)(2,1)S(1)} %add.36) | data formatting | bytes 294912
  54.8 1.4 %collective-permute-done.13 = bf16[1,48,576]{2,1,0:T(8,128)(2,1)S(1)} collective-permute-done((bf16[1,48,576]{2,1,0:T(8,128)(2,1)S(1)}, bf16[1,48,576]{2,1,0:T(8,128)(2,1)S(1)}, u32[]{:S(2)}, u32[]{:S(2)}) %collective-permute-start.13) | collective-permute-done | bytes 55328 | tf_op jit(solution)/shard_map/ppermute | solution.py:216
  56.2 0.7 %add_convert_fusion = bf16[1,48,576]{2,1,0:T(8,128)(2,1)} fusion(bf16[1,48,576]{2,1,0:T(8,128)(2,1)S(1)} %collective-permute-done.13, bf16[1,48,576]{2,1,0:T(8,128)(2,1)S(1)} %collective-permute-done.12, f32[1,48,576]{2,1,0:T(8,128)S(1)} %get-tuple-element.24, bf16[1,48,576]{2,1,0:T(8,128)(2,1)S(1)} %collective-permute-done.11), kind=kLoop, calls=%fused_computation | loop fusion | flops 193536 | bytes 331776 | tf_op jit(solution)/shard_map/convert_element_type | solution.py:244
  (30 shorter events, 0.7 us)
Async XLA Ops:
  0.6 4.6 %collective-permute-start.1 = (bf16[1,48,576]{2,1,0:T(8,128)(2,1)}, bf16[1,48,576]{2,1,0:T(8,128)(2,1)S(1)}, u32[]{:S(2)}, u32[]{:S(2)}) collective-permute-start(bf16[1,48,576]{2,1,0:T(8,128)(2,1)} %param.8), channel_id=1, source_target_pairs={{0,16},{1,5},{2,18},{3,7},{4,20},{5,1},{6,22},{7,3},{8,24},{9,13},... | collective-permute-start | bytes 165896 | tf_op jit(solution)/shard_map/ppermute | solution.py:216
  1.9 3.3 %collective-permute-start = (bf16[1,48,576]{2,1,0:T(8,128)(2,1)}, bf16[1,48,576]{2,1,0:T(8,128)(2,1)S(1)}, u32[]{:S(2)}, u32[]{:S(2)}) collective-permute-start(bf16[1,48,576]{2,1,0:T(8,128)(2,1)} %param.8), channel_id=1, source_target_pairs={{0,8},{1,3},{2,10},{3,1},{4,12},{5,7},{6,14},{7,5},{8,0},{9,11},{1... | collective-permute-start | bytes 165896 | tf_op jit(solution)/shard_map/ppermute | solution.py:216
  3.1 4.2 %collective-permute-start.2 = (bf16[1,48,576]{2,1,0:T(8,128)(2,1)}, bf16[1,48,576]{2,1,0:T(8,128)(2,1)S(1)}, u32[]{:S(2)}, u32[]{:S(2)}) collective-permute-start(bf16[1,48,576]{2,1,0:T(8,128)(2,1)} %param.8), channel_id=1, source_target_pairs={{0,24},{1,7},{2,26},{3,5},{4,28},{5,3},{6,30},{7,1},{8,16},{9,15},... | collective-permute-start | bytes 165896 | tf_op jit(solution)/shard_map/ppermute | solution.py:216
  7.3 8.9 %collective-permute-start.4 = (bf16[4,48,576]{2,1,0:T(8,128)(2,1)S(1)}, bf16[4,48,576]{2,1,0:T(8,128)(2,1)S(1)}, u32[]{:S(2)}, u32[]{:S(2)}) collective-permute-start(bf16[4,48,576]{2,1,0:T(8,128)(2,1)S(1)} %get-tuple-element.32), channel_id=1, source_target_pairs={{0,4},{1,17},{2,6},{3,19},{4,0},{5,21},{6,2},{7,23},{8,12},{9,25},... | collective-permute-start | bytes 663560 | tf_op jit(solution)/shard_map/ppermute | solution.py:216
  9.7 6.5 %collective-permute-start.3 = (bf16[4,48,576]{2,1,0:T(8,128)(2,1)S(1)}, bf16[4,48,576]{2,1,0:T(8,128)(2,1)S(1)}, u32[]{:S(2)}, u32[]{:S(2)}) collective-permute-start(bf16[4,48,576]{2,1,0:T(8,128)(2,1)S(1)} %get-tuple-element.32), channel_id=1, source_target_pairs={{0,2},{1,9},{2,0},{3,11},{4,6},{5,13},{6,4},{7,15},{8,10},{9,1},{1... | collective-permute-start | bytes 663560 | tf_op jit(solution)/shard_map/ppermute | solution.py:216
  10.4 10.2 %collective-permute-start.5 = (bf16[4,48,576]{2,1,0:T(8,128)(2,1)S(1)}, bf16[4,48,576]{2,1,0:T(8,128)(2,1)S(1)}, u32[]{:S(2)}, u32[]{:S(2)}) collective-permute-start(bf16[4,48,576]{2,1,0:T(8,128)(2,1)S(1)} %get-tuple-element.32), channel_id=1, source_target_pairs={{0,6},{1,25},{2,4},{3,27},{4,2},{5,29},{6,0},{7,31},{8,14},{9,17},... | collective-permute-start | bytes 663560 | tf_op jit(solution)/shard_map/ppermute | solution.py:216
  16.2 7.4 %copy-start.5 = (bf16[128,576]{0,1:T(8,128)(2,1)S(1)}, bf16[128,576]{0,1:T(8,128)(2,1)}, u32[]{:S(2)}) copy-start(bf16[128,576]{0,1:T(8,128)(2,1)} %param.7) | copy-start | bytes 442372
  20.7 0.9 %copy-start.4 = (bf16[16,48,576]{2,1,0:T(8,128)(2,1)}, bf16[16,48,576]{2,1,0:T(8,128)(2,1)S(1)}, u32[]{:S(2)}) copy-start(bf16[16,48,576]{2,1,0:T(8,128)(2,1)S(1)} %constant_dynamic-update-slice_fusion.4.table_ref) | copy-start | bytes 2654212
  23.6 2.5 %collective-permute-start.6 = (bf16[6,48,576]{2,1,0:T(8,128)(2,1)}, bf16[6,48,576]{2,1,0:T(8,128)(2,1)S(1)}, u32[]{:S(2)}, u32[]{:S(2)}) collective-permute-start(bf16[6,48,576]{2,1,0:T(8,128)(2,1)} %select_nodes.1.refs_0_), channel_id=1, source_target_pairs={{0,1},{1,0},{2,3},{3,2},{4,5},{5,4},{6,7},{7,6},{8,9},{9,8},{10,11... | collective-permute-start | bytes 995336 | tf_op jit(solution)/shard_map/ppermute | solution.py:219
  23.8 2.4 %copy-start = (bf16[6,48,576]{2,1,0:T(8,128)(2,1)S(1)}, bf16[6,48,576]{2,1,0:T(8,128)(2,1)}, u32[]{:S(2)}) copy-start(bf16[6,48,576]{2,1,0:T(8,128)(2,1)} %select_nodes.1.refs_0_) | copy-start | bytes 995332
  23.8 2.4 %copy-start.2 = (bf16[128,8,512]{2,1,0:T(8,128)(2,1)S(1)}, bf16[128,8,512]{2,1,0:T(8,128)(2,1)}, u32[]{:S(2)}) copy-start(bf16[128,8,512]{2,1,0:T(8,128)(2,1)} %param.9) | copy-start | bytes 3145732
  23.8 2.4 %copy-start.3 = (s32[2]{0:T(128)S(1)}, s32[2]{0:T(128)}, u32[]{:S(2)}) copy-start(s32[2]{0:T(128)} %len_ref.1) | copy-start | bytes 28
  26.2 5.0 %copy-start.1 = (s32[6]{0:T(128)S(1)}, s32[6]{0:T(128)}, u32[]{:S(2)}) copy-start(s32[6]{0:T(128)} %broadcast_select_fusion.where_ref) | copy-start | bytes 76
  29.4 1.9 %collective-permute-start.7 = (bf16[6,48,576]{2,1,0:T(8,128)(2,1)S(1)}, bf16[6,48,576]{2,1,0:T(8,128)(2,1)S(1)}, u32[]{:S(2)}, u32[]{:S(2)}) collective-permute-start(bf16[6,48,576]{2,1,0:T(8,128)(2,1)S(1)} %get-tuple-element.19), channel_id=1, source_target_pairs={{0,1},{1,0},{2,3},{3,2},{4,5},{5,4},{6,7},{7,6},{8,9},{9,8},{10,11... | collective-permute-start | bytes 995336 | tf_op jit(solution)/shard_map/ppermute | solution.py:219
  32.1 7.7 %collective-permute-start.8 = (bf16[4,48,576]{2,1,0:T(8,128)(2,1)S(1)}, bf16[4,48,576]{2,1,0:T(8,128)(2,1)S(1)}, u32[]{:S(2)}, u32[]{:S(2)}) collective-permute-start(bf16[4,48,576]{2,1,0:T(8,128)(2,1)S(1)} %get-tuple-element.21), channel_id=1, source_target_pairs={{0,2},{1,9},{2,0},{3,11},{4,6},{5,13},{6,4},{7,15},{8,10},{9,1},{1... | collective-permute-start | bytes 663560 | tf_op jit(solution)/shard_map/ppermute | solution.py:216
  34.7 9.0 %collective-permute-start.9 = (bf16[4,48,576]{2,1,0:T(8,128)(2,1)S(1)}, bf16[4,48,576]{2,1,0:T(8,128)(2,1)S(1)}, u32[]{:S(2)}, u32[]{:S(2)}) collective-permute-start(bf16[4,48,576]{2,1,0:T(8,128)(2,1)S(1)} %get-tuple-element.22), channel_id=1, source_target_pairs={{0,4},{1,17},{2,6},{3,19},{4,0},{5,21},{6,2},{7,23},{8,12},{9,25},... | collective-permute-start | bytes 663560 | tf_op jit(solution)/shard_map/ppermute | solution.py:216
  35.3 12.2 %collective-permute-start.10 = (bf16[4,48,576]{2,1,0:T(8,128)(2,1)S(1)}, bf16[4,48,576]{2,1,0:T(8,128)(2,1)S(1)}, u32[]{:S(2)}, u32[]{:S(2)}) collective-permute-start(bf16[4,48,576]{2,1,0:T(8,128)(2,1)S(1)} %get-tuple-element.23), channel_id=1, source_target_pairs={{0,6},{1,25},{2,4},{3,27},{4,2},{5,29},{6,0},{7,31},{8,14},{9,17},... | collective-permute-start | bytes 663560 | tf_op jit(solution)/shard_map/ppermute | solution.py:216
  36.0 18.0 %collective-permute-start.14 = (bf16[128,576]{1,0:T(8,128)(2,1)S(1)}, bf16[128,576]{1,0:T(8,128)(2,1)S(1)}, u32[]{:S(2)}, u32[]{:S(2)}) collective-permute-start(bf16[128,576]{1,0:T(8,128)(2,1)S(1)} %get-tuple-element.28), channel_id=1, source_target_pairs={{0,1},{1,0},{2,3},{3,2},{4,5},{5,4},{6,7},{7,6},{8,9},{9,8},{10,11... | collective-permute-start | bytes 442376 | tf_op jit(solution)/shard_map/ppermute | solution.py:219
  47.6 7.2 %collective-permute-start.11 = (bf16[1,48,576]{2,1,0:T(8,128)(2,1)S(1)}, bf16[1,48,576]{2,1,0:T(8,128)(2,1)S(1)}, u32[]{:S(2)}, u32[]{:S(2)}) collective-permute-start(bf16[1,48,576]{2,1,0:T(8,128)(2,1)S(1)} %get-tuple-element.25), channel_id=1, source_target_pairs={{0,8},{1,3},{2,10},{3,1},{4,12},{5,7},{6,14},{7,5},{8,0},{9,11},{1... | collective-permute-start | bytes 165896 | tf_op jit(solution)/shard_map/ppermute | solution.py:216
  48.1 6.7 %collective-permute-start.12 = (bf16[1,48,576]{2,1,0:T(8,128)(2,1)S(1)}, bf16[1,48,576]{2,1,0:T(8,128)(2,1)S(1)}, u32[]{:S(2)}, u32[]{:S(2)}) collective-permute-start(bf16[1,48,576]{2,1,0:T(8,128)(2,1)S(1)} %get-tuple-element.26), channel_id=1, source_target_pairs={{0,16},{1,5},{2,18},{3,7},{4,20},{5,1},{6,22},{7,3},{8,24},{9,13},... | collective-permute-start | bytes 165896 | tf_op jit(solution)/shard_map/ppermute | solution.py:216
  52.2 4.0 %collective-permute-start.13 = (bf16[1,48,576]{2,1,0:T(8,128)(2,1)S(1)}, bf16[1,48,576]{2,1,0:T(8,128)(2,1)S(1)}, u32[]{:S(2)}, u32[]{:S(2)}) collective-permute-start(bf16[1,48,576]{2,1,0:T(8,128)(2,1)S(1)} %get-tuple-element.27), channel_id=1, source_target_pairs={{0,24},{1,7},{2,26},{3,5},{4,28},{5,3},{6,30},{7,1},{8,16},{9,15},... | collective-permute-start | bytes 165896 | tf_op jit(solution)/shard_map/ppermute | solution.py:216

commit v2 on v1

--- a/solution.py
+++ b/solution.py
@@ -42,6 +42,7 @@
         out_shape=jax.ShapeDtypeStruct(shape, table.dtype),
         in_specs=[pl.BlockSpec(memory_space=pltpu.SMEM)] + vmem(1),
         out_specs=vmem(1)[0],
+        compiler_params=pltpu.CompilerParams(vmem_limit_bytes=4 << 20),
         name="select_nodes",
     )(where, table)
 
@@ -223,24 +224,29 @@
     even = lax.axis_index("head") % 2 == 0
     where = jnp.where(even, near * side + far, far * side + near)
 
-    inner = jnp.concatenate([node_latent] + [step(node_latent, 0, d) for d in range(1, side)], axis=0)
-    table = jnp.concatenate([inner] + [step(inner, 1, d) for d in range(1, side)], axis=0)
+    order = list(range(side - 1, 0, -1))
+    got = {d: step(node_latent, 0, d) for d in order}
+    inner = jnp.concatenate([node_latent] + [got[d] for d in range(1, side)], axis=0)
+    query = queries.reshape(rows * heads, width)
+    inner, query, own = lax.optimization_barrier((inner, query, leaf_latent))
+    got = {d: step(inner, 1, d) for d in order}
+    table = jnp.concatenate([inner] + [got[d] for d in range(1, side)], axis=0)
     mine = select(where, table)
     parts = [mine] + [swap(mine, d) for d in range(1, head_size)]
-
-    query = queries.reshape(rows * heads, width)
     grad = grad_out.reshape(rows * heads, LAT)
-    results = grads(leaf_lengths, leaf_latent, query, grad, parts, leaves, heads)
+    results = grads(leaf_lengths, own, query, grad, parts, leaves, heads)
     terms, (own_grad, probs, keys) = results[:head_size], results[head_size:]
 
     shares = [terms[0]] + [swap(terms[d], d) for d in range(1, head_size)]
     keep, *sends = spread(where, shares, side, side)
-    got = [step(send, 1, d + 1) for d, send in enumerate(sends)]
+    got = {d: step(sends[d - 1], 1, d) for d in order}
+    got = [got[d] for d in range(1, side)]
     attention = outputs(probs, keys).reshape(rows, heads, LAT)
     keep, *sends = merge(keep, got)
+    got = {d: step(sends[d - 1], 0, d) for d in order}
     total = keep
-    for d, send in enumerate(sends):
-        total = total + step(send, 0, d + 1).astype(jnp.float32)
+    for d in range(1, side):
+        total = total + got[d].astype(jnp.float32)
     node_grad = total.astype(jnp.bfloat16)
 
     leaf_grad = own_grad

time: 57.1 us -> 50.2 us (0.88)
  the two profiles are of different devices: /device:TPU:9 before, /device:TPU:0 now
where the time goes in v2:
time: 50.2 us; the launch traced here: 50.1 us
  waiting for transfers between devices  19.8 us (39%)
  starting transfers between devices  18.2 us (36%)
  Pallas kernels  6.46 us (13%)
  local copies, waits for them, and re-layouts  3.26 us (6%)
  other arithmetic  1.63 us (3%)
  between operations  0.75 us (1%)
    ppermute x12, starting transfers between devices, step(): return lax.ppermute(value, axes, pairs)  17.3 us
    ppermute x12, waiting for transfers between devices, step(): return lax.ppermute(value, axes, pairs)  17.1 us
    pallas_call x1, Pallas kernels, grads(): pl.pallas_call(functools.partial(grads_kernel, len(parts), leaves, heads)...  3.19 us
    unnamed x10, local copies, waits for them, and re-layouts  3.02 us
    ppermute x3, waiting for transfers between devices, swap(): lax.ppermute(value, 'head', [(i, i ^ distance) for i in range(head_size)])  2.74 us
    pallas_call x1, Pallas kernels, outputs(): pl.pallas_call(functools.partial(outputs_kernel, leaves), out_shape=jax.S...  1.71 us
  transfers between devices with their start and end apart: 15, of which 9 were waited for; matrix products, arithmetic and copies ran while one was open for 8% of the time, Pallas kernels for 4%

profile of v2, /device:TPU:0, one launch (start us, length us, event | category | flops | bytes accessed | tf_op | source)
XLA Modules:
  0.0 50.1 jit_solution(10154647531151918063)
XLA Ops:
  0.6 4.1 %collective-permute-start.1 = (bf16[1,48,576]{2,1,0:T(8,128)(2,1)}, bf16[1,48,576]{2,1,0:T(8,128)(2,1)S(1)}, u32[]{:S(2)}, u32[]{:S(2)}) collective-permute-start(bf16[1,48,576]{2,1,0:T(8,128)(2,1)} %param.8), channel_id=1, source_target_pairs={{0,16},{1,5},{2,18},{3,7},{4,20},{5,1},{6,22},{7,3},{8,24},{9,13},... | collective-permute-start | bytes 165896 | tf_op jit(solution)/shard_map/ppermute | solution.py:217
  4.8 1.6 %collective-permute-start = (bf16[1,48,576]{2,1,0:T(8,128)(2,1)}, bf16[1,48,576]{2,1,0:T(8,128)(2,1)S(1)}, u32[]{:S(2)}, u32[]{:S(2)}) collective-permute-start(bf16[1,48,576]{2,1,0:T(8,128)(2,1)} %param.8), channel_id=1, source_target_pairs={{0,8},{1,3},{2,10},{3,1},{4,12},{5,7},{6,14},{7,5},{8,0},{9,11},{1... | collective-permute-start | bytes 165896 | tf_op jit(solution)/shard_map/ppermute | solution.py:217
  6.4 0.7 %broadcast_xor_fusion = s32[2,3]{1,0:T(2,128)S(1)} fusion(s32[2,3]{1,0:T(2,128)} %param.10, s32[]{:T(128)S(6)} %axis_index.25), kind=kLoop, calls=%fused_computation.9 | loop fusion | flops 6 | bytes 52 | tf_op jit(solution)/shard_map/xor | solution.py:222
  7.1 2.2 %copy.9 = bf16[128,8,576]{2,1,0:T(8,128)(2,1)S(1)} copy(bf16[128,8,576]{0,2,1:T(8,128)(2,1)} %param.6) | data formatting | bytes 2359296 | tf_op args[0]
  9.3 3.2 %collective-permute-done.2 = bf16[1,48,576]{2,1,0:T(8,128)(2,1)S(1)} collective-permute-done((bf16[1,48,576]{2,1,0:T(8,128)(2,1)}, bf16[1,48,576]{2,1,0:T(8,128)(2,1)S(1)}, u32[]{:S(2)}, u32[]{:S(2)}) %collective-permute-start.2) | collective-permute-done | bytes 55328 | tf_op jit(solution)/shard_map/ppermute | solution.py:217
  12.7 2.9 %collective-permute-start.5 = (bf16[4,48,576]{2,1,0:T(8,128)(2,1)S(1)}, bf16[4,48,576]{2,1,0:T(8,128)(2,1)S(1)}, u32[]{:S(2)}, u32[]{:S(2)}) collective-permute-start(bf16[4,48,576]{2,1,0:T(8,128)(2,1)S(1)} %pad_maximum_fusion.1), channel_id=1, source_target_pairs={{0,6},{1,25},{2,4},{3,27},{4,2},{5,29},{6,0},{7,31},{8,14},{9,17},... | collective-permute-start | bytes 663560 | tf_op jit(solution)/shard_map/ppermute | solution.py:217
  15.6 0.2 collective-permute-start.4
  15.8 0.4 collective-permute-start.3
  16.2 3.7 %collective-permute-done.5 = bf16[4,48,576]{2,1,0:T(8,128)(2,1)S(1)} collective-permute-done((bf16[4,48,576]{2,1,0:T(8,128)(2,1)S(1)}, bf16[4,48,576]{2,1,0:T(8,128)(2,1)S(1)}, u32[]{:S(2)}, u32[]{:S(2)}) %collective-permute-start.5) | collective-permute-done | bytes 221216 | tf_op jit(solution)/shard_map/ppermute | solution.py:217
  19.9 2.6 %collective-permute-done.4 = bf16[4,48,576]{2,1,0:T(8,128)(2,1)S(1)} collective-permute-done((bf16[4,48,576]{2,1,0:T(8,128)(2,1)S(1)}, bf16[4,48,576]{2,1,0:T(8,128)(2,1)S(1)}, u32[]{:S(2)}, u32[]{:S(2)}) %collective-permute-start.4) | collective-permute-done | bytes 221216 | tf_op jit(solution)/shard_map/ppermute | solution.py:217
  22.4 0.2 collective-permute-done.3
  22.7 0.2 pad_maximum_fusion.table_ref
  22.9 0.6 %select_nodes.1.refs_0_ = bf16[6,48,576]{2,1,0:T(8,128)(2,1)S(1)} custom-call(s32[6]{0:T(128)S(1)} %broadcast_select_fusion.where_ref, bf16[16,48,576]{2,1,0:T(8,128)(2,1)S(1)} %pad_maximum_fusion.table_ref), custom_call_target="tpu_custom_call" | custom-call | tf_op jit(solution)/shard_map/select_nodes/pallas_call | solution.py:40
  23.5 0.3 collective-permute-start.6
  23.8 0.2 copy.10.own_ref
  24.0 1.3 %collective-permute-done.6.refs_1_ = bf16[6,48,576]{2,1,0:T(8,128)(2,1)S(1)} collective-permute-done((bf16[6,48,576]{2,1,0:T(8,128)(2,1)S(1)}, bf16[6,48,576]{2,1,0:T(8,128)(2,1)S(1)}, u32[]{:S(2)}, u32[]{:S(2)}) %collective-permute-start.6) | collective-permute-done | bytes 331808 | tf_op jit(solution)/shard_map/ppermute | solution.py:220
  25.2 3.2 %attend_grads.1 = (f32[6,48,576]{2,1,0:T(8,128)S(1)}, bf16[6,48,576]{2,1,0:T(8,128)(2,1)S(1)}, bf16[128,576]{1,0:T(8,128)(2,1)S(1)}, bf16[2,352,512]{2,1,0:T(8,128)(2,1)S(1)}, bf16[2,352,576]{2,1,0:T(8,128)(2,1)S(1)}) custom-call(s32[2]{0:T(128)S(1)} %copy-done.1, bf16[128,576]{1,0:T(8,128)(2,1)S(1)} %copy.10.own_ref, bf16[1024,576]{1,0:T(8,128)(2,1)S(1)} %bitcast.3, ...), custom_call_target="tpu_custom_call" | custom-call | flops 1660944384 | bytes 8388608 | tf_op jit(solution)/shard_map/attend_grads/pallas_call | solution.py:111
  28.4 0.3 collective-permute-start.7
  28.7 1.5 %collective-permute-done.7.refs_1_ = bf16[6,48,576]{2,1,0:T(8,128)(2,1)S(1)} collective-permute-done((bf16[6,48,576]{2,1,0:T(8,128)(2,1)S(1)}, bf16[6,48,576]{2,1,0:T(8,128)(2,1)S(1)}, u32[]{:S(2)}, u32[]{:S(2)}) %collective-permute-start.7) | collective-permute-done | bytes 331808 | tf_op jit(solution)/shard_map/ppermute | solution.py:220
  30.2 0.9 %spread_terms.1 = (f32[4,48,576]{2,1,0:T(8,128)S(1)}, bf16[4,48,576]{2,1,0:T(8,128)(2,1)S(1)}, bf16[4,48,576]{2,1,0:T(8,128)(2,1)S(1)}, bf16[4,48,576]{2,1,0:T(8,128)(2,1)S(1)}) custom-call(s32[6]{0:T(128)S(1)} %broadcast_select_fusion.where_ref, f32[6,48,576]{2,1,0:T(8,128)S(1)} %get-tuple-element.24.refs_0_, ...), custom_call_target="tpu_custom_call" | custom-call | tf_op jit(solution)/shard_map/spread_terms/pallas_call | solution.py:166
  31.1 1.8 %collective-permute-start.8 = (bf16[4,48,576]{2,1,0:T(8,128)(2,1)S(1)}, bf16[4,48,576]{2,1,0:T(8,128)(2,1)S(1)}, u32[]{:S(2)}, u32[]{:S(2)}) collective-permute-start(bf16[4,48,576]{2,1,0:T(8,128)(2,1)S(1)} %get-tuple-element.27), channel_id=1, source_target_pairs={{0,2},{1,9},{2,0},{3,11},{4,6},{5,13},{6,4},{7,15},{8,10},{9,1},{1... | collective-permute-start | bytes 663560 | tf_op jit(solution)/shard_map/ppermute | solution.py:217
  32.9 0.6 %collective-permute-start.9 = (bf16[4,48,576]{2,1,0:T(8,128)(2,1)S(1)}, bf16[4,48,576]{2,1,0:T(8,128)(2,1)S(1)}, u32[]{:S(2)}, u32[]{:S(2)}) collective-permute-start(bf16[4,48,576]{2,1,0:T(8,128)(2,1)S(1)} %get-tuple-element.28), channel_id=1, source_target_pairs={{0,4},{1,17},{2,6},{3,19},{4,0},{5,21},{6,2},{7,23},{8,12},{9,25},... | collective-permute-start | bytes 663560 | tf_op jit(solution)/shard_map/ppermute | solution.py:217
  33.5 1.1 %collective-permute-start.10 = (bf16[4,48,576]{2,1,0:T(8,128)(2,1)S(1)}, bf16[4,48,576]{2,1,0:T(8,128)(2,1)S(1)}, u32[]{:S(2)}, u32[]{:S(2)}) collective-permute-start(bf16[4,48,576]{2,1,0:T(8,128)(2,1)S(1)} %get-tuple-element.29), channel_id=1, source_target_pairs={{0,6},{1,25},{2,4},{3,27},{4,2},{5,29},{6,0},{7,31},{8,14},{9,17},... | collective-permute-start | bytes 663560 | tf_op jit(solution)/shard_map/ppermute | solution.py:217
  34.6 0.3 collective-permute-start.14
  34.9 2.4 %collective-permute-done.8.refs_1_ = bf16[4,48,576]{2,1,0:T(8,128)(2,1)S(1)} collective-permute-done((bf16[4,48,576]{2,1,0:T(8,128)(2,1)S(1)}, bf16[4,48,576]{2,1,0:T(8,128)(2,1)S(1)}, u32[]{:S(2)}, u32[]{:S(2)}) %collective-permute-start.8) | collective-permute-done | bytes 221216 | tf_op jit(solution)/shard_map/ppermute | solution.py:217
  37.3 4.4 %collective-permute-done.9.refs_2_ = bf16[4,48,576]{2,1,0:T(8,128)(2,1)S(1)} collective-permute-done((bf16[4,48,576]{2,1,0:T(8,128)(2,1)S(1)}, bf16[4,48,576]{2,1,0:T(8,128)(2,1)S(1)}, u32[]{:S(2)}, u32[]{:S(2)}) %collective-permute-start.9) | collective-permute-done | bytes 221216 | tf_op jit(solution)/shard_map/ppermute | solution.py:217
  41.9 1.5 %collective-permute-start.12 = (bf16[1,48,576]{2,1,0:T(8,128)(2,1)S(1)}, bf16[1,48,576]{2,1,0:T(8,128)(2,1)S(1)}, u32[]{:S(2)}, u32[]{:S(2)}) collective-permute-start(bf16[1,48,576]{2,1,0:T(8,128)(2,1)S(1)} %get-tuple-element.32), channel_id=1, source_target_pairs={{0,16},{1,5},{2,18},{3,7},{4,20},{5,1},{6,22},{7,3},{8,24},{9,13},... | collective-permute-start | bytes 165896 | tf_op jit(solution)/shard_map/ppermute | solution.py:217
  43.4 2.9 %collective-permute-start.13 = (bf16[1,48,576]{2,1,0:T(8,128)(2,1)S(1)}, bf16[1,48,576]{2,1,0:T(8,128)(2,1)S(1)}, u32[]{:S(2)}, u32[]{:S(2)}) collective-permute-start(bf16[1,48,576]{2,1,0:T(8,128)(2,1)S(1)} %get-tuple-element.33), channel_id=1, source_target_pairs={{0,24},{1,7},{2,26},{3,5},{4,28},{5,3},{6,30},{7,1},{8,16},{9,15},... | collective-permute-start | bytes 165896 | tf_op jit(solution)/shard_map/ppermute | solution.py:217
  46.3 1.7 %attend_outputs.1 = bf16[1024,512]{1,0:T(8,128)(2,1)} custom-call(bf16[2,352,512]{2,1,0:T(8,128)(2,1)S(1)} %get-tuple-element.22.probs_ref, bf16[2,352,576]{2,1,0:T(8,128)(2,1)S(1)} %get-tuple-element.23.keys_ref), custom_call_target="tpu_custom_call" | custom-call | flops 369098752 | bytes 4194304 | tf_op jit(solution)/shard_map/attend_outputs/pallas_call | solution.py:135
  48.0 0.8 %copy.11 = bf16[128,576]{0,1:T(8,128)(2,1)} copy(bf16[128,576]{1,0:T(8,128)(2,1)S(1)} %add.36) | data formatting | bytes 294912
  48.8 0.6 %collective-permute-done.13 = bf16[1,48,576]{2,1,0:T(8,128)(2,1)S(1)} collective-permute-done((bf16[1,48,576]{2,1,0:T(8,128)(2,1)S(1)}, bf16[1,48,576]{2,1,0:T(8,128)(2,1)S(1)}, u32[]{:S(2)}, u32[]{:S(2)}) %collective-permute-start.13) | collective-permute-done | bytes 55328 | tf_op jit(solution)/shard_map/ppermute | solution.py:217
  49.4 0.7 %add_convert_fusion = bf16[1,48,576]{2,1,0:T(8,128)(2,1)} fusion(bf16[1,48,576]{2,1,0:T(8,128)(2,1)S(1)} %collective-permute-done.13, bf16[1,48,576]{2,1,0:T(8,128)(2,1)S(1)} %collective-permute-done.12, f32[1,48,576]{2,1,0:T(8,128)S(1)} %get-tuple-element.30, bf16[1,48,576]{2,1,0:T(8,128)(2,1)S(1)} %collective-permute-done.11), kind=kLoop, calls=%fused_computation.2 | loop fusion | flops 193536 | bytes 331776 | tf_op jit(solution)/shard_map/convert_element_type | solution.py:250
  (21 shorter events, 0.4 us)
Async XLA Ops:
  0.6 12.0 %copy-start.3 = (bf16[1,48,576]{2,1,0:T(8,128)(2,1)S(1)}, bf16[1,48,576]{2,1,0:T(8,128)(2,1)}, u32[]{:S(2)}) copy-start(bf16[1,48,576]{2,1,0:T(8,128)(2,1)} %param.8) | copy-start | bytes 165892
  0.6 8.7 %collective-permute-start.1 = (bf16[1,48,576]{2,1,0:T(8,128)(2,1)}, bf16[1,48,576]{2,1,0:T(8,128)(2,1)S(1)}, u32[]{:S(2)}, u32[]{:S(2)}) collective-permute-start(bf16[1,48,576]{2,1,0:T(8,128)(2,1)} %param.8), channel_id=1, source_target_pairs={{0,16},{1,5},{2,18},{3,7},{4,20},{5,1},{6,22},{7,3},{8,24},{9,13},... | collective-permute-start | bytes 165896 | tf_op jit(solution)/shard_map/ppermute | solution.py:217
  4.8 4.6 %collective-permute-start = (bf16[1,48,576]{2,1,0:T(8,128)(2,1)}, bf16[1,48,576]{2,1,0:T(8,128)(2,1)S(1)}, u32[]{:S(2)}, u32[]{:S(2)}) collective-permute-start(bf16[1,48,576]{2,1,0:T(8,128)(2,1)} %param.8), channel_id=1, source_target_pairs={{0,8},{1,3},{2,10},{3,1},{4,12},{5,7},{6,14},{7,5},{8,0},{9,11},{1... | collective-permute-start | bytes 165896 | tf_op jit(solution)/shard_map/ppermute | solution.py:217
  6.3 6.2 %collective-permute-start.2 = (bf16[1,48,576]{2,1,0:T(8,128)(2,1)}, bf16[1,48,576]{2,1,0:T(8,128)(2,1)S(1)}, u32[]{:S(2)}, u32[]{:S(2)}) collective-permute-start(bf16[1,48,576]{2,1,0:T(8,128)(2,1)} %param.8), channel_id=1, source_target_pairs={{0,24},{1,7},{2,26},{3,5},{4,28},{5,3},{6,30},{7,1},{8,16},{9,15},... | collective-permute-start | bytes 165896 | tf_op jit(solution)/shard_map/ppermute | solution.py:217
  12.7 7.2 %collective-permute-start.5 = (bf16[4,48,576]{2,1,0:T(8,128)(2,1)S(1)}, bf16[4,48,576]{2,1,0:T(8,128)(2,1)S(1)}, u32[]{:S(2)}, u32[]{:S(2)}) collective-permute-start(bf16[4,48,576]{2,1,0:T(8,128)(2,1)S(1)} %pad_maximum_fusion.1), channel_id=1, source_target_pairs={{0,6},{1,25},{2,4},{3,27},{4,2},{5,29},{6,0},{7,31},{8,14},{9,17},... | collective-permute-start | bytes 663560 | tf_op jit(solution)/shard_map/ppermute | solution.py:217
  15.6 6.9 %collective-permute-start.4 = (bf16[4,48,576]{2,1,0:T(8,128)(2,1)S(1)}, bf16[4,48,576]{2,1,0:T(8,128)(2,1)S(1)}, u32[]{:S(2)}, u32[]{:S(2)}) collective-permute-start(bf16[4,48,576]{2,1,0:T(8,128)(2,1)S(1)} %pad_maximum_fusion.1), channel_id=1, source_target_pairs={{0,4},{1,17},{2,6},{3,19},{4,0},{5,21},{6,2},{7,23},{8,12},{9,25},... | collective-permute-start | bytes 663560 | tf_op jit(solution)/shard_map/ppermute | solution.py:217
  15.8 6.9 %collective-permute-start.3 = (bf16[4,48,576]{2,1,0:T(8,128)(2,1)S(1)}, bf16[4,48,576]{2,1,0:T(8,128)(2,1)S(1)}, u32[]{:S(2)}, u32[]{:S(2)}) collective-permute-start(bf16[4,48,576]{2,1,0:T(8,128)(2,1)S(1)} %pad_maximum_fusion.1), channel_id=1, source_target_pairs={{0,2},{1,9},{2,0},{3,11},{4,6},{5,13},{6,4},{7,15},{8,10},{9,1},{1... | collective-permute-start | bytes 663560 | tf_op jit(solution)/shard_map/ppermute | solution.py:217
  16.2 7.6 %copy-start.2 = (bf16[128,576]{0,1:T(8,128)(2,1)S(1)}, bf16[128,576]{0,1:T(8,128)(2,1)}, u32[]{:S(2)}) copy-start(bf16[128,576]{0,1:T(8,128)(2,1)} %param.7) | copy-start | bytes 442372
  22.9 2.4 %copy-start = (bf16[128,8,512]{2,1,0:T(8,128)(2,1)S(1)}, bf16[128,8,512]{2,1,0:T(8,128)(2,1)}, u32[]{:S(2)}) copy-start(bf16[128,8,512]{2,1,0:T(8,128)(2,1)} %param.9) | copy-start | bytes 3145732
  22.9 2.4 %copy-start.1 = (s32[2]{0:T(128)S(1)}, s32[2]{0:T(128)}, u32[]{:S(2)}) copy-start(s32[2]{0:T(128)} %len_ref.1) | copy-start | bytes 28
  23.5 1.8 %collective-permute-start.6 = (bf16[6,48,576]{2,1,0:T(8,128)(2,1)S(1)}, bf16[6,48,576]{2,1,0:T(8,128)(2,1)S(1)}, u32[]{:S(2)}, u32[]{:S(2)}) collective-permute-start(bf16[6,48,576]{2,1,0:T(8,128)(2,1)S(1)} %select_nodes.1.refs_0_), channel_id=1, source_target_pairs={{0,1},{1,0},{2,3},{3,2},{4,5},{5,4},{6,7},{7,6},{8,9},{9,8},{10,11... | collective-permute-start | bytes 995336 | tf_op jit(solution)/shard_map/ppermute | solution.py:220
  28.4 1.8 %collective-permute-start.7 = (bf16[6,48,576]{2,1,0:T(8,128)(2,1)S(1)}, bf16[6,48,576]{2,1,0:T(8,128)(2,1)S(1)}, u32[]{:S(2)}, u32[]{:S(2)}) collective-permute-start(bf16[6,48,576]{2,1,0:T(8,128)(2,1)S(1)} %get-tuple-element.25), channel_id=1, source_target_pairs={{0,1},{1,0},{2,3},{3,2},{4,5},{5,4},{6,7},{7,6},{8,9},{9,8},{10,11... | collective-permute-start | bytes 995336 | tf_op jit(solution)/shard_map/ppermute | solution.py:220
  31.1 6.3 %collective-permute-start.8 = (bf16[4,48,576]{2,1,0:T(8,128)(2,1)S(1)}, bf16[4,48,576]{2,1,0:T(8,128)(2,1)S(1)}, u32[]{:S(2)}, u32[]{:S(2)}) collective-permute-start(bf16[4,48,576]{2,1,0:T(8,128)(2,1)S(1)} %get-tuple-element.27), channel_id=1, source_target_pairs={{0,2},{1,9},{2,0},{3,11},{4,6},{5,13},{6,4},{7,15},{8,10},{9,1},{1... | collective-permute-start | bytes 663560 | tf_op jit(solution)/shard_map/ppermute | solution.py:217
  32.9 8.8 %collective-permute-start.9 = (bf16[4,48,576]{2,1,0:T(8,128)(2,1)S(1)}, bf16[4,48,576]{2,1,0:T(8,128)(2,1)S(1)}, u32[]{:S(2)}, u32[]{:S(2)}) collective-permute-start(bf16[4,48,576]{2,1,0:T(8,128)(2,1)S(1)} %get-tuple-element.28), channel_id=1, source_target_pairs={{0,4},{1,17},{2,6},{3,19},{4,0},{5,21},{6,2},{7,23},{8,12},{9,25},... | collective-permute-start | bytes 663560 | tf_op jit(solution)/shard_map/ppermute | solution.py:217
  33.5 8.2 %collective-permute-start.10 = (bf16[4,48,576]{2,1,0:T(8,128)(2,1)S(1)}, bf16[4,48,576]{2,1,0:T(8,128)(2,1)S(1)}, u32[]{:S(2)}, u32[]{:S(2)}) collective-permute-start(bf16[4,48,576]{2,1,0:T(8,128)(2,1)S(1)} %get-tuple-element.29), channel_id=1, source_target_pairs={{0,6},{1,25},{2,4},{3,27},{4,2},{5,29},{6,0},{7,31},{8,14},{9,17},... | collective-permute-start | bytes 663560 | tf_op jit(solution)/shard_map/ppermute | solution.py:217
  34.6 13.4 %collective-permute-start.14 = (bf16[128,576]{1,0:T(8,128)(2,1)S(1)}, bf16[128,576]{1,0:T(8,128)(2,1)S(1)}, u32[]{:S(2)}, u32[]{:S(2)}) collective-permute-start(bf16[128,576]{1,0:T(8,128)(2,1)S(1)} %get-tuple-element.34), channel_id=1, source_target_pairs={{0,1},{1,0},{2,3},{3,2},{4,5},{5,4},{6,7},{7,6},{8,9},{9,8},{10,11... | collective-permute-start | bytes 442376 | tf_op jit(solution)/shard_map/ppermute | solution.py:220
  41.8 7.0 %collective-permute-start.11 = (bf16[1,48,576]{2,1,0:T(8,128)(2,1)S(1)}, bf16[1,48,576]{2,1,0:T(8,128)(2,1)S(1)}, u32[]{:S(2)}, u32[]{:S(2)}) collective-permute-start(bf16[1,48,576]{2,1,0:T(8,128)(2,1)S(1)} %get-tuple-element.31), channel_id=1, source_target_pairs={{0,8},{1,3},{2,10},{3,1},{4,12},{5,7},{6,14},{7,5},{8,0},{9,11},{1... | collective-permute-start | bytes 165896 | tf_op jit(solution)/shard_map/ppermute | solution.py:217
  41.9 6.9 %collective-permute-start.12 = (bf16[1,48,576]{2,1,0:T(8,128)(2,1)S(1)}, bf16[1,48,576]{2,1,0:T(8,128)(2,1)S(1)}, u32[]{:S(2)}, u32[]{:S(2)}) collective-permute-start(bf16[1,48,576]{2,1,0:T(8,128)(2,1)S(1)} %get-tuple-element.32), channel_id=1, source_target_pairs={{0,16},{1,5},{2,18},{3,7},{4,20},{5,1},{6,22},{7,3},{8,24},{9,13},... | collective-permute-start | bytes 165896 | tf_op jit(solution)/shard_map/ppermute | solution.py:217
  43.4 6.0 %collective-permute-start.13 = (bf16[1,48,576]{2,1,0:T(8,128)(2,1)S(1)}, bf16[1,48,576]{2,1,0:T(8,128)(2,1)S(1)}, u32[]{:S(2)}, u32[]{:S(2)}) collective-permute-start(bf16[1,48,576]{2,1,0:T(8,128)(2,1)S(1)} %get-tuple-element.33), channel_id=1, source_target_pairs={{0,24},{1,7},{2,26},{3,5},{4,28},{5,3},{6,30},{7,1},{8,16},{9,15},... | collective-permute-start | bytes 165896 | tf_op jit(solution)/shard_map/ppermute | solution.py:217

commit v3 on v2

v3 whole, which is shorter than its diff:
```python
import functools

import jax
import jax.numpy as jnp
from jax import lax
from jax.experimental import pallas as pl
from jax.experimental.pallas import tpu as pltpu
from jax.sharding import PartitionSpec as P

LAT = 512
LEVELS = 3

score_scale = 192.0 ** (-0.5)

NT = (((1,), (1,)), ((), ()))
NN = (((1,), (0,)), ((), ()))
TN = (((0,), (0,)), ((), ()))


def dot(a, b, dims):
    return lax.dot_general(a, b, dims, preferred_element_type=jnp.float32)


def vmem(count):
    return [pl.BlockSpec(memory_space=pltpu.VMEM)] * count


def cost(flops, moved):
    return pl.CostEstimate(flops=flops, bytes_accessed=moved, transcendentals=0)


def select_kernel(where_ref, table_ref, out_ref):
    for slot in range(out_ref.shape[0]):
        out_ref[slot] = table_ref[where_ref[slot]]


def select(where, table):
    slots = where.shape[0]
    shape = (slots,) + table.shape[1:]
    return pl.pallas_call(
        select_kernel,
        out_shape=jax.ShapeDtypeStruct(shape, table.dtype),
        in_specs=[pl.BlockSpec(memory_space=pltpu.SMEM)] + vmem(1),
        out_specs=vmem(1)[0],
        compiler_params=pltpu.CompilerParams(vmem_limit_bytes=4 << 20),
        name="select_nodes",
    )(where, table)


def pieces(slice_rows, width):
    lanes = 128
    full, tail = width // lanes, width % lanes
    if slice_rows % 16 or 2 * tail != lanes:
        return [(slice(0, slice_rows), slice(0, width), slice(0, slice_rows), slice(0, width))]
    out = []
    for j in range(full):
        out.append((slice(j * slice_rows, (j + 1) * slice_rows), slice(0, lanes), slice(0, slice_rows), slice(j * lanes, (j + 1) * lanes)))
    half = slice_rows // 2
    last = slice(full * slice_rows, full * slice_rows + half)
    for k in range(2):
        out.append((last, slice(k * tail, (k + 1) * tail), slice(k * half, (k + 1) * half), slice(full * lanes, width)))
    return out


def packed_shape(slice_rows, width):
    parts = pieces(slice_rows, width)
    return (max(p[0].stop for p in parts), max(p[1].stop for p in parts))


def pack_kernel(*refs):
    out_ref = refs[-1]
    for i, ref in enumerate(refs[:-1]):
        for prow, plane, row, col in pieces(*ref.shape[1:]):
            out_ref[i, prow, plane] = ref[0, row, col]


def pack(blocks):
    slice_rows, width = blocks[0].shape[1:]
    shape = (len(blocks),) + packed_shape(slice_rows, width)
    return pl.pallas_call(
        pack_kernel,
        out_shape=jax.ShapeDtypeStruct(shape, blocks[0].dtype),
        in_specs=vmem(len(blocks)),
        out_specs=vmem(1)[0],
        compiler_params=pltpu.CompilerParams(vmem_limit_bytes=4 << 20),
        name="pack_nodes",
    )(*blocks)


def store_terms(ref, first_slot, slice_rows, width, base, head_part, tail_part):
    for level in range(LEVELS):
        offset = base + level * slice_rows
        for prow, plane, row, col in pieces(slice_rows, width):
            rows = slice(offset + row.start, offset + row.stop)
            if col.start >= LAT:
                value = tail_part[rows, col.start - LAT : col.stop - LAT]
            elif col.stop <= LAT:
                value = head_part[rows, col]
            else:
                value = jnp.concatenate([head_part[rows, :], tail_part[rows, :]], axis=1)
            ref[first_slot + level, prow, plane] = value.astype(ref.dtype)


def attend_kernel(parts, leaves, heads, slice_rows, len_ref, own_ref, query_ref, grad_ref, *refs):
    part_refs, refs = refs[:parts], refs[parts:]
    term_refs, refs = refs[: parts - 1], refs[parts - 1 :]
    dscores_ref, probs_ref, keys_ref = refs
    width = own_ref.shape[1]
    leaf_rows = own_ref.shape[0] // leaves
    lines = leaf_rows * heads
    level_rows = LEVELS * slice_rows
    node_rows = parts * level_rows
    sent_rows = node_rows - level_rows
    order = list(range(1, parts)) + [0]
    for leaf in range(leaves):
        for place, part in enumerate(order):
            for level in range(LEVELS):
                offset = place * level_rows + level * slice_rows
                for prow, plane, row, col in pieces(slice_rows, width):
                    rows = slice(offset + row.start, offset + row.stop)
                    keys_ref[leaf, rows, col] = part_refs[part][leaf * LEVELS + level, prow, plane]
        keys_ref[leaf, node_rows:, :] = own_ref[leaf * leaf_rows : (leaf + 1) * leaf_rows, :]
        query = query_ref[leaf * lines : (leaf + 1) * lines, :]
        grad = grad_ref[leaf * lines : (leaf + 1) * lines, :]
        scores = dot(keys_ref[leaf], query, NT) * score_scale
        row_of = lax.broadcasted_iota(jnp.int32, (leaf_rows, lines), 1) // heads
        own_key = lax.broadcasted_iota(jnp.int32, (leaf_rows, lines), 0)
        own_scores = jnp.where(own_key <= row_of, scores[node_rows:], -jnp.inf)
        scores = jnp.concatenate([scores[:node_rows], own_scores], axis=0)
        top = jnp.max(scores, axis=0, keepdims=True)
        expo = jnp.exp(scores - top)
        live = lax.broadcasted_iota(jnp.int32, (1, lines), 1) // heads < len_ref[leaf]
        scale = jnp.where(live, 1.0, 0.0) / jnp.sum(expo, axis=0, keepdims=True)
        probs = expo * scale
        probs_b = probs.astype(jnp.bfloat16)
        probs_ref[leaf] = probs_b
        dprobs = dot(keys_ref[leaf, :, :LAT], grad, NT)
        delta = jnp.sum(probs_b.astype(jnp.float32) * dprobs, axis=0, keepdims=True)
        dscores_ref[leaf] = (score_scale * probs * (dprobs - delta)).astype(jnp.bfloat16)
        if parts > 1:
            head_part, tail_part = key_grads(dscores_ref[leaf, :sent_rows, :], probs_ref[leaf, :sent_rows, :], query, grad)
            for place in range(parts - 1):
                store_terms(term_refs[place], leaf * LEVELS, slice_rows, width, place * level_rows, head_part, tail_part)


def key_grads(dscores, probs_b, query, grad):
    head_part = dot(dscores, query[:, :LAT], NN) + dot(probs_b, grad, NN)
    return head_part, dot(dscores, query[:, LAT:], NN)


def attend(lengths, own, query, grad, parts, leaves, heads, slice_rows):
    rows, width = own.shape
    lines = rows * heads // leaves
    total_keys = LEVELS * len(parts) * slice_rows + rows // leaves
    outs = [jax.ShapeDtypeStruct(parts[0].shape, jnp.bfloat16)] * (len(parts) - 1) + [
        jax.ShapeDtypeStruct((leaves, total_keys, lines), jnp.bfloat16),
        jax.ShapeDtypeStruct((leaves, total_keys, lines), jnp.bfloat16),
        jax.ShapeDtypeStruct((leaves, total_keys, width), jnp.bfloat16),
    ]
    return pl.pallas_call(
        functools.partial(attend_kernel, len(parts), leaves, heads, slice_rows),
        out_shape=outs,
        in_specs=[pl.BlockSpec(memory_space=pltpu.SMEM)] + vmem(3 + len(parts)),
        out_specs=vmem(len(outs)),
        compiler_params=pltpu.CompilerParams(vmem_limit_bytes=40 << 20),
        cost_estimate=cost(2 * rows * heads * total_keys * 3 * width, 8 << 20),
        name="attend",
    )(lengths, own, query, grad, *parts)


def own_kernel(leaves, slice_rows, level_rows, query_ref, grad_ref, dscores_ref, probs_ref, term_ref, own_grad_ref):
    lines = query_ref.shape[0] // leaves
    width = query_ref.shape[1]
    leaf_rows = own_grad_ref.shape[0] // leaves
    first = dscores_ref.shape[1] - leaf_rows - level_rows
    for leaf in range(leaves):
        query = query_ref[leaf * lines : (leaf + 1) * lines, :]
        grad = grad_ref[leaf * lines : (leaf + 1) * lines, :]
        head_part, tail_part = key_grads(dscores_ref[leaf, first:, :], probs_ref[leaf, first:, :], query, grad)
        store_terms(term_ref, leaf * LEVELS, slice_rows, width, 0, head_part, tail_part)
        rows = slice(leaf * leaf_rows, (leaf + 1) * leaf_rows)
        own_grad_ref[rows, :LAT] = head_part[level_rows:].astype(jnp.bfloat16)
        own_grad_ref[rows, LAT:] = tail_part[level_rows:].astype(jnp.bfloat16)


def own_terms(query, grad, dscores, probs, block, slice_rows, rows):
    leaves, total_keys, lines = dscores.shape
    width = query.shape[1]
    level_rows = LEVELS * slice_rows
    outs = [
        jax.ShapeDtypeStruct(block, jnp.float32),
        jax.ShapeDtypeStruct((rows, width), jnp.bfloat16),
    ]
    return pl.pallas_call(
        functools.partial(own_kernel, leaves, slice_rows, level_rows),
        out_shape=outs,
        in_specs=vmem(4),
        out_specs=vmem(2),
        compiler_params=pltpu.CompilerParams(vmem_limit_bytes=24 << 20),
        cost_estimate=cost(2 * leaves * lines * (level_rows + rows // leaves) * 2 * width, 4 << 20),
        name="own_terms",
    )(query, grad, dscores, probs)


def outputs_kernel(leaves, probs_ref, keys_ref, out_ref):
    lines = probs_ref.shape[2]
    for leaf in range(leaves):
        out = dot(probs_ref[leaf], keys_ref[leaf, :, :LAT], TN)
        out_ref[leaf * lines : (leaf + 1) * lines, :] = out.astype(jnp.bfloat16)


def outputs(probs, keys):
    leaves, total_keys, lines = probs.shape
    return pl.pallas_call(
        functools.partial(outputs_kernel, leaves),
        out_shape=jax.ShapeDtypeStruct((leaves * lines, LAT), jnp.bfloat16),
        in_specs=vmem(2),
        out_specs=vmem(1)[0],
        compiler_params=pltpu.CompilerParams(vmem_limit_bytes=24 << 20),
        cost_estimate=cost(2 * leaves * total_keys * lines * LAT, 4 << 20),
        name="attend_outputs",
    )(probs, keys)


def spread_kernel(shares, leaves, where_ref, *refs):
    share_refs, out_refs = refs[:shares], refs[shares:]
    inner = out_refs[0].shape[0]
    for ref in out_refs:
        ref[...] = jnp.zeros_like(ref)
    for level in range(LEVELS):
        slots = [leaf * LEVELS + level for leaf in range(leaves)]
        totals = []
        for slot in slots:
            total = share_refs[0][slot]
            for ref in share_refs[1:]:
                total = total + ref[slot].astype(jnp.float32)
            totals.append(total)
        for i, slot in enumerate(slots):
            total = totals[i]
            for j, other in enumerate(slots):
                if j != i:
                    shared = where_ref[other] == where_ref[slot]
                    total = total + jnp.where(shared, totals[j], 0.0)
            total = total.astype(jnp.bfloat16)
            place = where_ref[slot]
            for k, ref in enumerate(out_refs):

                @pl.when(place // inner == k)
                def _(ref=ref, total=total, place=place):
                    ref[place % inner] = total


def spread(where, shares, outer, inner):
    block = shares[0].shape[1:]
    outs = [jax.ShapeDtypeStruct((inner,) + block, jnp.bfloat16)] * outer
    return pl.pallas_call(
        functools.partial(spread_kernel, len(shares), shares[0].shape[0] // LEVELS),
        out_shape=outs,
        in_specs=[pl.BlockSpec(memory_space=pltpu.SMEM)] + vmem(len(shares)),
        out_specs=vmem(len(outs)),
        compiler_params=pltpu.CompilerParams(vmem_limit_bytes=16 << 20),
        name="spread_terms",
    )(where, *shares)


def merge_kernel(count, *refs):
    got_refs, out_refs = refs[:count], refs[count:]
    for i, ref in enumerate(out_refs):
        total = got_refs[0][i].astype(jnp.float32)
        for got in got_refs[1:]:
            total = total + got[i].astype(jnp.float32)
        ref[0] = total.astype(ref.dtype)


def merge(got):
    inner = got[0].shape[0]
    block = (1,) + got[0].shape[1:]
    outs = [jax.ShapeDtypeStruct(block, jnp.float32)] + [
        jax.ShapeDtypeStruct(block, jnp.bfloat16)
    ] * (inner - 1)
    return pl.pallas_call(
        functools.partial(merge_kernel, len(got)),
        out_shape=outs,
        in_specs=vmem(len(got)),
        out_specs=vmem(len(outs)),
        compiler_params=pltpu.CompilerParams(vmem_limit_bytes=16 << 20),
        name="merge_terms",
    )(*got)


def finish_kernel(keep_ref, *refs):
    out_ref = refs[-1]
    for prow, plane, row, col in pieces(*out_ref.shape[1:]):
        total = keep_ref[0, prow, plane]
        for ref in refs[:-1]:
            total = total + ref[0, prow, plane].astype(jnp.float32)
        out_ref[0, row, col] = total.astype(jnp.bfloat16)


def finish(keep, got, shape):
    return pl.pallas_call(
        finish_kernel,
        out_shape=jax.ShapeDtypeStruct(shape, jnp.bfloat16),
        in_specs=vmem(1 + len(got)),
        out_specs=vmem(1)[0],
        compiler_params=pltpu.CompilerParams(vmem_limit_bytes=4 << 20),
        name="finish_nodes",
    )(keep, *got)


def body(leaf_size, head_size, queries, leaf_latent, node_latent, grad_out, leaf_nodes, leaf_lengths):
    rows, heads, width = queries.shape
    leaves = leaf_nodes.shape[0]
    side = 1
    while side * side < leaf_size:
        side *= 2
    axes = ("leaf", "head")

    def step(value, which, distance):
        pairs = []
        for leaf in range(leaf_size):
            for head in range(head_size):
                far = (which + head) % 2 == 0
                target = leaf ^ (distance * side if far else distance)
                pairs.append((leaf * head_size + head, target * head_size + head))
        return lax.ppermute(value, axes, pairs)

    def swap(value, distance):
        return lax.ppermute(value, "head", [(i, i ^ distance) for i in range(head_size)])

    relative = leaf_nodes.reshape(-1) ^ lax.axis_index("leaf")
    far, near = relative // side, relative % side
    even = lax.axis_index("head") % 2 == 0
    where = jnp.where(even, near * side + far, far * side + near)

    order = list(range(side - 1, 0, -1))
    got = {d: step(node_latent, 0, d) for d in order}
    query = queries.reshape(rows * heads, width)
    got, query, own = lax.optimization_barrier(([got[d] for d in range(1, side)], query, leaf_latent))
    inner = pack([node_latent] + got)
    got = {d: step(inner, 1, d) for d in order}
    table = jnp.concatenate([inner] + [got[d] for d in range(1, side)], axis=0)
    mine = select(where, table)
    parts = [mine] + [swap(mine, d) for d in range(1, head_size)]
    grad = grad_out.reshape(rows * heads, LAT)
    slice_rows = node_latent.shape[1]

    *terms, dscores, probs, keys = attend(leaf_lengths, own, query, grad, parts, leaves, heads, slice_rows)
    shares = [swap(terms[d - 1], d) for d in range(1, head_size)]
    mine, own_grad = own_terms(query, grad, dscores, probs, mine.shape, slice_rows, rows)
    sends = spread(where, [mine] + shares, side, side)
    sends, probs, own_grad = lax.optimization_barrier((sends, probs, own_grad))
    got = {d: step(sends[d], 1, d) for d in order}
    attention = outputs(probs, keys).reshape(rows, heads, LAT)
    got, attention = lax.optimization_barrier(([sends[0]] + [got[d] for d in range(1, side)], attention))
    keep, *sends = merge(got)
    got = {d: step(sends[d - 1], 0, d) for d in order}
    node_grad = finish(keep, [got[d] for d in range(1, side)], node_latent.shape)

    leaf_grad = own_grad
    distance = 1
    while distance < head_size:
        leaf_grad = leaf_grad + swap(leaf_grad, distance)
        distance *= 2
    return (attention, node_grad, leaf_grad)


def solution(mesh):
    return jax.shard_map(
        functools.partial(body, mesh.shape["leaf"], mesh.shape["head"]),
        mesh=mesh,
        in_specs=(
            P("leaf", "head", None),
            P("leaf", None),
            P("leaf", "head", None),
            P("leaf", "head", None),
            P("leaf", None),
            P("leaf"),
        ),
        out_specs=(P("leaf", "head", None), P("leaf", "head", None), P("leaf", None)),
        check_vma=False,
    )
```

time: 50.2 us -> 48.2 us (0.960)
  waiting for transfers between devices: 19.8 us -> 17.8 us
  Pallas kernels: 6.46 us -> 7.66 us
  other arithmetic: 1.63 us -> 0.85 us
    ppermute x12, waiting for transfers between devices: 17.1 us -> 15.7 us  [step(): return lax.ppermute(value, axes, pairs)]
    pallas_call x3 -> x6, Pallas kernels: 4.18 us -> 5.37 us  [the longest x1 2.79 us: attend(): pl.pallas_call(functools.partial(attend_kernel, len(parts), leaves, heads...]
    convert_element_type x1 -> x0, other arithmetic: 0.66 us -> none  [body(): node_grad = total.astype(jnp.bfloat16)]
    ppermute x3, waiting for transfers between devices: 2.74 us -> 2.17 us  [swap(): lax.ppermute(value, 'head', [(i, i ^ distance) for i in range(head_size)])]
  transfers between devices with their start and end apart: 15 -> 15, of which waited for: 9 -> 9; matrix products, arithmetic and copies ran while one was open for 8% -> 8% of each run, Pallas kernels for 4% -> 5%
where the time goes in v3:
time: 48.2 us; the launch traced here: 48.1 us
  waiting for transfers between devices  17.8 us (37%)
  starting transfers between devices  17.7 us (37%)
  Pallas kernels  7.66 us (16%)
  local copies, waits for them, and re-layouts  3.26 us (7%)
  other arithmetic  0.85 us (2%)
  between operations  0.76 us (2%)
    ppermute x12, starting transfers between devices, step(): return lax.ppermute(value, axes, pairs)  17.2 us
    ppermute x12, waiting for transfers between devices, step(): return lax.ppermute(value, axes, pairs)  15.7 us
    unnamed x10, local copies, waits for them, and re-layouts  3.02 us
    pallas_call x1, Pallas kernels, attend(): pl.pallas_call(functools.partial(attend_kernel, len(parts), leaves, heads...  2.79 us
    ppermute x3, waiting for transfers between devices, swap(): lax.ppermute(value, 'head', [(i, i ^ distance) for i in range(head_size)])  2.17 us
    pallas_call x1, Pallas kernels, outputs(): pl.pallas_call(functools.partial(outputs_kernel, leaves), out_shape=jax.S...  1.71 us
  transfers between devices with their start and end apart: 15, of which 9 were waited for; matrix products, arithmetic and copies ran while one was open for 8% of the time, Pallas kernels for 5%

profile of v3, /device:TPU:0, one launch (start us, length us, event | category | flops | bytes accessed | tf_op | source)
XLA Modules:
  0.0 48.1 jit_solution(7706036421788967040)
XLA Ops:
  0.6 4.1 %collective-permute-start.1 = (bf16[1,48,576]{2,1,0:T(8,128)(2,1)}, bf16[1,48,576]{2,1,0:T(8,128)(2,1)S(1)}, u32[]{:S(2)}, u32[]{:S(2)}) collective-permute-start(bf16[1,48,576]{2,1,0:T(8,128)(2,1)} %refs_0_.1), channel_id=1, source_target_pairs={{0,16},{1,5},{2,18},{3,7},{4,20},{5,1},{6,22},{7,3},{8,24},{9,13},... | collective-permute-start | bytes 165896 | tf_op jit(solution)/shard_map/ppermute | solution.py:326
  4.8 1.6 %collective-permute-start = (bf16[1,48,576]{2,1,0:T(8,128)(2,1)}, bf16[1,48,576]{2,1,0:T(8,128)(2,1)S(1)}, u32[]{:S(2)}, u32[]{:S(2)}) collective-permute-start(bf16[1,48,576]{2,1,0:T(8,128)(2,1)} %refs_0_.1), channel_id=1, source_target_pairs={{0,8},{1,3},{2,10},{3,1},{4,12},{5,7},{6,14},{7,5},{8,0},{9,11},{1... | collective-permute-start | bytes 165896 | tf_op jit(solution)/shard_map/ppermute | solution.py:326
  6.4 0.7 %broadcast_xor_fusion = s32[2,3]{1,0:T(2,128)S(1)} fusion(s32[2,3]{1,0:T(2,128)} %param.10, s32[]{:T(128)S(6)} %axis_index.25), kind=kLoop, calls=%fused_computation.7 | loop fusion | flops 6 | bytes 52 | tf_op jit(solution)/shard_map/xor | solution.py:331
  7.1 2.2 %copy.9 = bf16[128,8,576]{2,1,0:T(8,128)(2,1)S(1)} copy(bf16[128,8,576]{0,2,1:T(8,128)(2,1)} %param.6) | data formatting | bytes 2359296 | tf_op args[0]
  9.3 3.2 %collective-permute-done.2.refs_3_ = bf16[1,48,576]{2,1,0:T(8,128)(2,1)S(1)} collective-permute-done((bf16[1,48,576]{2,1,0:T(8,128)(2,1)}, bf16[1,48,576]{2,1,0:T(8,128)(2,1)S(1)}, u32[]{:S(2)}, u32[]{:S(2)}) %collective-permute-start.2) | collective-permute-done | bytes 55328 | tf_op jit(solution)/shard_map/ppermute | solution.py:326
  12.7 2.9 %collective-permute-start.5 = (bf16[4,216,128]{2,1,0:T(8,128)(2,1)S(1)}, bf16[4,216,128]{2,1,0:T(8,128)(2,1)S(1)}, u32[]{:S(2)}, u32[]{:S(2)}) collective-permute-start(bf16[4,216,128]{2,1,0:T(8,128)(2,1)S(1)} %pack_nodes.1), channel_id=1, source_target_pairs={{0,6},{1,25},{2,4},{3,27},{4,2},{5,29},{6,0},{7,31},{8,14},{9,17},... | collective-permute-start | bytes 663560 | tf_op jit(solution)/shard_map/ppermute | solution.py:326
  15.6 0.2 collective-permute-start.4
  15.8 0.4 collective-permute-start.3
  16.3 3.3 %collective-permute-done.5 = bf16[4,216,128]{2,1,0:T(8,128)(2,1)S(1)} collective-permute-done((bf16[4,216,128]{2,1,0:T(8,128)(2,1)S(1)}, bf16[4,216,128]{2,1,0:T(8,128)(2,1)S(1)}, u32[]{:S(2)}, u32[]{:S(2)}) %collective-permute-start.5) | collective-permute-done | bytes 221216 | tf_op jit(solution)/shard_map/ppermute | solution.py:326
  19.6 2.3 %collective-permute-done.4 = bf16[4,216,128]{2,1,0:T(8,128)(2,1)S(1)} collective-permute-done((bf16[4,216,128]{2,1,0:T(8,128)(2,1)S(1)}, bf16[4,216,128]{2,1,0:T(8,128)(2,1)S(1)}, u32[]{:S(2)}, u32[]{:S(2)}) %collective-permute-start.4) | collective-permute-done | bytes 221216 | tf_op jit(solution)/shard_map/ppermute | solution.py:326
  21.9 0.2 collective-permute-done.3
  22.3 0.6 %select_nodes.1.refs_0_ = bf16[6,216,128]{2,1,0:T(8,128)(2,1)S(1)} custom-call(s32[6]{0:T(128)S(1)} %broadcast_select_fusion.where_ref, bf16[16,216,128]{2,1,0:T(8,128)(2,1)S(1)} %pad_maximum_fusion.table_ref), custom_call_target="tpu_custom_call" | custom-call | tf_op jit(solution)/shard_map/select_nodes/pallas_call | solution.py:40
  23.0 0.2 copy.10.own_ref
  23.1 1.4 %collective-permute-done.6.refs_1_ = bf16[6,216,128]{2,1,0:T(8,128)(2,1)S(1)} collective-permute-done((bf16[6,216,128]{2,1,0:T(8,128)(2,1)S(1)}, bf16[6,216,128]{2,1,0:T(8,128)(2,1)S(1)}, u32[]{:S(2)}, u32[]{:S(2)}) %collective-permute-start.6) | collective-permute-done | bytes 331808 | tf_op jit(solution)/shard_map/ppermute | solution.py:329
  24.6 2.8 %attend.1 = (bf16[6,216,128]{2,1,0:T(8,128)(2,1)S(1)}, bf16[2,352,512]{2,1,0:T(8,128)(2,1)S(1)}, bf16[2,352,512]{2,1,0:T(8,128)(2,1)S(1)}, bf16[2,352,576]{2,1,0:T(8,128)(2,1)S(1)}) custom-call(s32[2]{0:T(128)S(1)} %copy-done.2, bf16[128,576]{1,0:T(8,128)(2,1)S(1)} %copy.10.own_ref, bf16[1024,576]{1,0:T(8,128)(2,1)S(1)} %bitcast.3, ...), custom_call_target="tpu_custom_call" | custom-call | flops 1245708288 | bytes 8388608 | tf_op jit(solution)/shard_map/attend/pallas_call | solution.py:160
  27.4 0.2 collective-permute-start.7
  27.6 0.8 %own_terms.1 = (f32[6,216,128]{2,1,0:T(8,128)S(1)}, bf16[128,576]{1,0:T(8,128)(2,1)S(1)}) custom-call(bf16[1024,576]{1,0:T(8,128)(2,1)S(1)} %bitcast.4, bf16[1024,512]{1,0:T(8,128)(2,1)S(1)} %bitcast.6, bf16[2,352,512]{2,1,0:T(8,128)(2,1)S(1)} %get-tuple-element.38.dscores_ref, bf16[2,352,512]{2,1,0:T(8,128)(2,1)S(1)} %get-tuple-element.51.probs_ref), custom_call_target="tpu_custom_call" | custom-call | flops 490733568 | bytes 4194304 | tf_op jit(solution)/shard_map/own_terms/pallas_call | solution.py:194
  28.3 0.7 %collective-permute-done.7.refs_1_ = bf16[6,216,128]{2,1,0:T(8,128)(2,1)S(1)} collective-permute-done((bf16[6,216,128]{2,1,0:T(8,128)(2,1)S(1)}, bf16[6,216,128]{2,1,0:T(8,128)(2,1)S(1)}, u32[]{:S(2)}, u32[]{:S(2)}) %collective-permute-start.7) | collective-permute-done | bytes 331808 | tf_op jit(solution)/shard_map/ppermute | solution.py:329
  29.1 0.9 %spread_terms.1 = (bf16[4,216,128]{2,1,0:T(8,128)(2,1)S(1)}, bf16[4,216,128]{2,1,0:T(8,128)(2,1)S(1)}, bf16[4,216,128]{2,1,0:T(8,128)(2,1)S(1)}, bf16[4,216,128]{2,1,0:T(8,128)(2,1)S(1)}) custom-call(s32[6]{0:T(128)S(1)} %broadcast_select_fusion.where_ref, f32[6,216,128]{2,1,0:T(8,128)S(1)} %get-tuple-element.40.refs_0_, ...), custom_call_target="tpu_custom_call" | custom-call | tf_op jit(solution)/shard_map/spread_terms/pallas_call | solution.py:256
  29.9 1.8 %collective-permute-start.8 = (bf16[4,216,128]{2,1,0:T(8,128)(2,1)S(1)}, bf16[4,216,128]{2,1,0:T(8,128)(2,1)S(1)}, u32[]{:S(2)}, u32[]{:S(2)}) collective-permute-start(bf16[4,216,128]{2,1,0:T(8,128)(2,1)S(1)} %get-tuple-element.48), channel_id=1, source_target_pairs={{0,2},{1,9},{2,0},{3,11},{4,6},{5,13},{6,4},{7,15},{8,10},{9,1},{1... | collective-permute-start | bytes 663560 | tf_op jit(solution)/shard_map/ppermute | solution.py:326
  31.7 0.6 %collective-permute-start.9 = (bf16[4,216,128]{2,1,0:T(8,128)(2,1)S(1)}, bf16[4,216,128]{2,1,0:T(8,128)(2,1)S(1)}, u32[]{:S(2)}, u32[]{:S(2)}) collective-permute-start(bf16[4,216,128]{2,1,0:T(8,128)(2,1)S(1)} %get-tuple-element.49), channel_id=1, source_target_pairs={{0,4},{1,17},{2,6},{3,19},{4,0},{5,21},{6,2},{7,23},{8,12},{9,25},... | collective-permute-start | bytes 663560 | tf_op jit(solution)/shard_map/ppermute | solution.py:326
  32.4 1.1 %collective-permute-start.10 = (bf16[4,216,128]{2,1,0:T(8,128)(2,1)S(1)}, bf16[4,216,128]{2,1,0:T(8,128)(2,1)S(1)}, u32[]{:S(2)}, u32[]{:S(2)}) collective-permute-start(bf16[4,216,128]{2,1,0:T(8,128)(2,1)S(1)} %get-tuple-element.50), channel_id=1, source_target_pairs={{0,6},{1,25},{2,4},{3,27},{4,2},{5,29},{6,0},{7,31},{8,14},{9,17},... | collective-permute-start | bytes 663560 | tf_op jit(solution)/shard_map/ppermute | solution.py:326
  33.5 0.2 collective-permute-start.14
  33.7 1.7 %attend_outputs.1 = bf16[1024,512]{1,0:T(8,128)(2,1)} custom-call(bf16[2,352,512]{2,1,0:T(8,128)(2,1)S(1)} %get-tuple-element.51.probs_ref, bf16[2,352,576]{2,1,0:T(8,128)(2,1)S(1)} %get-tuple-element.52.keys_ref), custom_call_target="tpu_custom_call" | custom-call | flops 369098752 | bytes 4194304 | tf_op jit(solution)/shard_map/attend_outputs/pallas_call | solution.py:214
  35.4 0.5 %collective-permute-done.8.refs_1_ = bf16[4,216,128]{2,1,0:T(8,128)(2,1)S(1)} collective-permute-done((bf16[4,216,128]{2,1,0:T(8,128)(2,1)S(1)}, bf16[4,216,128]{2,1,0:T(8,128)(2,1)S(1)}, u32[]{:S(2)}, u32[]{:S(2)}) %collective-permute-start.8) | collective-permute-done | bytes 221216 | tf_op jit(solution)/shard_map/ppermute | solution.py:326
  35.9 4.1 %collective-permute-done.9.refs_2_ = bf16[4,216,128]{2,1,0:T(8,128)(2,1)S(1)} collective-permute-done((bf16[4,216,128]{2,1,0:T(8,128)(2,1)S(1)}, bf16[4,216,128]{2,1,0:T(8,128)(2,1)S(1)}, u32[]{:S(2)}, u32[]{:S(2)}) %collective-permute-start.9) | collective-permute-done | bytes 221216 | tf_op jit(solution)/shard_map/ppermute | solution.py:326
  40.1 0.1 merge_terms.1
  40.3 1.0 %collective-permute-start.12 = (bf16[1,216,128]{2,1,0:T(8,128)(2,1)S(1)}, bf16[1,216,128]{2,1,0:T(8,128)(2,1)S(1)}, u32[]{:S(2)}, u32[]{:S(2)}) collective-permute-start(bf16[1,216,128]{2,1,0:T(8,128)(2,1)S(1)} %get-tuple-element.60), channel_id=1, source_target_pairs={{0,16},{1,5},{2,18},{3,7},{4,20},{5,1},{6,22},{7,3},{8,24},{9,13},... | collective-permute-start | bytes 165896 | tf_op jit(solution)/shard_map/ppermute | solution.py:326
  41.3 3.3 %collective-permute-start.13 = (bf16[1,216,128]{2,1,0:T(8,128)(2,1)S(1)}, bf16[1,216,128]{2,1,0:T(8,128)(2,1)S(1)}, u32[]{:S(2)}, u32[]{:S(2)}) collective-permute-start(bf16[1,216,128]{2,1,0:T(8,128)(2,1)S(1)} %get-tuple-element.61), channel_id=1, source_target_pairs={{0,24},{1,7},{2,26},{3,5},{4,28},{5,3},{6,30},{7,1},{8,16},{9,15},... | collective-permute-start | bytes 165896 | tf_op jit(solution)/shard_map/ppermute | solution.py:326
  44.7 0.8 %copy.11 = bf16[128,576]{0,1:T(8,128)(2,1)} copy(bf16[128,576]{1,0:T(8,128)(2,1)S(1)} %add.24) | data formatting | bytes 294912
  45.5 1.9 %collective-permute-done.13.refs_2_ = bf16[1,216,128]{2,1,0:T(8,128)(2,1)S(1)} collective-permute-done((bf16[1,216,128]{2,1,0:T(8,128)(2,1)S(1)}, bf16[1,216,128]{2,1,0:T(8,128)(2,1)S(1)}, u32[]{:S(2)}, u32[]{:S(2)}) %collective-permute-start.13) | collective-permute-done | bytes 55328 | tf_op jit(solution)/shard_map/ppermute | solution.py:326
  47.4 0.7 %finish_nodes.1 = bf16[1,48,576]{2,1,0:T(8,128)(2,1)} custom-call(f32[1,216,128]{2,1,0:T(8,128)S(1)} %get-tuple-element.58.keep_ref, bf16[1,216,128]{2,1,0:T(8,128)(2,1)S(1)} %collective-permute-done.11.refs_0_, bf16[1,216,128]{2,1,0:T(8,128)(2,1)S(1)} %collective-permute-done.12.refs_1_, bf16[1,216,128]{2,1,0:T(8,128)(2,1)S(1)} %collective-permute-done.13.refs_2_), custom_call_target="tpu_custom_call" | custom-call | tf_op jit(solution)/shard_map/finish_nodes/pallas_call | solution.py:301
  (22 shorter events, 0.5 us)
Async XLA Ops:
  0.6 12.0 %copy-start.1 = (bf16[1,48,576]{2,1,0:T(8,128)(2,1)S(1)}, bf16[1,48,576]{2,1,0:T(8,128)(2,1)}, u32[]{:S(2)}) copy-start(bf16[1,48,576]{2,1,0:T(8,128)(2,1)} %refs_0_.1) | copy-start | bytes 165892
  0.6 8.7 %collective-permute-start.1 = (bf16[1,48,576]{2,1,0:T(8,128)(2,1)}, bf16[1,48,576]{2,1,0:T(8,128)(2,1)S(1)}, u32[]{:S(2)}, u32[]{:S(2)}) collective-permute-start(bf16[1,48,576]{2,1,0:T(8,128)(2,1)} %refs_0_.1), channel_id=1, source_target_pairs={{0,16},{1,5},{2,18},{3,7},{4,20},{5,1},{6,22},{7,3},{8,24},{9,13},... | collective-permute-start | bytes 165896 | tf_op jit(solution)/shard_map/ppermute | solution.py:326
  4.8 4.6 %collective-permute-start = (bf16[1,48,576]{2,1,0:T(8,128)(2,1)}, bf16[1,48,576]{2,1,0:T(8,128)(2,1)S(1)}, u32[]{:S(2)}, u32[]{:S(2)}) collective-permute-start(bf16[1,48,576]{2,1,0:T(8,128)(2,1)} %refs_0_.1), channel_id=1, source_target_pairs={{0,8},{1,3},{2,10},{3,1},{4,12},{5,7},{6,14},{7,5},{8,0},{9,11},{1... | collective-permute-start | bytes 165896 | tf_op jit(solution)/shard_map/ppermute | solution.py:326
  6.3 6.2 %collective-permute-start.2 = (bf16[1,48,576]{2,1,0:T(8,128)(2,1)}, bf16[1,48,576]{2,1,0:T(8,128)(2,1)S(1)}, u32[]{:S(2)}, u32[]{:S(2)}) collective-permute-start(bf16[1,48,576]{2,1,0:T(8,128)(2,1)} %refs_0_.1), channel_id=1, source_target_pairs={{0,24},{1,7},{2,26},{3,5},{4,28},{5,3},{6,30},{7,1},{8,16},{9,15},... | collective-permute-start | bytes 165896 | tf_op jit(solution)/shard_map/ppermute | solution.py:326
  12.7 6.9 %collective-permute-start.5 = (bf16[4,216,128]{2,1,0:T(8,128)(2,1)S(1)}, bf16[4,216,128]{2,1,0:T(8,128)(2,1)S(1)}, u32[]{:S(2)}, u32[]{:S(2)}) collective-permute-start(bf16[4,216,128]{2,1,0:T(8,128)(2,1)S(1)} %pack_nodes.1), channel_id=1, source_target_pairs={{0,6},{1,25},{2,4},{3,27},{4,2},{5,29},{6,0},{7,31},{8,14},{9,17},... | collective-permute-start | bytes 663560 | tf_op jit(solution)/shard_map/ppermute | solution.py:326
  15.6 6.4 %collective-permute-start.4 = (bf16[4,216,128]{2,1,0:T(8,128)(2,1)S(1)}, bf16[4,216,128]{2,1,0:T(8,128)(2,1)S(1)}, u32[]{:S(2)}, u32[]{:S(2)}) collective-permute-start(bf16[4,216,128]{2,1,0:T(8,128)(2,1)S(1)} %pack_nodes.1), channel_id=1, source_target_pairs={{0,4},{1,17},{2,6},{3,19},{4,0},{5,21},{6,2},{7,23},{8,12},{9,25},... | collective-permute-start | bytes 663560 | tf_op jit(solution)/shard_map/ppermute | solution.py:326
  15.8 6.4 %collective-permute-start.3 = (bf16[4,216,128]{2,1,0:T(8,128)(2,1)S(1)}, bf16[4,216,128]{2,1,0:T(8,128)(2,1)S(1)}, u32[]{:S(2)}, u32[]{:S(2)}) collective-permute-start(bf16[4,216,128]{2,1,0:T(8,128)(2,1)S(1)} %pack_nodes.1), channel_id=1, source_target_pairs={{0,2},{1,9},{2,0},{3,11},{4,6},{5,13},{6,4},{7,15},{8,10},{9,1},{1... | collective-permute-start | bytes 663560 | tf_op jit(solution)/shard_map/ppermute | solution.py:326
  16.2 6.7 %copy-start.3 = (bf16[128,576]{0,1:T(8,128)(2,1)S(1)}, bf16[128,576]{0,1:T(8,128)(2,1)}, u32[]{:S(2)}) copy-start(bf16[128,576]{0,1:T(8,128)(2,1)} %param.7) | copy-start | bytes 442372
  16.3 8.3 %copy-start = (bf16[128,8,512]{2,1,0:T(8,128)(2,1)S(1)}, bf16[128,8,512]{2,1,0:T(8,128)(2,1)}, u32[]{:S(2)}) copy-start(bf16[128,8,512]{2,1,0:T(8,128)(2,1)} %param.9) | copy-start | bytes 3145732
  16.3 8.3 %copy-start.2 = (s32[2]{0:T(128)S(1)}, s32[2]{0:T(128)}, u32[]{:S(2)}) copy-start(s32[2]{0:T(128)} %len_ref.1) | copy-start | bytes 28
  22.9 1.7 %collective-permute-start.6 = (bf16[6,216,128]{2,1,0:T(8,128)(2,1)S(1)}, bf16[6,216,128]{2,1,0:T(8,128)(2,1)S(1)}, u32[]{:S(2)}, u32[]{:S(2)}) collective-permute-start(bf16[6,216,128]{2,1,0:T(8,128)(2,1)S(1)} %select_nodes.1.refs_0_), channel_id=1, source_target_pairs={{0,1},{1,0},{2,3},{3,2},{4,5},{5,4},{6,7},{7,6},{8,9},{9,8},{10,11... | collective-permute-start | bytes 995336 | tf_op jit(solution)/shard_map/ppermute | solution.py:329
  27.4 1.7 %collective-permute-start.7 = (bf16[6,216,128]{2,1,0:T(8,128)(2,1)S(1)}, bf16[6,216,128]{2,1,0:T(8,128)(2,1)S(1)}, u32[]{:S(2)}, u32[]{:S(2)}) collective-permute-start(bf16[6,216,128]{2,1,0:T(8,128)(2,1)S(1)} %get-tuple-element.41), channel_id=1, source_target_pairs={{0,1},{1,0},{2,3},{3,2},{4,5},{5,4},{6,7},{7,6},{8,9},{9,8},{10,11... | collective-permute-start | bytes 995336 | tf_op jit(solution)/shard_map/ppermute | solution.py:329
  29.9 6.0 %collective-permute-start.8 = (bf16[4,216,128]{2,1,0:T(8,128)(2,1)S(1)}, bf16[4,216,128]{2,1,0:T(8,128)(2,1)S(1)}, u32[]{:S(2)}, u32[]{:S(2)}) collective-permute-start(bf16[4,216,128]{2,1,0:T(8,128)(2,1)S(1)} %get-tuple-element.48), channel_id=1, source_target_pairs={{0,2},{1,9},{2,0},{3,11},{4,6},{5,13},{6,4},{7,15},{8,10},{9,1},{1... | collective-permute-start | bytes 663560 | tf_op jit(solution)/shard_map/ppermute | solution.py:326
  31.7 8.3 %collective-permute-start.9 = (bf16[4,216,128]{2,1,0:T(8,128)(2,1)S(1)}, bf16[4,216,128]{2,1,0:T(8,128)(2,1)S(1)}, u32[]{:S(2)}, u32[]{:S(2)}) collective-permute-start(bf16[4,216,128]{2,1,0:T(8,128)(2,1)S(1)} %get-tuple-element.49), channel_id=1, source_target_pairs={{0,4},{1,17},{2,6},{3,19},{4,0},{5,21},{6,2},{7,23},{8,12},{9,25},... | collective-permute-start | bytes 663560 | tf_op jit(solution)/shard_map/ppermute | solution.py:326
  32.4 7.7 %collective-permute-start.10 = (bf16[4,216,128]{2,1,0:T(8,128)(2,1)S(1)}, bf16[4,216,128]{2,1,0:T(8,128)(2,1)S(1)}, u32[]{:S(2)}, u32[]{:S(2)}) collective-permute-start(bf16[4,216,128]{2,1,0:T(8,128)(2,1)S(1)} %get-tuple-element.50), channel_id=1, source_target_pairs={{0,6},{1,25},{2,4},{3,27},{4,2},{5,29},{6,0},{7,31},{8,14},{9,17},... | collective-permute-start | bytes 663560 | tf_op jit(solution)/shard_map/ppermute | solution.py:326
  33.5 11.1 %collective-permute-start.14 = (bf16[128,576]{1,0:T(8,128)(2,1)S(1)}, bf16[128,576]{1,0:T(8,128)(2,1)S(1)}, u32[]{:S(2)}, u32[]{:S(2)}) collective-permute-start(bf16[128,576]{1,0:T(8,128)(2,1)S(1)} %get-tuple-element.62), channel_id=1, source_target_pairs={{0,1},{1,0},{2,3},{3,2},{4,5},{5,4},{6,7},{7,6},{8,9},{9,8},{10,11... | collective-permute-start | bytes 442376 | tf_op jit(solution)/shard_map/ppermute | solution.py:329
  40.2 5.3 %collective-permute-start.11 = (bf16[1,216,128]{2,1,0:T(8,128)(2,1)S(1)}, bf16[1,216,128]{2,1,0:T(8,128)(2,1)S(1)}, u32[]{:S(2)}, u32[]{:S(2)}) collective-permute-start(bf16[1,216,128]{2,1,0:T(8,128)(2,1)S(1)} %get-tuple-element.59), channel_id=1, source_target_pairs={{0,8},{1,3},{2,10},{3,1},{4,12},{5,7},{6,14},{7,5},{8,0},{9,11},{1... | collective-permute-start | bytes 165896 | tf_op jit(solution)/shard_map/ppermute | solution.py:326
  40.3 5.2 %collective-permute-start.12 = (bf16[1,216,128]{2,1,0:T(8,128)(2,1)S(1)}, bf16[1,216,128]{2,1,0:T(8,128)(2,1)S(1)}, u32[]{:S(2)}, u32[]{:S(2)}) collective-permute-start(bf16[1,216,128]{2,1,0:T(8,128)(2,1)S(1)} %get-tuple-element.60), channel_id=1, source_target_pairs={{0,16},{1,5},{2,18},{3,7},{4,20},{5,1},{6,22},{7,3},{8,24},{9,13},... | collective-permute-start | bytes 165896 | tf_op jit(solution)/shard_map/ppermute | solution.py:326
  41.3 6.1 %collective-permute-start.13 = (bf16[1,216,128]{2,1,0:T(8,128)(2,1)S(1)}, bf16[1,216,128]{2,1,0:T(8,128)(2,1)S(1)}, u32[]{:S(2)}, u32[]{:S(2)}) collective-permute-start(bf16[1,216,128]{2,1,0:T(8,128)(2,1)S(1)} %get-tuple-element.61), channel_id=1, source_target_pairs={{0,24},{1,7},{2,26},{3,5},{4,28},{5,3},{6,30},{7,1},{8,16},{9,15},... | collective-permute-start | bytes 165896 | tf_op jit(solution)/shard_map/ppermute | solution.py:326

commit v4 on v3

--- a/solution.py
+++ b/solution.py
@@ -31,16 +31,16 @@
 
 def select_kernel(where_ref, table_ref, out_ref):
     for slot in range(out_ref.shape[0]):
-        out_ref[slot] = table_ref[where_ref[slot]]
+        out_ref[slot] = table_ref[where_ref[0, slot]]
 
 
 def select(where, table):
-    slots = where.shape[0]
+    slots = where.shape[1]
     shape = (slots,) + table.shape[1:]
     return pl.pallas_call(
         select_kernel,
         out_shape=jax.ShapeDtypeStruct(shape, table.dtype),
-        in_specs=[pl.BlockSpec(memory_space=pltpu.SMEM)] + vmem(1),
+        in_specs=vmem(2),
         out_specs=vmem(1)[0],
         compiler_params=pltpu.CompilerParams(vmem_limit_bytes=4 << 20),
         name="select_nodes",
@@ -101,7 +101,7 @@
             ref[first_slot + level, prow, plane] = value.astype(ref.dtype)
 
 
-def attend_kernel(parts, leaves, heads, slice_rows, len_ref, own_ref, query_ref, grad_ref, *refs):
+def attend_kernel(parts, leaves, heads, slice_rows, live_ref, own_ref, query_ref, grad_ref, *refs):
     part_refs, refs = refs[:parts], refs[parts:]
     term_refs, refs = refs[: parts - 1], refs[parts - 1 :]
     dscores_ref, probs_ref, keys_ref = refs
@@ -129,8 +129,7 @@
         scores = jnp.concatenate([scores[:node_rows], own_scores], axis=0)
         top = jnp.max(scores, axis=0, keepdims=True)
         expo = jnp.exp(scores - top)
-        live = lax.broadcasted_iota(jnp.int32, (1, lines), 1) // heads < len_ref[leaf]
-        scale = jnp.where(live, 1.0, 0.0) / jnp.sum(expo, axis=0, keepdims=True)
+        scale = live_ref[leaf] / jnp.sum(expo, axis=0, keepdims=True)
         probs = expo * scale
         probs_b = probs.astype(jnp.bfloat16)
         probs_ref[leaf] = probs_b
@@ -148,7 +147,7 @@
     return head_part, dot(dscores, query[:, LAT:], NN)
 
 
-def attend(lengths, own, query, grad, parts, leaves, heads, slice_rows):
+def attend(live, own, query, grad, parts, leaves, heads, slice_rows):
     rows, width = own.shape
     lines = rows * heads // leaves
     total_keys = LEVELS * len(parts) * slice_rows + rows // leaves
@@ -160,12 +159,12 @@
     return pl.pallas_call(
         functools.partial(attend_kernel, len(parts), leaves, heads, slice_rows),
         out_shape=outs,
-        in_specs=[pl.BlockSpec(memory_space=pltpu.SMEM)] + vmem(3 + len(parts)),
+        in_specs=vmem(4 + len(parts)),
         out_specs=vmem(len(outs)),
         compiler_params=pltpu.CompilerParams(vmem_limit_bytes=40 << 20),
         cost_estimate=cost(2 * rows * heads * total_keys * 3 * width, 8 << 20),
         name="attend",
-    )(lengths, own, query, grad, *parts)
+    )(live, own, query, grad, *parts)
 
 
 def own_kernel(leaves, slice_rows, level_rows, query_ref, grad_ref, dscores_ref, probs_ref, term_ref, own_grad_ref):
@@ -229,6 +228,7 @@
         ref[...] = jnp.zeros_like(ref)
     for level in range(LEVELS):
         slots = [leaf * LEVELS + level for leaf in range(leaves)]
+        places = {slot: where_ref[0, slot] for slot in slots}
         totals = []
         for slot in slots:
             total = share_refs[0][slot]
@@ -239,10 +239,10 @@
             total = totals[i]
             for j, other in enumerate(slots):
                 if j != i:
-                    shared = where_ref[other] == where_ref[slot]
+                    shared = places[other] == places[slot]
                     total = total + jnp.where(shared, totals[j], 0.0)
             total = total.astype(jnp.bfloat16)
-            place = where_ref[slot]
+            place = places[slot]
             for k, ref in enumerate(out_refs):
 
                 @pl.when(place // inner == k)
@@ -256,7 +256,7 @@
     return pl.pallas_call(
         functools.partial(spread_kernel, len(shares), shares[0].shape[0] // LEVELS),
         out_shape=outs,
-        in_specs=[pl.BlockSpec(memory_space=pltpu.SMEM)] + vmem(len(shares)),
+        in_specs=vmem(1 + len(shares)),
         out_specs=vmem(len(outs)),
         compiler_params=pltpu.CompilerParams(vmem_limit_bytes=16 << 20),
         name="spread_terms",
@@ -328,11 +328,13 @@
     def swap(value, distance):
         return lax.ppermute(value, "head", [(i, i ^ distance) for i in range(head_size)])
 
-    relative = leaf_nodes.reshape(-1) ^ lax.axis_index("leaf")
+    relative = leaf_nodes.reshape(1, -1) ^ lax.axis_index("leaf")
     far, near = relative // side, relative % side
     even = lax.axis_index("head") % 2 == 0
     where = jnp.where(even, near * side + far, far * side + near)
 
+    live = jnp.arange(rows * heads // leaves, dtype=jnp.int32) // heads < leaf_lengths[:, None, None]
+    live = live.astype(jnp.float32)
     order = list(range(side - 1, 0, -1))
     got = {d: step(node_latent, 0, d) for d in order}
     query = queries.reshape(rows * heads, width)
@@ -345,17 +347,17 @@
     grad = grad_out.reshape(rows * heads, LAT)
     slice_rows = node_latent.shape[1]
 
-    *terms, dscores, probs, keys = attend(leaf_lengths, own, query, grad, parts, leaves, heads, slice_rows)
+    *terms, dscores, probs, keys = attend(live, own, query, grad, parts, leaves, heads, slice_rows)
     shares = [swap(terms[d - 1], d) for d in range(1, head_size)]
     mine, own_grad = own_terms(query, grad, dscores, probs, mine.shape, slice_rows, rows)
     sends = spread(where, [mine] + shares, side, side)
     sends, probs, own_grad = lax.optimization_barrier((sends, probs, own_grad))
     got = {d: step(sends[d], 1, d) for d in order}
     attention = outputs(probs, keys).reshape(rows, heads, LAT)
-    got, attention = lax.optimization_barrier(([sends[0]] + [got[d] for d in range(1, side)], attention))
+    got, attention = lax.optimization_barrier(([sends[0]] + [got[d] for d in order], attention))
     keep, *sends = merge(got)
     got = {d: step(sends[d - 1], 0, d) for d in order}
-    node_grad = finish(keep, [got[d] for d in range(1, side)], node_latent.shape)
+    node_grad = finish(keep, [got[d] for d in (*range(2, side), 1)], node_latent.shape)
 
     leaf_grad = own_grad
     distance = 1

time: 48.2 us -> 45.9 us (0.952)
  Pallas kernels: 7.66 us -> 6.38 us
  starting transfers between devices: 17.7 us -> 16.8 us
  waiting for transfers between devices: 17.8 us -> 17.3 us
    ppermute x12, starting transfers between devices: 17.2 us -> 16.3 us  [step(): return lax.ppermute(value, axes, pairs)]
    pallas_call x1, Pallas kernels: 2.79 us -> 2.3 us  [attend(): pl.pallas_call(functools.partial(attend_kernel, len(parts), leaves, heads...]
  transfers between devices with their start and end apart: 15 -> 15, of which waited for: 9 -> 11; matrix products, arithmetic and copies ran while one was open for 8% -> 9% of each run, Pallas kernels for 5% -> 6%
where the time goes in v4:
time: 45.9 us; the launch traced here: 45.4 us
  waiting for transfers between devices  17.3 us (38%)
  starting transfers between devices  16.8 us (37%)
  Pallas kernels  6.38 us (14%)
  local copies, waits for them, and re-layouts  3.27 us (7%)
  other arithmetic  0.93 us (2%)
  between operations  0.76 us (2%)
    ppermute x12, starting transfers between devices, step(): return lax.ppermute(value, axes, pairs)  16.3 us
    ppermute x12, waiting for transfers between devices, step(): return lax.ppermute(value, axes, pairs)  15.2 us
    unnamed x10, local copies, waits for them, and re-layouts  3.02 us
    pallas_call x1, Pallas kernels, attend(): pl.pallas_call(functools.partial(attend_kernel, len(parts), leaves, heads...  2.3 us
    ppermute x3, waiting for transfers between devices, swap(): lax.ppermute(value, 'head', [(i, i ^ distance) for i in range(head_size)])  2.09 us
    pallas_call x1, Pallas kernels, outputs(): pl.pallas_call(functools.partial(outputs_kernel, leaves), out_shape=jax.S...  1.71 us
  transfers between devices with their start and end apart: 15, of which 11 were waited for; matrix products, arithmetic and copies ran while one was open for 9% of the time, Pallas kernels for 6%

profile of v4, /device:TPU:0, one launch (start us, length us, event | category | flops | bytes accessed | tf_op | source)
XLA Modules:
  0.0 45.4 jit_solution(12993934955919537509)
XLA Ops:
  0.6 4.1 %collective-permute-start.1 = (bf16[1,48,576]{2,1,0:T(8,128)(2,1)}, bf16[1,48,576]{2,1,0:T(8,128)(2,1)S(1)}, u32[]{:S(2)}, u32[]{:S(2)}) collective-permute-start(bf16[1,48,576]{2,1,0:T(8,128)(2,1)} %refs_0_.1), channel_id=1, source_target_pairs={{0,16},{1,5},{2,18},{3,7},{4,20},{5,1},{6,22},{7,3},{8,24},{9,13},... | collective-permute-start | bytes 165896 | tf_op jit(solution)/shard_map/ppermute | solution.py:326
  4.8 1.6 %collective-permute-start = (bf16[1,48,576]{2,1,0:T(8,128)(2,1)}, bf16[1,48,576]{2,1,0:T(8,128)(2,1)S(1)}, u32[]{:S(2)}, u32[]{:S(2)}) collective-permute-start(bf16[1,48,576]{2,1,0:T(8,128)(2,1)} %refs_0_.1), channel_id=1, source_target_pairs={{0,8},{1,3},{2,10},{3,1},{4,12},{5,7},{6,14},{7,5},{8,0},{9,11},{1... | collective-permute-start | bytes 165896 | tf_op jit(solution)/shard_map/ppermute | solution.py:326
  6.4 0.7 %broadcast_xor_fusion = s32[2,3]{1,0:T(2,128)S(1)} fusion(s32[2,3]{1,0:T(2,128)} %param.10, s32[]{:T(128)S(6)} %axis_index.25), kind=kLoop, calls=%fused_computation.15 | loop fusion | flops 6 | bytes 52 | tf_op jit(solution)/shard_map/xor | solution.py:331
  7.1 2.2 %copy.9 = bf16[128,8,576]{2,1,0:T(8,128)(2,1)S(1)} copy(bf16[128,8,576]{0,2,1:T(8,128)(2,1)} %param.6) | data formatting | bytes 2359296 | tf_op args[0]
  9.3 3.2 %collective-permute-done.2.refs_3_ = bf16[1,48,576]{2,1,0:T(8,128)(2,1)S(1)} collective-permute-done((bf16[1,48,576]{2,1,0:T(8,128)(2,1)}, bf16[1,48,576]{2,1,0:T(8,128)(2,1)S(1)}, u32[]{:S(2)}, u32[]{:S(2)}) %collective-permute-start.2) | collective-permute-done | bytes 55328 | tf_op jit(solution)/shard_map/ppermute | solution.py:326
  12.7 2.9 %collective-permute-start.5 = (bf16[4,216,128]{2,1,0:T(8,128)(2,1)S(1)}, bf16[4,216,128]{2,1,0:T(8,128)(2,1)S(1)}, u32[]{:S(2)}, u32[]{:S(2)}) collective-permute-start(bf16[4,216,128]{2,1,0:T(8,128)(2,1)S(1)} %pack_nodes.1), channel_id=1, source_target_pairs={{0,6},{1,25},{2,4},{3,27},{4,2},{5,29},{6,0},{7,31},{8,14},{9,17},... | collective-permute-start | bytes 663560 | tf_op jit(solution)/shard_map/ppermute | solution.py:326
  15.6 0.2 collective-permute-start.4
  15.8 0.4 collective-permute-start.3
  16.3 3.3 %collective-permute-done.5 = bf16[4,216,128]{2,1,0:T(8,128)(2,1)S(1)} collective-permute-done((bf16[4,216,128]{2,1,0:T(8,128)(2,1)S(1)}, bf16[4,216,128]{2,1,0:T(8,128)(2,1)S(1)}, u32[]{:S(2)}, u32[]{:S(2)}) %collective-permute-start.5) | collective-permute-done | bytes 221216 | tf_op jit(solution)/shard_map/ppermute | solution.py:326
  19.6 2.3 %collective-permute-done.4 = bf16[4,216,128]{2,1,0:T(8,128)(2,1)S(1)} collective-permute-done((bf16[4,216,128]{2,1,0:T(8,128)(2,1)S(1)}, bf16[4,216,128]{2,1,0:T(8,128)(2,1)S(1)}, u32[]{:S(2)}, u32[]{:S(2)}) %collective-permute-start.4) | collective-permute-done | bytes 221216 | tf_op jit(solution)/shard_map/ppermute | solution.py:326
  21.9 0.2 collective-permute-done.3
  22.6 0.2 copy.10.own_ref
  22.8 1.4 %collective-permute-done.6.refs_1_ = bf16[6,216,128]{2,1,0:T(8,128)(2,1)S(1)} collective-permute-done((bf16[6,216,128]{2,1,0:T(8,128)(2,1)S(1)}, bf16[6,216,128]{2,1,0:T(8,128)(2,1)S(1)}, u32[]{:S(2)}, u32[]{:S(2)}) %collective-permute-start.6) | collective-permute-done | bytes 331808 | tf_op jit(solution)/shard_map/ppermute | solution.py:329
  24.1 2.3 %attend.1 = (bf16[6,216,128]{2,1,0:T(8,128)(2,1)S(1)}, bf16[2,352,512]{2,1,0:T(8,128)(2,1)S(1)}, bf16[2,352,512]{2,1,0:T(8,128)(2,1)S(1)}, bf16[2,352,576]{2,1,0:T(8,128)(2,1)S(1)}) custom-call(f32[2,1,512]{2,1,0:T(1,128)S(1)} %compare_convert_fusion.live_ref, bf16[128,576]{1,0:T(8,128)(2,1)S(1)} %copy.10.own_ref, bf16[1024,576]{1,0:T(8,128)(2,1)S(1)} %bitcast.3, ...), custom_call_target="tpu_custom_call" | custom-call | flops 1245708288 | bytes 8388608 | tf_op jit(solution)/shard_map/attend/pallas_call | solution.py:159
  26.4 0.2 collective-permute-start.7
  26.6 0.8 %own_terms.1 = (f32[6,216,128]{2,1,0:T(8,128)S(1)}, bf16[128,576]{1,0:T(8,128)(2,1)S(1)}) custom-call(bf16[1024,576]{1,0:T(8,128)(2,1)S(1)} %bitcast.4, bf16[1024,512]{1,0:T(8,128)(2,1)S(1)} %bitcast.6, bf16[2,352,512]{2,1,0:T(8,128)(2,1)S(1)} %get-tuple-element.38.dscores_ref, bf16[2,352,512]{2,1,0:T(8,128)(2,1)S(1)} %get-tuple-element.51.probs_ref), custom_call_target="tpu_custom_call" | custom-call | flops 490733568 | bytes 4194304 | tf_op jit(solution)/shard_map/own_terms/pallas_call | solution.py:193
  27.4 0.7 %collective-permute-done.7.refs_1_ = bf16[6,216,128]{2,1,0:T(8,128)(2,1)S(1)} collective-permute-done((bf16[6,216,128]{2,1,0:T(8,128)(2,1)S(1)}, bf16[6,216,128]{2,1,0:T(8,128)(2,1)S(1)}, u32[]{:S(2)}, u32[]{:S(2)}) %collective-permute-start.7) | collective-permute-done | bytes 331808 | tf_op jit(solution)/shard_map/ppermute | solution.py:329
  28.1 0.6 %spread_terms.1 = (bf16[4,216,128]{2,1,0:T(8,128)(2,1)S(1)}, bf16[4,216,128]{2,1,0:T(8,128)(2,1)S(1)}, bf16[4,216,128]{2,1,0:T(8,128)(2,1)S(1)}, bf16[4,216,128]{2,1,0:T(8,128)(2,1)S(1)}) custom-call(s32[1,6]{1,0:T(1,128)S(1)} %broadcast_select_fusion.where_ref, f32[6,216,128]{2,1,0:T(8,128)S(1)} %get-tuple-element.40.refs_0_, ...), custom_call_target="tpu_custom_call" | custom-call | tf_op jit(solution)/shard_map/spread_terms/pallas_call | solution.py:256
  28.7 1.9 %collective-permute-start.8 = (bf16[4,216,128]{2,1,0:T(8,128)(2,1)S(1)}, bf16[4,216,128]{2,1,0:T(8,128)(2,1)S(1)}, u32[]{:S(2)}, u32[]{:S(2)}) collective-permute-start(bf16[4,216,128]{2,1,0:T(8,128)(2,1)S(1)} %get-tuple-element.48), channel_id=1, source_target_pairs={{0,6},{1,25},{2,4},{3,27},{4,2},{5,29},{6,0},{7,31},{8,14},{9,17},... | collective-permute-start | bytes 663560 | tf_op jit(solution)/shard_map/ppermute | solution.py:326
  30.5 1.4 %collective-permute-start.9 = (bf16[4,216,128]{2,1,0:T(8,128)(2,1)S(1)}, bf16[4,216,128]{2,1,0:T(8,128)(2,1)S(1)}, u32[]{:S(2)}, u32[]{:S(2)}) collective-permute-start(bf16[4,216,128]{2,1,0:T(8,128)(2,1)S(1)} %get-tuple-element.49), channel_id=1, source_target_pairs={{0,4},{1,17},{2,6},{3,19},{4,0},{5,21},{6,2},{7,23},{8,12},{9,25},... | collective-permute-start | bytes 663560 | tf_op jit(solution)/shard_map/ppermute | solution.py:326
  31.9 0.3 collective-permute-start.10
  32.2 0.2 collective-permute-start.14
  32.4 1.7 %attend_outputs.1 = bf16[1024,512]{1,0:T(8,128)(2,1)} custom-call(bf16[2,352,512]{2,1,0:T(8,128)(2,1)S(1)} %get-tuple-element.51.probs_ref, bf16[2,352,576]{2,1,0:T(8,128)(2,1)S(1)} %get-tuple-element.52.keys_ref), custom_call_target="tpu_custom_call" | custom-call | flops 369098752 | bytes 4194304 | tf_op jit(solution)/shard_map/attend_outputs/pallas_call | solution.py:213
  34.1 1.5 %collective-permute-done.8.refs_1_ = bf16[4,216,128]{2,1,0:T(8,128)(2,1)S(1)} collective-permute-done((bf16[4,216,128]{2,1,0:T(8,128)(2,1)S(1)}, bf16[4,216,128]{2,1,0:T(8,128)(2,1)S(1)}, u32[]{:S(2)}, u32[]{:S(2)}) %collective-permute-start.8) | collective-permute-done | bytes 221216 | tf_op jit(solution)/shard_map/ppermute | solution.py:326
  35.7 2.3 %collective-permute-done.9.refs_2_ = bf16[4,216,128]{2,1,0:T(8,128)(2,1)S(1)} collective-permute-done((bf16[4,216,128]{2,1,0:T(8,128)(2,1)S(1)}, bf16[4,216,128]{2,1,0:T(8,128)(2,1)S(1)}, u32[]{:S(2)}, u32[]{:S(2)}) %collective-permute-start.9) | collective-permute-done | bytes 221216 | tf_op jit(solution)/shard_map/ppermute | solution.py:326
  38.1 1.8 %collective-permute-start.12 = (bf16[1,216,128]{2,1,0:T(8,128)(2,1)S(1)}, bf16[1,216,128]{2,1,0:T(8,128)(2,1)S(1)}, u32[]{:S(2)}, u32[]{:S(2)}) collective-permute-start(bf16[1,216,128]{2,1,0:T(8,128)(2,1)S(1)} %get-tuple-element.60), channel_id=1, source_target_pairs={{0,24},{1,7},{2,26},{3,5},{4,28},{5,3},{6,30},{7,1},{8,16},{9,15},... | collective-permute-start | bytes 165896 | tf_op jit(solution)/shard_map/ppermute | solution.py:326
  40.0 1.7 %collective-permute-start.13 = (bf16[1,216,128]{2,1,0:T(8,128)(2,1)S(1)}, bf16[1,216,128]{2,1,0:T(8,128)(2,1)S(1)}, u32[]{:S(2)}, u32[]{:S(2)}) collective-permute-start(bf16[1,216,128]{2,1,0:T(8,128)(2,1)S(1)} %get-tuple-element.61), channel_id=1, source_target_pairs={{0,8},{1,3},{2,10},{3,1},{4,12},{5,7},{6,14},{7,5},{8,0},{9,11},{1... | collective-permute-start | bytes 165896 | tf_op jit(solution)/shard_map/ppermute | solution.py:326
  41.7 0.8 %copy.11 = bf16[128,576]{0,1:T(8,128)(2,1)} copy(bf16[128,576]{1,0:T(8,128)(2,1)S(1)} %add.61) | data formatting | bytes 294912
  42.5 0.7 %collective-permute-done.11.refs_0_ = bf16[1,216,128]{2,1,0:T(8,128)(2,1)S(1)} collective-permute-done((bf16[1,216,128]{2,1,0:T(8,128)(2,1)S(1)}, bf16[1,216,128]{2,1,0:T(8,128)(2,1)S(1)}, u32[]{:S(2)}, u32[]{:S(2)}) %collective-permute-start.11) | collective-permute-done | bytes 55328 | tf_op jit(solution)/shard_map/ppermute | solution.py:326
  43.2 1.1 %collective-permute-done.12.refs_1_ = bf16[1,216,128]{2,1,0:T(8,128)(2,1)S(1)} collective-permute-done((bf16[1,216,128]{2,1,0:T(8,128)(2,1)S(1)}, bf16[1,216,128]{2,1,0:T(8,128)(2,1)S(1)}, u32[]{:S(2)}, u32[]{:S(2)}) %collective-permute-start.12) | collective-permute-done | bytes 55328 | tf_op jit(solution)/shard_map/ppermute | solution.py:326
  44.3 0.4 collective-permute-done.13.refs_2_
  44.7 0.7 %finish_nodes.1 = bf16[1,48,576]{2,1,0:T(8,128)(2,1)} custom-call(f32[1,216,128]{2,1,0:T(8,128)S(1)} %get-tuple-element.58.keep_ref, bf16[1,216,128]{2,1,0:T(8,128)(2,1)S(1)} %collective-permute-done.11.refs_0_, bf16[1,216,128]{2,1,0:T(8,128)(2,1)S(1)} %collective-permute-done.12.refs_1_, bf16[1,216,128]{2,1,0:T(8,128)(2,1)S(1)} %collective-permute-done.13.refs_2_), custom_call_target="tpu_custom_call" | custom-call | tf_op jit(solution)/shard_map/finish_nodes/pallas_call | solution.py:301
  (24 shorter events, 0.9 us)
Async XLA Ops:
  0.6 12.0 %copy-start.1 = (bf16[1,48,576]{2,1,0:T(8,128)(2,1)S(1)}, bf16[1,48,576]{2,1,0:T(8,128)(2,1)}, u32[]{:S(2)}) copy-start(bf16[1,48,576]{2,1,0:T(8,128)(2,1)} %refs_0_.1) | copy-start | bytes 165892
  0.6 8.7 %collective-permute-start.1 = (bf16[1,48,576]{2,1,0:T(8,128)(2,1)}, bf16[1,48,576]{2,1,0:T(8,128)(2,1)S(1)}, u32[]{:S(2)}, u32[]{:S(2)}) collective-permute-start(bf16[1,48,576]{2,1,0:T(8,128)(2,1)} %refs_0_.1), channel_id=1, source_target_pairs={{0,16},{1,5},{2,18},{3,7},{4,20},{5,1},{6,22},{7,3},{8,24},{9,13},... | collective-permute-start | bytes 165896 | tf_op jit(solution)/shard_map/ppermute | solution.py:326
  4.8 4.6 %collective-permute-start = (bf16[1,48,576]{2,1,0:T(8,128)(2,1)}, bf16[1,48,576]{2,1,0:T(8,128)(2,1)S(1)}, u32[]{:S(2)}, u32[]{:S(2)}) collective-permute-start(bf16[1,48,576]{2,1,0:T(8,128)(2,1)} %refs_0_.1), channel_id=1, source_target_pairs={{0,8},{1,3},{2,10},{3,1},{4,12},{5,7},{6,14},{7,5},{8,0},{9,11},{1... | collective-permute-start | bytes 165896 | tf_op jit(solution)/shard_map/ppermute | solution.py:326
  6.3 6.2 %collective-permute-start.2 = (bf16[1,48,576]{2,1,0:T(8,128)(2,1)}, bf16[1,48,576]{2,1,0:T(8,128)(2,1)S(1)}, u32[]{:S(2)}, u32[]{:S(2)}) collective-permute-start(bf16[1,48,576]{2,1,0:T(8,128)(2,1)} %refs_0_.1), channel_id=1, source_target_pairs={{0,24},{1,7},{2,26},{3,5},{4,28},{5,3},{6,30},{7,1},{8,16},{9,15},... | collective-permute-start | bytes 165896 | tf_op jit(solution)/shard_map/ppermute | solution.py:326
  12.7 6.9 %collective-permute-start.5 = (bf16[4,216,128]{2,1,0:T(8,128)(2,1)S(1)}, bf16[4,216,128]{2,1,0:T(8,128)(2,1)S(1)}, u32[]{:S(2)}, u32[]{:S(2)}) collective-permute-start(bf16[4,216,128]{2,1,0:T(8,128)(2,1)S(1)} %pack_nodes.1), channel_id=1, source_target_pairs={{0,6},{1,25},{2,4},{3,27},{4,2},{5,29},{6,0},{7,31},{8,14},{9,17},... | collective-permute-start | bytes 663560 | tf_op jit(solution)/shard_map/ppermute | solution.py:326
  15.6 6.4 %collective-permute-start.4 = (bf16[4,216,128]{2,1,0:T(8,128)(2,1)S(1)}, bf16[4,216,128]{2,1,0:T(8,128)(2,1)S(1)}, u32[]{:S(2)}, u32[]{:S(2)}) collective-permute-start(bf16[4,216,128]{2,1,0:T(8,128)(2,1)S(1)} %pack_nodes.1), channel_id=1, source_target_pairs={{0,4},{1,17},{2,6},{3,19},{4,0},{5,21},{6,2},{7,23},{8,12},{9,25},... | collective-permute-start | bytes 663560 | tf_op jit(solution)/shard_map/ppermute | solution.py:326
  15.8 6.4 %collective-permute-start.3 = (bf16[4,216,128]{2,1,0:T(8,128)(2,1)S(1)}, bf16[4,216,128]{2,1,0:T(8,128)(2,1)S(1)}, u32[]{:S(2)}, u32[]{:S(2)}) collective-permute-start(bf16[4,216,128]{2,1,0:T(8,128)(2,1)S(1)} %pack_nodes.1), channel_id=1, source_target_pairs={{0,2},{1,9},{2,0},{3,11},{4,6},{5,13},{6,4},{7,15},{8,10},{9,1},{1... | collective-permute-start | bytes 663560 | tf_op jit(solution)/shard_map/ppermute | solution.py:326
  16.2 6.3 %copy-start.3 = (s32[2]{0:T(128)S(1)}, s32[2]{0:T(128)}, u32[]{:S(2)}) copy-start(s32[2]{0:T(128)} %param.11) | copy-start | bytes 28
  16.3 6.3 %copy-start.2 = (bf16[128,576]{0,1:T(8,128)(2,1)S(1)}, bf16[128,576]{0,1:T(8,128)(2,1)}, u32[]{:S(2)}) copy-start(bf16[128,576]{0,1:T(8,128)(2,1)} %param.7) | copy-start | bytes 442372
  16.3 7.9 %copy-start = (bf16[128,8,512]{2,1,0:T(8,128)(2,1)S(1)}, bf16[128,8,512]{2,1,0:T(8,128)(2,1)}, u32[]{:S(2)}) copy-start(bf16[128,8,512]{2,1,0:T(8,128)(2,1)} %param.9) | copy-start | bytes 3145732
  22.4 1.7 %collective-permute-start.6 = (bf16[6,216,128]{2,1,0:T(8,128)(2,1)S(1)}, bf16[6,216,128]{2,1,0:T(8,128)(2,1)S(1)}, u32[]{:S(2)}, u32[]{:S(2)}) collective-permute-start(bf16[6,216,128]{2,1,0:T(8,128)(2,1)S(1)} %select_nodes.1.refs_0_), channel_id=1, source_target_pairs={{0,1},{1,0},{2,3},{3,2},{4,5},{5,4},{6,7},{7,6},{8,9},{9,8},{10,11... | collective-permute-start | bytes 995336 | tf_op jit(solution)/shard_map/ppermute | solution.py:329
  26.4 1.7 %collective-permute-start.7 = (bf16[6,216,128]{2,1,0:T(8,128)(2,1)S(1)}, bf16[6,216,128]{2,1,0:T(8,128)(2,1)S(1)}, u32[]{:S(2)}, u32[]{:S(2)}) collective-permute-start(bf16[6,216,128]{2,1,0:T(8,128)(2,1)S(1)} %get-tuple-element.41), channel_id=1, source_target_pairs={{0,1},{1,0},{2,3},{3,2},{4,5},{5,4},{6,7},{7,6},{8,9},{9,8},{10,11... | collective-permute-start | bytes 995336 | tf_op jit(solution)/shard_map/ppermute | solution.py:329
  28.7 7.0 %collective-permute-start.8 = (bf16[4,216,128]{2,1,0:T(8,128)(2,1)S(1)}, bf16[4,216,128]{2,1,0:T(8,128)(2,1)S(1)}, u32[]{:S(2)}, u32[]{:S(2)}) collective-permute-start(bf16[4,216,128]{2,1,0:T(8,128)(2,1)S(1)} %get-tuple-element.48), channel_id=1, source_target_pairs={{0,6},{1,25},{2,4},{3,27},{4,2},{5,29},{6,0},{7,31},{8,14},{9,17},... | collective-permute-start | bytes 663560 | tf_op jit(solution)/shard_map/ppermute | solution.py:326
  30.5 7.4 %collective-permute-start.9 = (bf16[4,216,128]{2,1,0:T(8,128)(2,1)S(1)}, bf16[4,216,128]{2,1,0:T(8,128)(2,1)S(1)}, u32[]{:S(2)}, u32[]{:S(2)}) collective-permute-start(bf16[4,216,128]{2,1,0:T(8,128)(2,1)S(1)} %get-tuple-element.49), channel_id=1, source_target_pairs={{0,4},{1,17},{2,6},{3,19},{4,0},{5,21},{6,2},{7,23},{8,12},{9,25},... | collective-permute-start | bytes 663560 | tf_op jit(solution)/shard_map/ppermute | solution.py:326
  31.9 6.0 %collective-permute-start.10 = (bf16[4,216,128]{2,1,0:T(8,128)(2,1)S(1)}, bf16[4,216,128]{2,1,0:T(8,128)(2,1)S(1)}, u32[]{:S(2)}, u32[]{:S(2)}) collective-permute-start(bf16[4,216,128]{2,1,0:T(8,128)(2,1)S(1)} %get-tuple-element.50), channel_id=1, source_target_pairs={{0,2},{1,9},{2,0},{3,11},{4,6},{5,13},{6,4},{7,15},{8,10},{9,1},{1... | collective-permute-start | bytes 663560 | tf_op jit(solution)/shard_map/ppermute | solution.py:326
  32.2 9.4 %collective-permute-start.14 = (bf16[128,576]{1,0:T(8,128)(2,1)S(1)}, bf16[128,576]{1,0:T(8,128)(2,1)S(1)}, u32[]{:S(2)}, u32[]{:S(2)}) collective-permute-start(bf16[128,576]{1,0:T(8,128)(2,1)S(1)} %get-tuple-element.62), channel_id=1, source_target_pairs={{0,1},{1,0},{2,3},{3,2},{4,5},{5,4},{6,7},{7,6},{8,9},{9,8},{10,11... | collective-permute-start | bytes 442376 | tf_op jit(solution)/shard_map/ppermute | solution.py:329
  38.1 5.1 %collective-permute-start.11 = (bf16[1,216,128]{2,1,0:T(8,128)(2,1)S(1)}, bf16[1,216,128]{2,1,0:T(8,128)(2,1)S(1)}, u32[]{:S(2)}, u32[]{:S(2)}) collective-permute-start(bf16[1,216,128]{2,1,0:T(8,128)(2,1)S(1)} %get-tuple-element.59), channel_id=1, source_target_pairs={{0,16},{1,5},{2,18},{3,7},{4,20},{5,1},{6,22},{7,3},{8,24},{9,13},... | collective-permute-start | bytes 165896 | tf_op jit(solution)/shard_map/ppermute | solution.py:326
  38.1 6.1 %collective-permute-start.12 = (bf16[1,216,128]{2,1,0:T(8,128)(2,1)S(1)}, bf16[1,216,128]{2,1,0:T(8,128)(2,1)S(1)}, u32[]{:S(2)}, u32[]{:S(2)}) collective-permute-start(bf16[1,216,128]{2,1,0:T(8,128)(2,1)S(1)} %get-tuple-element.60), channel_id=1, source_target_pairs={{0,24},{1,7},{2,26},{3,5},{4,28},{5,3},{6,30},{7,1},{8,16},{9,15},... | collective-permute-start | bytes 165896 | tf_op jit(solution)/shard_map/ppermute | solution.py:326
  40.0 4.7 %collective-permute-start.13 = (bf16[1,216,128]{2,1,0:T(8,128)(2,1)S(1)}, bf16[1,216,128]{2,1,0:T(8,128)(2,1)S(1)}, u32[]{:S(2)}, u32[]{:S(2)}) collective-permute-start(bf16[1,216,128]{2,1,0:T(8,128)(2,1)S(1)} %get-tuple-element.61), channel_id=1, source_target_pairs={{0,8},{1,3},{2,10},{3,1},{4,12},{5,7},{6,14},{7,5},{8,0},{9,11},{1... | collective-permute-start | bytes 165896 | tf_op jit(solution)/shard_map/ppermute | solution.py:326

commit v5 on v4

--- a/solution.py
+++ b/solution.py
@@ -101,45 +101,91 @@
             ref[first_slot + level, prow, plane] = value.astype(ref.dtype)
 
 
-def attend_kernel(parts, leaves, heads, slice_rows, live_ref, own_ref, query_ref, grad_ref, *refs):
-    part_refs, refs = refs[:parts], refs[parts:]
-    term_refs, refs = refs[: parts - 1], refs[parts - 1 :]
-    dscores_ref, probs_ref, keys_ref = refs
+def load_keys(ref, leaf, place, part_ref, slice_rows, width):
+    for level in range(LEVELS):
+        offset = (place * LEVELS + level) * slice_rows
+        for prow, plane, row, col in pieces(slice_rows, width):
+            rows = slice(offset + row.start, offset + row.stop)
+            ref[leaf, rows, col] = part_ref[leaf * LEVELS + level, prow, plane]
+
+
+def near_kernel(leaves, heads, slice_rows, part_ref, own_ref, query_ref, grad_ref, expo_ref, dprob_ref, top_ref, sum_ref, dot_ref, keys_ref):
     width = own_ref.shape[1]
     leaf_rows = own_ref.shape[0] // leaves
     lines = leaf_rows * heads
     level_rows = LEVELS * slice_rows
-    node_rows = parts * level_rows
-    sent_rows = node_rows - level_rows
-    order = list(range(1, parts)) + [0]
     for leaf in range(leaves):
-        for place, part in enumerate(order):
-            for level in range(LEVELS):
-                offset = place * level_rows + level * slice_rows
-                for prow, plane, row, col in pieces(slice_rows, width):
-                    rows = slice(offset + row.start, offset + row.stop)
-                    keys_ref[leaf, rows, col] = part_refs[part][leaf * LEVELS + level, prow, plane]
-        keys_ref[leaf, node_rows:, :] = own_ref[leaf * leaf_rows : (leaf + 1) * leaf_rows, :]
+        load_keys(keys_ref, leaf, 0, part_ref, slice_rows, width)
+        keys_ref[leaf, level_rows:, :] = own_ref[leaf * leaf_rows : (leaf + 1) * leaf_rows, :]
         query = query_ref[leaf * lines : (leaf + 1) * lines, :]
         grad = grad_ref[leaf * lines : (leaf + 1) * lines, :]
         scores = dot(keys_ref[leaf], query, NT) * score_scale
         row_of = lax.broadcasted_iota(jnp.int32, (leaf_rows, lines), 1) // heads
         own_key = lax.broadcasted_iota(jnp.int32, (leaf_rows, lines), 0)
-        own_scores = jnp.where(own_key <= row_of, scores[node_rows:], -jnp.inf)
-        scores = jnp.concatenate([scores[:node_rows], own_scores], axis=0)
+        own_scores = jnp.where(own_key <= row_of, scores[level_rows:], -jnp.inf)
+        scores = jnp.concatenate([scores[:level_rows], own_scores], axis=0)
         top = jnp.max(scores, axis=0, keepdims=True)
         expo = jnp.exp(scores - top)
-        scale = live_ref[leaf] / jnp.sum(expo, axis=0, keepdims=True)
+        dprobs = dot(keys_ref[leaf, :, :LAT], grad, NT)
+        expo_ref[leaf] = expo
+        dprob_ref[leaf] = dprobs
+        top_ref[leaf] = top
+        sum_ref[leaf] = jnp.sum(expo, axis=0, keepdims=True)
+        dot_ref[leaf] = jnp.sum(expo * dprobs, axis=0, keepdims=True)
+
+
+def near_scores(part, own, query, grad, leaves, heads, slice_rows):
+    rows, width = own.shape
+    lines = rows * heads // leaves
+    near_rows = LEVELS * slice_rows + rows // leaves
+    line = jax.ShapeDtypeStruct((leaves, 1, lines), jnp.float32)
+    outs = [
+        jax.ShapeDtypeStruct((leaves, near_rows, lines), jnp.float32),
+        jax.ShapeDtypeStruct((leaves, near_rows, lines), jnp.float32),
+        line,
+        line,
+        line,
+        jax.ShapeDtypeStruct((leaves, near_rows, width), jnp.bfloat16),
+    ]
+    return pl.pallas_call(
+        functools.partial(near_kernel, leaves, heads, slice_rows),
+        out_shape=outs,
+        in_specs=vmem(4),
+        out_specs=vmem(len(outs)),
+        compiler_params=pltpu.CompilerParams(vmem_limit_bytes=24 << 20),
+        cost_estimate=cost(2 * rows * heads * near_rows * 2 * width, 4 << 20),
+        name="near_scores",
+    )(part, own, query, grad)
+
+
+def attend_kernel(parts, leaves, slice_rows, live_ref, query_ref, grad_ref, top_ref, sum_ref, dot_ref, *refs):
+    part_refs, refs = refs[:parts], refs[parts:]
+    term_refs, refs = refs[:parts], refs[parts:]
+    near_scale_ref, delta_ref, probs_ref, keys_ref, dscores_ref = refs
+    width = query_ref.shape[1]
+    lines = query_ref.shape[0] // leaves
+    level_rows = LEVELS * slice_rows
+    for leaf in range(leaves):
+        query = query_ref[leaf * lines : (leaf + 1) * lines, :]
+        grad = grad_ref[leaf * lines : (leaf + 1) * lines, :]
+        for place in range(parts):
+            load_keys(keys_ref, leaf, place, part_refs[place], slice_rows, width)
+        scores = dot(keys_ref[leaf], query, NT) * score_scale
+        dprobs = dot(keys_ref[leaf, :, :LAT], grad, NT)
+        top = jnp.maximum(top_ref[leaf], jnp.max(scores, axis=0, keepdims=True))
+        shift = jnp.exp(top_ref[leaf] - top)
+        expo = jnp.exp(scores - top)
+        total = shift * sum_ref[leaf] + jnp.sum(expo, axis=0, keepdims=True)
+        scale = live_ref[leaf] / total
+        delta = (shift * dot_ref[leaf] + jnp.sum(expo * dprobs, axis=0, keepdims=True)) * scale
+        near_scale_ref[leaf] = shift * scale
+        delta_ref[leaf] = delta
         probs = expo * scale
-        probs_b = probs.astype(jnp.bfloat16)
-        probs_ref[leaf] = probs_b
-        dprobs = dot(keys_ref[leaf, :, :LAT], grad, NT)
-        delta = jnp.sum(probs_b.astype(jnp.float32) * dprobs, axis=0, keepdims=True)
-        dscores_ref[leaf] = (score_scale * probs * (dprobs - delta)).astype(jnp.bfloat16)
-        if parts > 1:
-            head_part, tail_part = key_grads(dscores_ref[leaf, :sent_rows, :], probs_ref[leaf, :sent_rows, :], query, grad)
-            for place in range(parts - 1):
-                store_terms(term_refs[place], leaf * LEVELS, slice_rows, width, place * level_rows, head_part, tail_part)
+        probs_ref[leaf] = probs.astype(jnp.bfloat16)
+        dscores_ref[...] = (score_scale * probs * (dprobs - delta)).astype(jnp.bfloat16)
+        head_part, tail_part = key_grads(dscores_ref[...], probs_ref[leaf], query, grad)
+        for place in range(parts):
+            store_terms(term_refs[place], leaf * LEVELS, slice_rows, width, place * level_rows, head_part, tail_part)
 
 
 def key_grads(dscores, probs_b, query, grad):
@@ -147,85 +193,96 @@
     return head_part, dot(dscores, query[:, LAT:], NN)
 
 
-def attend(live, own, query, grad, parts, leaves, heads, slice_rows):
-    rows, width = own.shape
-    lines = rows * heads // leaves
-    total_keys = LEVELS * len(parts) * slice_rows + rows // leaves
-    outs = [jax.ShapeDtypeStruct(parts[0].shape, jnp.bfloat16)] * (len(parts) - 1) + [
-        jax.ShapeDtypeStruct((leaves, total_keys, lines), jnp.bfloat16),
-        jax.ShapeDtypeStruct((leaves, total_keys, lines), jnp.bfloat16),
-        jax.ShapeDtypeStruct((leaves, total_keys, width), jnp.bfloat16),
+def attend(live, query, grad, stats, parts, leaves, slice_rows):
+    width = query.shape[1]
+    lines = live.shape[2]
+    sent_rows = LEVELS * len(parts) * slice_rows
+    line = jax.ShapeDtypeStruct((leaves, 1, lines), jnp.float32)
+    outs = [jax.ShapeDtypeStruct(part.shape, jnp.bfloat16) for part in parts] + [
+        line,
+        line,
+        jax.ShapeDtypeStruct((leaves, sent_rows, lines), jnp.bfloat16),
+        jax.ShapeDtypeStruct((leaves, sent_rows, width), jnp.bfloat16),
     ]
     return pl.pallas_call(
-        functools.partial(attend_kernel, len(parts), leaves, heads, slice_rows),
+        functools.partial(attend_kernel, len(parts), leaves, slice_rows),
         out_shape=outs,
-        in_specs=vmem(4 + len(parts)),
+        in_specs=vmem(6 + len(parts)),
         out_specs=vmem(len(outs)),
+        scratch_shapes=[pltpu.VMEM((sent_rows, lines), jnp.bfloat16)],
         compiler_params=pltpu.CompilerParams(vmem_limit_bytes=40 << 20),
-        cost_estimate=cost(2 * rows * heads * total_keys * 3 * width, 8 << 20),
+        cost_estimate=cost(2 * leaves * lines * sent_rows * 4 * width, 8 << 20),
         name="attend",
-    )(live, own, query, grad, *parts)
-
-
-def own_kernel(leaves, slice_rows, level_rows, query_ref, grad_ref, dscores_ref, probs_ref, term_ref, own_grad_ref):
+    )(live, query, grad, *stats, *parts)
+
+
+def own_kernel(leaves, slice_rows, query_ref, grad_ref, expo_ref, dprob_ref, scale_ref, delta_ref, term_ref, own_grad_ref, probs_ref, *refs):
+    dscores_ref = refs[-1]
+    for ref in refs[:-1]:
+        ref[...] = jnp.zeros_like(ref)
     lines = query_ref.shape[0] // leaves
     width = query_ref.shape[1]
     leaf_rows = own_grad_ref.shape[0] // leaves
-    first = dscores_ref.shape[1] - leaf_rows - level_rows
+    level_rows = LEVELS * slice_rows
     for leaf in range(leaves):
         query = query_ref[leaf * lines : (leaf + 1) * lines, :]
         grad = grad_ref[leaf * lines : (leaf + 1) * lines, :]
-        head_part, tail_part = key_grads(dscores_ref[leaf, first:, :], probs_ref[leaf, first:, :], query, grad)
+        probs = expo_ref[leaf] * scale_ref[leaf]
+        probs_ref[leaf] = probs.astype(jnp.bfloat16)
+        dscores_ref[...] = (score_scale * probs * (dprob_ref[leaf] - delta_ref[leaf])).astype(jnp.bfloat16)
+        head_part, tail_part = key_grads(dscores_ref[...], probs_ref[leaf], query, grad)
         store_terms(term_ref, leaf * LEVELS, slice_rows, width, 0, head_part, tail_part)
         rows = slice(leaf * leaf_rows, (leaf + 1) * leaf_rows)
         own_grad_ref[rows, :LAT] = head_part[level_rows:].astype(jnp.bfloat16)
         own_grad_ref[rows, LAT:] = tail_part[level_rows:].astype(jnp.bfloat16)
 
 
-def own_terms(query, grad, dscores, probs, block, slice_rows, rows):
-    leaves, total_keys, lines = dscores.shape
+def own_terms(query, grad, expo, dprobs, scale, delta, block, slice_rows, rows, side):
+    leaves, near_rows, lines = expo.shape
     width = query.shape[1]
-    level_rows = LEVELS * slice_rows
     outs = [
         jax.ShapeDtypeStruct(block, jnp.float32),
         jax.ShapeDtypeStruct((rows, width), jnp.bfloat16),
-    ]
-    return pl.pallas_call(
-        functools.partial(own_kernel, leaves, slice_rows, level_rows),
+        jax.ShapeDtypeStruct(expo.shape, jnp.bfloat16),
+    ] + [jax.ShapeDtypeStruct((side,) + block[1:], jnp.bfloat16)] * side
+    return pl.pallas_call(
+        functools.partial(own_kernel, leaves, slice_rows),
         out_shape=outs,
-        in_specs=vmem(4),
-        out_specs=vmem(2),
+        in_specs=vmem(6),
+        out_specs=vmem(len(outs)),
+        scratch_shapes=[pltpu.VMEM((near_rows, lines), jnp.bfloat16)],
         compiler_params=pltpu.CompilerParams(vmem_limit_bytes=24 << 20),
-        cost_estimate=cost(2 * leaves * lines * (level_rows + rows // leaves) * 2 * width, 4 << 20),
+        cost_estimate=cost(2 * leaves * lines * near_rows * 2 * width, 4 << 20),
         name="own_terms",
-    )(query, grad, dscores, probs)
-
-
-def outputs_kernel(leaves, probs_ref, keys_ref, out_ref):
+    )(query, grad, expo, dprobs, scale, delta)
+
+
+def outputs_kernel(leaves, probs_ref, keys_ref, near_probs_ref, near_keys_ref, out_ref):
     lines = probs_ref.shape[2]
     for leaf in range(leaves):
         out = dot(probs_ref[leaf], keys_ref[leaf, :, :LAT], TN)
+        out = out + dot(near_probs_ref[leaf], near_keys_ref[leaf, :, :LAT], TN)
         out_ref[leaf * lines : (leaf + 1) * lines, :] = out.astype(jnp.bfloat16)
 
 
-def outputs(probs, keys):
-    leaves, total_keys, lines = probs.shape
+def outputs(probs, keys, near_probs, near_keys):
+    leaves, sent_rows, lines = probs.shape
+    total_keys = sent_rows + near_probs.shape[1]
     return pl.pallas_call(
         functools.partial(outputs_kernel, leaves),
         out_shape=jax.ShapeDtypeStruct((leaves * lines, LAT), jnp.bfloat16),
-        in_specs=vmem(2),
+        in_specs=vmem(4),
         out_specs=vmem(1)[0],
         compiler_params=pltpu.CompilerParams(vmem_limit_bytes=24 << 20),
         cost_estimate=cost(2 * leaves * total_keys * lines * LAT, 4 << 20),
         name="attend_outputs",
-    )(probs, keys)
+    )(probs, keys, near_probs, near_keys)
 
 
 def spread_kernel(shares, leaves, where_ref, *refs):
-    share_refs, out_refs = refs[:shares], refs[shares:]
+    share_refs, refs = refs[:shares], refs[shares:]
+    out_refs = refs[len(refs) // 2 :]
     inner = out_refs[0].shape[0]
-    for ref in out_refs:
-        ref[...] = jnp.zeros_like(ref)
     for level in range(LEVELS):
         slots = [leaf * LEVELS + level for leaf in range(leaves)]
         places = {slot: where_ref[0, slot] for slot in slots}
@@ -250,17 +307,17 @@
                     ref[place % inner] = total
 
 
-def spread(where, shares, outer, inner):
-    block = shares[0].shape[1:]
-    outs = [jax.ShapeDtypeStruct((inner,) + block, jnp.bfloat16)] * outer
+def spread(where, shares, zeros):
+    first = 1 + len(shares)
     return pl.pallas_call(
         functools.partial(spread_kernel, len(shares), shares[0].shape[0] // LEVELS),
-        out_shape=outs,
-        in_specs=vmem(1 + len(shares)),
-        out_specs=vmem(len(outs)),
+        out_shape=[jax.ShapeDtypeStruct(zero.shape, zero.dtype) for zero in zeros],
+        in_specs=vmem(first + len(zeros)),
+        out_specs=vmem(len(zeros)),
+        input_output_aliases={first + i: i for i in range(len(zeros))},
         compiler_params=pltpu.CompilerParams(vmem_limit_bytes=16 << 20),
         name="spread_terms",
-    )(where, *shares)
+    )(where, *shares, *zeros)
 
 
 def merge_kernel(count, *refs):
@@ -343,17 +400,18 @@
     got = {d: step(inner, 1, d) for d in order}
     table = jnp.concatenate([inner] + [got[d] for d in range(1, side)], axis=0)
     mine = select(where, table)
-    parts = [mine] + [swap(mine, d) for d in range(1, head_size)]
+    parts = [swap(mine, d) for d in range(1, head_size)]
     grad = grad_out.reshape(rows * heads, LAT)
     slice_rows = node_latent.shape[1]
 
-    *terms, dscores, probs, keys = attend(live, own, query, grad, parts, leaves, heads, slice_rows)
+    expo, dprobs, *stats, near_keys = near_scores(mine, own, query, grad, leaves, heads, slice_rows)
+    *terms, scale, delta, probs, keys = attend(live, query, grad, stats, parts, leaves, slice_rows)
     shares = [swap(terms[d - 1], d) for d in range(1, head_size)]
-    mine, own_grad = own_terms(query, grad, dscores, probs, mine.shape, slice_rows, rows)
-    sends = spread(where, [mine] + shares, side, side)
+    mine, own_grad, near_probs, *zeros = own_terms(query, grad, expo, dprobs, scale, delta, mine.shape, slice_rows, rows, side)
+    sends = spread(where, [mine] + shares, zeros)
     sends, probs, own_grad = lax.optimization_barrier((sends, probs, own_grad))
     got = {d: step(sends[d], 1, d) for d in order}
-    attention = outputs(probs, keys).reshape(rows, heads, LAT)
+    attention = outputs(probs, keys, near_probs, near_keys).reshape(rows, heads, LAT)
     got, attention = lax.optimization_barrier(([sends[0]] + [got[d] for d in order], attention))
     keep, *sends = merge(got)
     got = {d: step(sends[d - 1], 0, d) for d in order}

time: 45.9 us -> 45.2 us (0.985)
  waiting for transfers between devices: 17.3 us -> 16.2 us
    ppermute x3, waiting for transfers between devices: 2.09 us -> 1 us  [swap(): lax.ppermute(value, 'head', [(i, i ^ distance) for i in range(head_size)])]
    pallas_call x2 -> x3, Pallas kernels: 3.07 us -> 3.43 us  [the longest x1 1.6 us: attend(): pl.pallas_call(functools.partial(attend_kernel, len(parts), leaves, slice...]
  transfers between devices with their start and end apart: 15 -> 15, of which waited for: 11 -> 11; matrix products, arithmetic and copies ran while one was open for 9% -> 9% of each run, Pallas kernels for 6% -> 8%
where the time goes in v5:
time: 45.2 us; the launch traced here: 44.7 us
  starting transfers between devices  16.8 us (37%)
  waiting for transfers between devices  16.2 us (36%)
  Pallas kernels  6.7 us (15%)
  local copies, waits for them, and re-layouts  3.27 us (7%)
  other arithmetic  0.93 us (2%)
  between operations  0.78 us (2%)
    ppermute x12, starting transfers between devices, step(): return lax.ppermute(value, axes, pairs)  16.3 us
    ppermute x12, waiting for transfers between devices, step(): return lax.ppermute(value, axes, pairs)  15.2 us
    unnamed x10, local copies, waits for them, and re-layouts  3.02 us
    pallas_call x1, Pallas kernels, outputs(): pl.pallas_call(functools.partial(outputs_kernel, leaves), out_shape=jax.S...  1.72 us
    pallas_call x1, Pallas kernels, attend(): pl.pallas_call(functools.partial(attend_kernel, len(parts), leaves, slice...  1.6 us
    ppermute x3, waiting for transfers between devices, swap(): lax.ppermute(value, 'head', [(i, i ^ distance) for i in range(head_size)])  1 us
    pallas_call x1, Pallas kernels, near_scores(): pl.pallas_call(functools.partial(near_kernel, leaves, heads, slice_rows),...  0.99 us
  transfers between devices with their start and end apart: 15, of which 11 were waited for; matrix products, arithmetic and copies ran while one was open for 9% of the time, Pallas kernels for 8%

profile of v5, /device:TPU:0, one launch (start us, length us, event | category | flops | bytes accessed | tf_op | source)
XLA Modules:
  0.0 44.7 jit_solution(7967808864216500061)
XLA Ops:
  0.6 4.1 %collective-permute-start.1 = (bf16[1,48,576]{2,1,0:T(8,128)(2,1)}, bf16[1,48,576]{2,1,0:T(8,128)(2,1)S(1)}, u32[]{:S(2)}, u32[]{:S(2)}) collective-permute-start(bf16[1,48,576]{2,1,0:T(8,128)(2,1)} %refs_0_.1), channel_id=1, source_target_pairs={{0,16},{1,5},{2,18},{3,7},{4,20},{5,1},{6,22},{7,3},{8,24},{9,13},... | collective-permute-start | bytes 165896 | tf_op jit(solution)/shard_map/ppermute | solution.py:383
  4.8 1.6 %collective-permute-start = (bf16[1,48,576]{2,1,0:T(8,128)(2,1)}, bf16[1,48,576]{2,1,0:T(8,128)(2,1)S(1)}, u32[]{:S(2)}, u32[]{:S(2)}) collective-permute-start(bf16[1,48,576]{2,1,0:T(8,128)(2,1)} %refs_0_.1), channel_id=1, source_target_pairs={{0,8},{1,3},{2,10},{3,1},{4,12},{5,7},{6,14},{7,5},{8,0},{9,11},{1... | collective-permute-start | bytes 165896 | tf_op jit(solution)/shard_map/ppermute | solution.py:383
  6.4 0.7 %broadcast_xor_fusion = s32[2,3]{1,0:T(2,128)S(1)} fusion(s32[2,3]{1,0:T(2,128)} %param.10, s32[]{:T(128)S(6)} %axis_index.25), kind=kLoop, calls=%fused_computation.15 | loop fusion | flops 6 | bytes 52 | tf_op jit(solution)/shard_map/xor | solution.py:388
  7.1 2.2 %copy.13 = bf16[128,8,576]{2,1,0:T(8,128)(2,1)S(1)} copy(bf16[128,8,576]{0,2,1:T(8,128)(2,1)} %param.6) | data formatting | bytes 2359296 | tf_op args[0]
  9.3 3.2 %collective-permute-done.2.refs_3_ = bf16[1,48,576]{2,1,0:T(8,128)(2,1)S(1)} collective-permute-done((bf16[1,48,576]{2,1,0:T(8,128)(2,1)}, bf16[1,48,576]{2,1,0:T(8,128)(2,1)S(1)}, u32[]{:S(2)}, u32[]{:S(2)}) %collective-permute-start.2) | collective-permute-done | bytes 55328 | tf_op jit(solution)/shard_map/ppermute | solution.py:383
  12.7 2.9 %collective-permute-start.5 = (bf16[4,216,128]{2,1,0:T(8,128)(2,1)S(1)}, bf16[4,216,128]{2,1,0:T(8,128)(2,1)S(1)}, u32[]{:S(2)}, u32[]{:S(2)}) collective-permute-start(bf16[4,216,128]{2,1,0:T(8,128)(2,1)S(1)} %pack_nodes.1), channel_id=1, source_target_pairs={{0,6},{1,25},{2,4},{3,27},{4,2},{5,29},{6,0},{7,31},{8,14},{9,17},... | collective-permute-start | bytes 663560 | tf_op jit(solution)/shard_map/ppermute | solution.py:383
  15.6 0.2 collective-permute-start.4
  15.8 0.4 %collective-permute-start.3 = (bf16[4,216,128]{2,1,0:T(8,128)(2,1)S(1)}, bf16[4,216,128]{2,1,0:T(8,128)(2,1)S(1)}, u32[]{:S(2)}, u32[]{:S(2)}) collective-permute-start(bf16[4,216,128]{2,1,0:T(8,128)(2,1)S(1)} %pack_nodes.1), channel_id=1, source_target_pairs={{0,2},{1,9},{2,0},{3,11},{4,6},{5,13},{6,4},{7,15},{8,10},{9,1},{1... | collective-permute-start | bytes 663560 | tf_op jit(solution)/shard_map/ppermute | solution.py:383
  16.3 3.3 %collective-permute-done.5 = bf16[4,216,128]{2,1,0:T(8,128)(2,1)S(1)} collective-permute-done((bf16[4,216,128]{2,1,0:T(8,128)(2,1)S(1)}, bf16[4,216,128]{2,1,0:T(8,128)(2,1)S(1)}, u32[]{:S(2)}, u32[]{:S(2)}) %collective-permute-start.5) | collective-permute-done | bytes 221216 | tf_op jit(solution)/shard_map/ppermute | solution.py:383
  19.6 2.3 %collective-permute-done.4 = bf16[4,216,128]{2,1,0:T(8,128)(2,1)S(1)} collective-permute-done((bf16[4,216,128]{2,1,0:T(8,128)(2,1)S(1)}, bf16[4,216,128]{2,1,0:T(8,128)(2,1)S(1)}, u32[]{:S(2)}, u32[]{:S(2)}) %collective-permute-start.4) | collective-permute-done | bytes 221216 | tf_op jit(solution)/shard_map/ppermute | solution.py:383
  21.9 0.2 collective-permute-done.3
  22.8 1.0 %near_scores.1 = (f32[2,208,512]{2,1,0:T(8,128)S(1)}, f32[2,208,512]{2,1,0:T(8,128)S(1)}, f32[2,1,512]{2,1,0:T(1,128)S(1)}, f32[2,1,512]{2,1,0:T(1,128)S(1)}, f3...) custom-call(bf16[6,216,128]{2,1,0:T(8,128)(2,1)S(1)} %select_nodes.1.part_ref, ...), custom_call_target="tpu_custom_call" | custom-call | flops 490733568 | bytes 4194304 | tf_op jit(solution)/shard_map/near_scores/pallas_call | solution.py:150
  23.8 0.4 collective-permute-done.6.refs_0_
  24.1 1.6 %attend.1 = (bf16[6,216,128]{2,1,0:T(8,128)(2,1)S(1)}, f32[2,1,512]{2,1,0:T(1,128)S(1)}, f32[2,1,512]{2,1,0:T(1,128)S(1)}, bf16[2,144,512]{2,1,0:T(8,128)(2,1)S(1)}, bf16[2,144,576]{2,1,0:T(8,128)(2,1)S(1)}) custom-call(f32[2,1,512]{2,1,0:T(1,128)S(1)} %compare_convert_fusion.live_ref, bf16[1024,576]{1,0:T(8,128)(2,1)S(1)} %bitcast.4, ...), custom_call_target="tpu_custom_call" | custom-call | flops 679477248 | bytes 8388608 | tf_op jit(solution)/shard_map/attend/pallas_call | solution.py:207
  25.7 0.2 collective-permute-start.7
  25.9 0.8 %own_terms.1 = (f32[6,216,128]{2,1,0:T(8,128)S(1)}, bf16[128,576]{1,0:T(8,128)(2,1)S(1)}, bf16[2,208,512]{2,1,0:T(8,128)(2,1)S(1)}, bf16[4,216,128]{2,1,0:T(8,12...) custom-call(bf16[1024,576]{1,0:T(8,128)(2,1)S(1)} %bitcast.5, ...), custom_call_target="tpu_custom_call" | custom-call | flops 490733568 | bytes 4194304 | tf_op jit(solution)/shard_map/own_terms/pallas_call | solution.py:248
  26.8 0.6 %collective-permute-done.7.refs_1_ = bf16[6,216,128]{2,1,0:T(8,128)(2,1)S(1)} collective-permute-done((bf16[6,216,128]{2,1,0:T(8,128)(2,1)S(1)}, bf16[6,216,128]{2,1,0:T(8,128)(2,1)S(1)}, u32[]{:S(2)}, u32[]{:S(2)}) %collective-permute-start.7) | collective-permute-done | bytes 331808 | tf_op jit(solution)/shard_map/ppermute | solution.py:386
  27.4 0.5 %spread_terms.1 = (bf16[4,216,128]{2,1,0:T(8,128)(2,1)S(1)}, bf16[4,216,128]{2,1,0:T(8,128)(2,1)S(1)}, bf16[4,216,128]{2,1,0:T(8,128)(2,1)S(1)}, bf16[4,216,128]{2,1,0:T(8,128)(2,1)S(1)}) custom-call(s32[1,6]{1,0:T(1,128)S(1)} %broadcast_select_fusion.where_ref, ...), custom_call_target="tpu_custom_call", output_to_operand_aliasing={{0}: (3, {}), {1}: (4, {}), {2}: (5, {}), {3}: (6, {})} | custom-call | tf_op jit(solution)/shard_map/spread_terms/pallas_call | solution.py:312
  27.9 1.9 %collective-permute-start.8 = (bf16[4,216,128]{2,1,0:T(8,128)(2,1)S(1)}, bf16[4,216,128]{2,1,0:T(8,128)(2,1)S(1)}, u32[]{:S(2)}, u32[]{:S(2)}) collective-permute-start(bf16[4,216,128]{2,1,0:T(8,128)(2,1)S(1)} %get-tuple-element.70), channel_id=1, source_target_pairs={{0,6},{1,25},{2,4},{3,27},{4,2},{5,29},{6,0},{7,31},{8,14},{9,17},... | collective-permute-start | bytes 663560 | tf_op jit(solution)/shard_map/ppermute | solution.py:383
  29.8 1.4 %collective-permute-start.9 = (bf16[4,216,128]{2,1,0:T(8,128)(2,1)S(1)}, bf16[4,216,128]{2,1,0:T(8,128)(2,1)S(1)}, u32[]{:S(2)}, u32[]{:S(2)}) collective-permute-start(bf16[4,216,128]{2,1,0:T(8,128)(2,1)S(1)} %get-tuple-element.71), channel_id=1, source_target_pairs={{0,4},{1,17},{2,6},{3,19},{4,0},{5,21},{6,2},{7,23},{8,12},{9,25},... | collective-permute-start | bytes 663560 | tf_op jit(solution)/shard_map/ppermute | solution.py:383
  31.2 0.3 collective-permute-start.10
  31.5 0.2 collective-permute-start.14
  31.7 1.7 %attend_outputs.1 = bf16[1024,512]{1,0:T(8,128)(2,1)} custom-call(bf16[2,144,512]{2,1,0:T(8,128)(2,1)S(1)} %get-tuple-element.73.probs_ref, bf16[2,144,576]{2,1,0:T(8,128)(2,1)S(1)} %get-tuple-element.74.keys_ref, bf16[2,208,512]{2,1,0:T(8,128)(2,1)S(1)} %get-tuple-element.75.near_probs_ref, bf16[2,208,576]{2,1,0:T(8,128)(2,1)S(1)} %get-tuple-element.76.near_keys_ref), custom_call_target="tpu_custom_call" | custom-call | flops 369098752 | bytes 4194304 | tf_op jit(solution)/shard_map/attend_outputs/pallas_call | solution.py:271
  33.4 1.5 %collective-permute-done.8.refs_1_ = bf16[4,216,128]{2,1,0:T(8,128)(2,1)S(1)} collective-permute-done((bf16[4,216,128]{2,1,0:T(8,128)(2,1)S(1)}, bf16[4,216,128]{2,1,0:T(8,128)(2,1)S(1)}, u32[]{:S(2)}, u32[]{:S(2)}) %collective-permute-start.8) | collective-permute-done | bytes 221216 | tf_op jit(solution)/shard_map/ppermute | solution.py:383
  34.9 2.3 %collective-permute-done.9.refs_2_ = bf16[4,216,128]{2,1,0:T(8,128)(2,1)S(1)} collective-permute-done((bf16[4,216,128]{2,1,0:T(8,128)(2,1)S(1)}, bf16[4,216,128]{2,1,0:T(8,128)(2,1)S(1)}, u32[]{:S(2)}, u32[]{:S(2)}) %collective-permute-start.9) | collective-permute-done | bytes 221216 | tf_op jit(solution)/shard_map/ppermute | solution.py:383
  37.4 1.8 %collective-permute-start.12 = (bf16[1,216,128]{2,1,0:T(8,128)(2,1)S(1)}, bf16[1,216,128]{2,1,0:T(8,128)(2,1)S(1)}, u32[]{:S(2)}, u32[]{:S(2)}) collective-permute-start(bf16[1,216,128]{2,1,0:T(8,128)(2,1)S(1)} %get-tuple-element.84), channel_id=1, source_target_pairs={{0,24},{1,7},{2,26},{3,5},{4,28},{5,3},{6,30},{7,1},{8,16},{9,15},... | collective-permute-start | bytes 165896 | tf_op jit(solution)/shard_map/ppermute | solution.py:383
  39.2 1.6 %collective-permute-start.13 = (bf16[1,216,128]{2,1,0:T(8,128)(2,1)S(1)}, bf16[1,216,128]{2,1,0:T(8,128)(2,1)S(1)}, u32[]{:S(2)}, u32[]{:S(2)}) collective-permute-start(bf16[1,216,128]{2,1,0:T(8,128)(2,1)S(1)} %get-tuple-element.85), channel_id=1, source_target_pairs={{0,8},{1,3},{2,10},{3,1},{4,12},{5,7},{6,14},{7,5},{8,0},{9,11},{1... | collective-permute-start | bytes 165896 | tf_op jit(solution)/shard_map/ppermute | solution.py:383
  40.9 0.8 %copy.15 = bf16[128,576]{0,1:T(8,128)(2,1)} copy(bf16[128,576]{1,0:T(8,128)(2,1)S(1)} %add.61) | data formatting | bytes 294912
  41.7 0.7 %collective-permute-done.11.refs_0_ = bf16[1,216,128]{2,1,0:T(8,128)(2,1)S(1)} collective-permute-done((bf16[1,216,128]{2,1,0:T(8,128)(2,1)S(1)}, bf16[1,216,128]{2,1,0:T(8,128)(2,1)S(1)}, u32[]{:S(2)}, u32[]{:S(2)}) %collective-permute-start.11) | collective-permute-done | bytes 55328 | tf_op jit(solution)/shard_map/ppermute | solution.py:383
  42.4 1.1 %collective-permute-done.12.refs_1_ = bf16[1,216,128]{2,1,0:T(8,128)(2,1)S(1)} collective-permute-done((bf16[1,216,128]{2,1,0:T(8,128)(2,1)S(1)}, bf16[1,216,128]{2,1,0:T(8,128)(2,1)S(1)}, u32[]{:S(2)}, u32[]{:S(2)}) %collective-permute-start.12) | collective-permute-done | bytes 55328 | tf_op jit(solution)/shard_map/ppermute | solution.py:383
  43.5 0.5 %collective-permute-done.13.refs_2_ = bf16[1,216,128]{2,1,0:T(8,128)(2,1)S(1)} collective-permute-done((bf16[1,216,128]{2,1,0:T(8,128)(2,1)S(1)}, bf16[1,216,128]{2,1,0:T(8,128)(2,1)S(1)}, u32[]{:S(2)}, u32[]{:S(2)}) %collective-permute-start.13) | collective-permute-done | bytes 55328 | tf_op jit(solution)/shard_map/ppermute | solution.py:383
  44.0 0.7 %finish_nodes.1 = bf16[1,48,576]{2,1,0:T(8,128)(2,1)} custom-call(f32[1,216,128]{2,1,0:T(8,128)S(1)} %get-tuple-element.82.keep_ref, bf16[1,216,128]{2,1,0:T(8,128)(2,1)S(1)} %collective-permute-done.11.refs_0_, bf16[1,216,128]{2,1,0:T(8,128)(2,1)S(1)} %collective-permute-done.12.refs_1_, bf16[1,216,128]{2,1,0:T(8,128)(2,1)S(1)} %collective-permute-done.13.refs_2_), custom_call_target="tpu_custom_call" | custom-call | tf_op jit(solution)/shard_map/finish_nodes/pallas_call | solution.py:358
  (25 shorter events, 1.0 us)
Async XLA Ops:
  0.6 12.0 %copy-start.1 = (bf16[1,48,576]{2,1,0:T(8,128)(2,1)S(1)}, bf16[1,48,576]{2,1,0:T(8,128)(2,1)}, u32[]{:S(2)}) copy-start(bf16[1,48,576]{2,1,0:T(8,128)(2,1)} %refs_0_.1) | copy-start | bytes 165892
  0.6 8.7 %collective-permute-start.1 = (bf16[1,48,576]{2,1,0:T(8,128)(2,1)}, bf16[1,48,576]{2,1,0:T(8,128)(2,1)S(1)}, u32[]{:S(2)}, u32[]{:S(2)}) collective-permute-start(bf16[1,48,576]{2,1,0:T(8,128)(2,1)} %refs_0_.1), channel_id=1, source_target_pairs={{0,16},{1,5},{2,18},{3,7},{4,20},{5,1},{6,22},{7,3},{8,24},{9,13},... | collective-permute-start | bytes 165896 | tf_op jit(solution)/shard_map/ppermute | solution.py:383
  4.8 4.6 %collective-permute-start = (bf16[1,48,576]{2,1,0:T(8,128)(2,1)}, bf16[1,48,576]{2,1,0:T(8,128)(2,1)S(1)}, u32[]{:S(2)}, u32[]{:S(2)}) collective-permute-start(bf16[1,48,576]{2,1,0:T(8,128)(2,1)} %refs_0_.1), channel_id=1, source_target_pairs={{0,8},{1,3},{2,10},{3,1},{4,12},{5,7},{6,14},{7,5},{8,0},{9,11},{1... | collective-permute-start | bytes 165896 | tf_op jit(solution)/shard_map/ppermute | solution.py:383
  6.3 6.2 %collective-permute-start.2 = (bf16[1,48,576]{2,1,0:T(8,128)(2,1)}, bf16[1,48,576]{2,1,0:T(8,128)(2,1)S(1)}, u32[]{:S(2)}, u32[]{:S(2)}) collective-permute-start(bf16[1,48,576]{2,1,0:T(8,128)(2,1)} %refs_0_.1), channel_id=1, source_target_pairs={{0,24},{1,7},{2,26},{3,5},{4,28},{5,3},{6,30},{7,1},{8,16},{9,15},... | collective-permute-start | bytes 165896 | tf_op jit(solution)/shard_map/ppermute | solution.py:383
  12.7 6.9 %collective-permute-start.5 = (bf16[4,216,128]{2,1,0:T(8,128)(2,1)S(1)}, bf16[4,216,128]{2,1,0:T(8,128)(2,1)S(1)}, u32[]{:S(2)}, u32[]{:S(2)}) collective-permute-start(bf16[4,216,128]{2,1,0:T(8,128)(2,1)S(1)} %pack_nodes.1), channel_id=1, source_target_pairs={{0,6},{1,25},{2,4},{3,27},{4,2},{5,29},{6,0},{7,31},{8,14},{9,17},... | collective-permute-start | bytes 663560 | tf_op jit(solution)/shard_map/ppermute | solution.py:383
  15.6 6.4 %collective-permute-start.4 = (bf16[4,216,128]{2,1,0:T(8,128)(2,1)S(1)}, bf16[4,216,128]{2,1,0:T(8,128)(2,1)S(1)}, u32[]{:S(2)}, u32[]{:S(2)}) collective-permute-start(bf16[4,216,128]{2,1,0:T(8,128)(2,1)S(1)} %pack_nodes.1), channel_id=1, source_target_pairs={{0,4},{1,17},{2,6},{3,19},{4,0},{5,21},{6,2},{7,23},{8,12},{9,25},... | collective-permute-start | bytes 663560 | tf_op jit(solution)/shard_map/ppermute | solution.py:383
  15.8 6.4 %collective-permute-start.3 = (bf16[4,216,128]{2,1,0:T(8,128)(2,1)S(1)}, bf16[4,216,128]{2,1,0:T(8,128)(2,1)S(1)}, u32[]{:S(2)}, u32[]{:S(2)}) collective-permute-start(bf16[4,216,128]{2,1,0:T(8,128)(2,1)S(1)} %pack_nodes.1), channel_id=1, source_target_pairs={{0,2},{1,9},{2,0},{3,11},{4,6},{5,13},{6,4},{7,15},{8,10},{9,1},{1... | collective-permute-start | bytes 663560 | tf_op jit(solution)/shard_map/ppermute | solution.py:383
  16.2 6.3 %copy-start.3 = (s32[2]{0:T(128)S(1)}, s32[2]{0:T(128)}, u32[]{:S(2)}) copy-start(s32[2]{0:T(128)} %param.11) | copy-start | bytes 28
  16.3 6.3 %copy-start.2 = (bf16[128,576]{0,1:T(8,128)(2,1)S(1)}, bf16[128,576]{0,1:T(8,128)(2,1)}, u32[]{:S(2)}) copy-start(bf16[128,576]{0,1:T(8,128)(2,1)} %param.7) | copy-start | bytes 442372
  16.3 6.5 %copy-start = (bf16[128,8,512]{2,1,0:T(8,128)(2,1)S(1)}, bf16[128,8,512]{2,1,0:T(8,128)(2,1)}, u32[]{:S(2)}) copy-start(bf16[128,8,512]{2,1,0:T(8,128)(2,1)} %param.9) | copy-start | bytes 3145732
  22.4 1.7 %collective-permute-start.6 = (bf16[6,216,128]{2,1,0:T(8,128)(2,1)S(1)}, bf16[6,216,128]{2,1,0:T(8,128)(2,1)S(1)}, u32[]{:S(2)}, u32[]{:S(2)}) collective-permute-start(bf16[6,216,128]{2,1,0:T(8,128)(2,1)S(1)} %select_nodes.1.part_ref), channel_id=1, source_target_pairs={{0,1},{1,0},{2,3},{3,2},{4,5},{5,4},{6,7},{7,6},{8,9},{9,8},{10,11... | collective-permute-start | bytes 995336 | tf_op jit(solution)/shard_map/ppermute | solution.py:386
  25.7 1.7 %collective-permute-start.7 = (bf16[6,216,128]{2,1,0:T(8,128)(2,1)S(1)}, bf16[6,216,128]{2,1,0:T(8,128)(2,1)S(1)}, u32[]{:S(2)}, u32[]{:S(2)}) collective-permute-start(bf16[6,216,128]{2,1,0:T(8,128)(2,1)S(1)} %get-tuple-element.58), channel_id=1, source_target_pairs={{0,1},{1,0},{2,3},{3,2},{4,5},{5,4},{6,7},{7,6},{8,9},{9,8},{10,11... | collective-permute-start | bytes 995336 | tf_op jit(solution)/shard_map/ppermute | solution.py:386
  27.9 7.0 %collective-permute-start.8 = (bf16[4,216,128]{2,1,0:T(8,128)(2,1)S(1)}, bf16[4,216,128]{2,1,0:T(8,128)(2,1)S(1)}, u32[]{:S(2)}, u32[]{:S(2)}) collective-permute-start(bf16[4,216,128]{2,1,0:T(8,128)(2,1)S(1)} %get-tuple-element.70), channel_id=1, source_target_pairs={{0,6},{1,25},{2,4},{3,27},{4,2},{5,29},{6,0},{7,31},{8,14},{9,17},... | collective-permute-start | bytes 663560 | tf_op jit(solution)/shard_map/ppermute | solution.py:383
  29.8 7.4 %collective-permute-start.9 = (bf16[4,216,128]{2,1,0:T(8,128)(2,1)S(1)}, bf16[4,216,128]{2,1,0:T(8,128)(2,1)S(1)}, u32[]{:S(2)}, u32[]{:S(2)}) collective-permute-start(bf16[4,216,128]{2,1,0:T(8,128)(2,1)S(1)} %get-tuple-element.71), channel_id=1, source_target_pairs={{0,4},{1,17},{2,6},{3,19},{4,0},{5,21},{6,2},{7,23},{8,12},{9,25},... | collective-permute-start | bytes 663560 | tf_op jit(solution)/shard_map/ppermute | solution.py:383
  31.2 6.0 %collective-permute-start.10 = (bf16[4,216,128]{2,1,0:T(8,128)(2,1)S(1)}, bf16[4,216,128]{2,1,0:T(8,128)(2,1)S(1)}, u32[]{:S(2)}, u32[]{:S(2)}) collective-permute-start(bf16[4,216,128]{2,1,0:T(8,128)(2,1)S(1)} %get-tuple-element.72), channel_id=1, source_target_pairs={{0,2},{1,9},{2,0},{3,11},{4,6},{5,13},{6,4},{7,15},{8,10},{9,1},{1... | collective-permute-start | bytes 663560 | tf_op jit(solution)/shard_map/ppermute | solution.py:383
  31.5 9.4 %collective-permute-start.14 = (bf16[128,576]{1,0:T(8,128)(2,1)S(1)}, bf16[128,576]{1,0:T(8,128)(2,1)S(1)}, u32[]{:S(2)}, u32[]{:S(2)}) collective-permute-start(bf16[128,576]{1,0:T(8,128)(2,1)S(1)} %get-tuple-element.86), channel_id=1, source_target_pairs={{0,1},{1,0},{2,3},{3,2},{4,5},{5,4},{6,7},{7,6},{8,9},{9,8},{10,11... | collective-permute-start | bytes 442376 | tf_op jit(solution)/shard_map/ppermute | solution.py:386
  37.3 5.1 %collective-permute-start.11 = (bf16[1,216,128]{2,1,0:T(8,128)(2,1)S(1)}, bf16[1,216,128]{2,1,0:T(8,128)(2,1)S(1)}, u32[]{:S(2)}, u32[]{:S(2)}) collective-permute-start(bf16[1,216,128]{2,1,0:T(8,128)(2,1)S(1)} %get-tuple-element.83), channel_id=1, source_target_pairs={{0,16},{1,5},{2,18},{3,7},{4,20},{5,1},{6,22},{7,3},{8,24},{9,13},... | collective-permute-start | bytes 165896 | tf_op jit(solution)/shard_map/ppermute | solution.py:383
  37.4 6.1 %collective-permute-start.12 = (bf16[1,216,128]{2,1,0:T(8,128)(2,1)S(1)}, bf16[1,216,128]{2,1,0:T(8,128)(2,1)S(1)}, u32[]{:S(2)}, u32[]{:S(2)}) collective-permute-start(bf16[1,216,128]{2,1,0:T(8,128)(2,1)S(1)} %get-tuple-element.84), channel_id=1, source_target_pairs={{0,24},{1,7},{2,26},{3,5},{4,28},{5,3},{6,30},{7,1},{8,16},{9,15},... | collective-permute-start | bytes 165896 | tf_op jit(solution)/shard_map/ppermute | solution.py:383
  39.2 4.7 %collective-permute-start.13 = (bf16[1,216,128]{2,1,0:T(8,128)(2,1)S(1)}, bf16[1,216,128]{2,1,0:T(8,128)(2,1)S(1)}, u32[]{:S(2)}, u32[]{:S(2)}) collective-permute-start(bf16[1,216,128]{2,1,0:T(8,128)(2,1)S(1)} %get-tuple-element.85), channel_id=1, source_target_pairs={{0,8},{1,3},{2,10},{3,1},{4,12},{5,7},{6,14},{7,5},{8,0},{9,11},{1... | collective-permute-start | bytes 165896 | tf_op jit(solution)/shard_map/ppermute | solution.py:383

commit v6 on v5

--- a/solution.py
+++ b/solution.py
@@ -67,18 +67,18 @@
     return (max(p[0].stop for p in parts), max(p[1].stop for p in parts))
 
 
-def pack_kernel(*refs):
+def pack_kernel(places, *refs):
     out_ref = refs[-1]
-    for i, ref in enumerate(refs[:-1]):
+    for i, ref in zip(places, refs[:-1]):
         for prow, plane, row, col in pieces(*ref.shape[1:]):
             out_ref[i, prow, plane] = ref[0, row, col]
 
 
-def pack(blocks):
+def pack(blocks, places):
     slice_rows, width = blocks[0].shape[1:]
     shape = (len(blocks),) + packed_shape(slice_rows, width)
     return pl.pallas_call(
-        pack_kernel,
+        functools.partial(pack_kernel, places),
         out_shape=jax.ShapeDtypeStruct(shape, blocks[0].dtype),
         in_specs=vmem(len(blocks)),
         out_specs=vmem(1)[0],
@@ -395,8 +395,8 @@
     order = list(range(side - 1, 0, -1))
     got = {d: step(node_latent, 0, d) for d in order}
     query = queries.reshape(rows * heads, width)
-    got, query, own = lax.optimization_barrier(([got[d] for d in range(1, side)], query, leaf_latent))
-    inner = pack([node_latent] + got)
+    got, query, own = lax.optimization_barrier(([got[d] for d in order], query, leaf_latent))
+    inner = pack([node_latent] + got, [0] + order)
     got = {d: step(inner, 1, d) for d in order}
     table = jnp.concatenate([inner] + [got[d] for d in range(1, side)], axis=0)
     mine = select(where, table)

time: 45.2 us -> 44.3 us (0.980)
  waiting for transfers between devices: 16.2 us -> 15.6 us
    ppermute x12, waiting for transfers between devices: 15.2 us -> 14.6 us  [step(): return lax.ppermute(value, axes, pairs)]
  transfers between devices with their start and end apart: 15 -> 15, of which waited for: 11 -> 12; matrix products, arithmetic and copies ran while one was open for 9% -> 9% of each run, Pallas kernels for 8% -> 8%
where the time goes in v6:
time: 44.3 us; the launch traced here: 44.1 us
  starting transfers between devices  16.9 us (38%)
  waiting for transfers between devices  15.6 us (35%)
  Pallas kernels  6.71 us (15%)
  local copies, waits for them, and re-layouts  3.27 us (7%)
  other arithmetic  0.93 us (2%)
  between operations  0.74 us (2%)
    ppermute x12, starting transfers between devices, step(): return lax.ppermute(value, axes, pairs)  16.3 us
    ppermute x12, waiting for transfers between devices, step(): return lax.ppermute(value, axes, pairs)  14.6 us
    unnamed x10, local copies, waits for them, and re-layouts  3.02 us
    pallas_call x1, Pallas kernels, outputs(): pl.pallas_call(functools.partial(outputs_kernel, leaves), out_shape=jax.S...  1.72 us
    pallas_call x1, Pallas kernels, attend(): pl.pallas_call(functools.partial(attend_kernel, len(parts), leaves, slice...  1.61 us
    pallas_call x1, Pallas kernels, near_scores(): pl.pallas_call(functools.partial(near_kernel, leaves, heads, slice_rows),...  0.99 us
    ppermute x3, waiting for transfers between devices, swap(): lax.ppermute(value, 'head', [(i, i ^ distance) for i in range(head_size)])  0.95 us
  transfers between devices with their start and end apart: 15, of which 12 were waited for; matrix products, arithmetic and copies ran while one was open for 9% of the time, Pallas kernels for 8%

profile of v6, /device:TPU:0, one launch (start us, length us, event | category | flops | bytes accessed | tf_op | source)
XLA Modules:
  0.0 44.1 jit_solution(7097476860458829190)
XLA Ops:
  0.6 4.1 %collective-permute-start.1 = (bf16[1,48,576]{2,1,0:T(8,128)(2,1)}, bf16[1,48,576]{2,1,0:T(8,128)(2,1)S(1)}, u32[]{:S(2)}, u32[]{:S(2)}) collective-permute-start(bf16[1,48,576]{2,1,0:T(8,128)(2,1)} %refs_0_.1), channel_id=1, source_target_pairs={{0,16},{1,5},{2,18},{3,7},{4,20},{5,1},{6,22},{7,3},{8,24},{9,13},... | collective-permute-start | bytes 165896 | tf_op jit(solution)/shard_map/ppermute | solution.py:383
  4.8 1.3 %collective-permute-start = (bf16[1,48,576]{2,1,0:T(8,128)(2,1)}, bf16[1,48,576]{2,1,0:T(8,128)(2,1)S(1)}, u32[]{:S(2)}, u32[]{:S(2)}) collective-permute-start(bf16[1,48,576]{2,1,0:T(8,128)(2,1)} %refs_0_.1), channel_id=1, source_target_pairs={{0,24},{1,7},{2,26},{3,5},{4,28},{5,3},{6,30},{7,1},{8,16},{9,15},... | collective-permute-start | bytes 165896 | tf_op jit(solution)/shard_map/ppermute | solution.py:383
  6.1 0.2 collective-permute-start.2
  6.4 0.7 %broadcast_xor_fusion = s32[2,3]{1,0:T(2,128)S(1)} fusion(s32[2,3]{1,0:T(2,128)} %param.10, s32[]{:T(128)S(6)} %axis_index.25), kind=kLoop, calls=%fused_computation.15 | loop fusion | flops 6 | bytes 52 | tf_op jit(solution)/shard_map/xor | solution.py:388
  7.1 2.2 %copy.13 = bf16[128,8,576]{2,1,0:T(8,128)(2,1)S(1)} copy(bf16[128,8,576]{0,2,1:T(8,128)(2,1)} %param.6) | data formatting | bytes 2359296 | tf_op args[0]
  9.3 1.8 %collective-permute-done.refs_1_ = bf16[1,48,576]{2,1,0:T(8,128)(2,1)S(1)} collective-permute-done((bf16[1,48,576]{2,1,0:T(8,128)(2,1)}, bf16[1,48,576]{2,1,0:T(8,128)(2,1)S(1)}, u32[]{:S(2)}, u32[]{:S(2)}) %collective-permute-start) | collective-permute-done | bytes 55328 | tf_op jit(solution)/shard_map/ppermute | solution.py:383
  11.3 2.5 %collective-permute-start.5 = (bf16[4,216,128]{2,1,0:T(8,128)(2,1)S(1)}, bf16[4,216,128]{2,1,0:T(8,128)(2,1)S(1)}, u32[]{:S(2)}, u32[]{:S(2)}) collective-permute-start(bf16[4,216,128]{2,1,0:T(8,128)(2,1)S(1)} %pack_nodes.1), channel_id=1, source_target_pairs={{0,6},{1,25},{2,4},{3,27},{4,2},{5,29},{6,0},{7,31},{8,14},{9,17},... | collective-permute-start | bytes 663560 | tf_op jit(solution)/shard_map/ppermute | solution.py:383
  13.8 0.5 %collective-permute-start.4 = (bf16[4,216,128]{2,1,0:T(8,128)(2,1)S(1)}, bf16[4,216,128]{2,1,0:T(8,128)(2,1)S(1)}, u32[]{:S(2)}, u32[]{:S(2)}) collective-permute-start(bf16[4,216,128]{2,1,0:T(8,128)(2,1)S(1)} %pack_nodes.1), channel_id=1, source_target_pairs={{0,4},{1,17},{2,6},{3,19},{4,0},{5,21},{6,2},{7,23},{8,12},{9,25},... | collective-permute-start | bytes 663560 | tf_op jit(solution)/shard_map/ppermute | solution.py:383
  14.3 0.5 %collective-permute-start.3 = (bf16[4,216,128]{2,1,0:T(8,128)(2,1)S(1)}, bf16[4,216,128]{2,1,0:T(8,128)(2,1)S(1)}, u32[]{:S(2)}, u32[]{:S(2)}) collective-permute-start(bf16[4,216,128]{2,1,0:T(8,128)(2,1)S(1)} %pack_nodes.1), channel_id=1, source_target_pairs={{0,2},{1,9},{2,0},{3,11},{4,6},{5,13},{6,4},{7,15},{8,10},{9,1},{1... | collective-permute-start | bytes 663560 | tf_op jit(solution)/shard_map/ppermute | solution.py:383
  14.9 3.4 %collective-permute-done.5 = bf16[4,216,128]{2,1,0:T(8,128)(2,1)S(1)} collective-permute-done((bf16[4,216,128]{2,1,0:T(8,128)(2,1)S(1)}, bf16[4,216,128]{2,1,0:T(8,128)(2,1)S(1)}, u32[]{:S(2)}, u32[]{:S(2)}) %collective-permute-start.5) | collective-permute-done | bytes 221216 | tf_op jit(solution)/shard_map/ppermute | solution.py:383
  18.3 2.3 %collective-permute-done.4 = bf16[4,216,128]{2,1,0:T(8,128)(2,1)S(1)} collective-permute-done((bf16[4,216,128]{2,1,0:T(8,128)(2,1)S(1)}, bf16[4,216,128]{2,1,0:T(8,128)(2,1)S(1)}, u32[]{:S(2)}, u32[]{:S(2)}) %collective-permute-start.4) | collective-permute-done | bytes 221216 | tf_op jit(solution)/shard_map/ppermute | solution.py:383
  21.3 1.0 %near_scores.1 = (f32[2,208,512]{2,1,0:T(8,128)S(1)}, f32[2,208,512]{2,1,0:T(8,128)S(1)}, f32[2,1,512]{2,1,0:T(1,128)S(1)}, f32[2,1,512]{2,1,0:T(1,128)S(1)}, f3...) custom-call(bf16[6,216,128]{2,1,0:T(8,128)(2,1)S(1)} %select_nodes.1.part_ref, ...), custom_call_target="tpu_custom_call" | custom-call | flops 490733568 | bytes 4194304 | tf_op jit(solution)/shard_map/near_scores/pallas_call | solution.py:150
  22.3 0.3 collective-permute-done.6.refs_0_
  22.6 1.6 %attend.1 = (bf16[6,216,128]{2,1,0:T(8,128)(2,1)S(1)}, f32[2,1,512]{2,1,0:T(1,128)S(1)}, f32[2,1,512]{2,1,0:T(1,128)S(1)}, bf16[2,144,512]{2,1,0:T(8,128)(2,1)S(1)}, bf16[2,144,576]{2,1,0:T(8,128)(2,1)S(1)}) custom-call(f32[2,1,512]{2,1,0:T(1,128)S(1)} %compare_convert_fusion.live_ref, bf16[1024,576]{1,0:T(8,128)(2,1)S(1)} %bitcast.4, ...), custom_call_target="tpu_custom_call" | custom-call | flops 679477248 | bytes 8388608 | tf_op jit(solution)/shard_map/attend/pallas_call | solution.py:207
  24.4 0.8 %own_terms.1 = (f32[6,216,128]{2,1,0:T(8,128)S(1)}, bf16[128,576]{1,0:T(8,128)(2,1)S(1)}, bf16[2,208,512]{2,1,0:T(8,128)(2,1)S(1)}, bf16[4,216,128]{2,1,0:T(8,12...) custom-call(bf16[1024,576]{1,0:T(8,128)(2,1)S(1)} %bitcast.5, ...), custom_call_target="tpu_custom_call" | custom-call | flops 490733568 | bytes 4194304 | tf_op jit(solution)/shard_map/own_terms/pallas_call | solution.py:248
  25.2 0.7 %collective-permute-done.7.refs_1_ = bf16[6,216,128]{2,1,0:T(8,128)(2,1)S(1)} collective-permute-done((bf16[6,216,128]{2,1,0:T(8,128)(2,1)S(1)}, bf16[6,216,128]{2,1,0:T(8,128)(2,1)S(1)}, u32[]{:S(2)}, u32[]{:S(2)}) %collective-permute-start.7) | collective-permute-done | bytes 331808 | tf_op jit(solution)/shard_map/ppermute | solution.py:386
  25.9 0.5 %spread_terms.1 = (bf16[4,216,128]{2,1,0:T(8,128)(2,1)S(1)}, bf16[4,216,128]{2,1,0:T(8,128)(2,1)S(1)}, bf16[4,216,128]{2,1,0:T(8,128)(2,1)S(1)}, bf16[4,216,128]{2,1,0:T(8,128)(2,1)S(1)}) custom-call(s32[1,6]{1,0:T(1,128)S(1)} %broadcast_select_fusion.where_ref, ...), custom_call_target="tpu_custom_call", output_to_operand_aliasing={{0}: (3, {}), {1}: (4, {}), {2}: (5, {}), {3}: (6, {})} | custom-call | tf_op jit(solution)/shard_map/spread_terms/pallas_call | solution.py:312
  26.4 2.2 %collective-permute-start.8 = (bf16[4,216,128]{2,1,0:T(8,128)(2,1)S(1)}, bf16[4,216,128]{2,1,0:T(8,128)(2,1)S(1)}, u32[]{:S(2)}, u32[]{:S(2)}) collective-permute-start(bf16[4,216,128]{2,1,0:T(8,128)(2,1)S(1)} %get-tuple-element.70), channel_id=1, source_target_pairs={{0,6},{1,25},{2,4},{3,27},{4,2},{5,29},{6,0},{7,31},{8,14},{9,17},... | collective-permute-start | bytes 663560 | tf_op jit(solution)/shard_map/ppermute | solution.py:383
  28.6 0.8 %collective-permute-start.9 = (bf16[4,216,128]{2,1,0:T(8,128)(2,1)S(1)}, bf16[4,216,128]{2,1,0:T(8,128)(2,1)S(1)}, u32[]{:S(2)}, u32[]{:S(2)}) collective-permute-start(bf16[4,216,128]{2,1,0:T(8,128)(2,1)S(1)} %get-tuple-element.71), channel_id=1, source_target_pairs={{0,4},{1,17},{2,6},{3,19},{4,0},{5,21},{6,2},{7,23},{8,12},{9,25},... | collective-permute-start | bytes 663560 | tf_op jit(solution)/shard_map/ppermute | solution.py:383
  29.4 0.5 %collective-permute-start.10 = (bf16[4,216,128]{2,1,0:T(8,128)(2,1)S(1)}, bf16[4,216,128]{2,1,0:T(8,128)(2,1)S(1)}, u32[]{:S(2)}, u32[]{:S(2)}) collective-permute-start(bf16[4,216,128]{2,1,0:T(8,128)(2,1)S(1)} %get-tuple-element.72), channel_id=1, source_target_pairs={{0,2},{1,9},{2,0},{3,11},{4,6},{5,13},{6,4},{7,15},{8,10},{9,1},{1... | collective-permute-start | bytes 663560 | tf_op jit(solution)/shard_map/ppermute | solution.py:383
  30.0 0.2 collective-permute-start.14
  30.2 1.7 %attend_outputs.1 = bf16[1024,512]{1,0:T(8,128)(2,1)} custom-call(bf16[2,144,512]{2,1,0:T(8,128)(2,1)S(1)} %get-tuple-element.73.probs_ref, bf16[2,144,576]{2,1,0:T(8,128)(2,1)S(1)} %get-tuple-element.74.keys_ref, bf16[2,208,512]{2,1,0:T(8,128)(2,1)S(1)} %get-tuple-element.75.near_probs_ref, bf16[2,208,576]{2,1,0:T(8,128)(2,1)S(1)} %get-tuple-element.76.near_keys_ref), custom_call_target="tpu_custom_call" | custom-call | flops 369098752 | bytes 4194304 | tf_op jit(solution)/shard_map/attend_outputs/pallas_call | solution.py:271
  31.9 1.5 %collective-permute-done.8.refs_1_ = bf16[4,216,128]{2,1,0:T(8,128)(2,1)S(1)} collective-permute-done((bf16[4,216,128]{2,1,0:T(8,128)(2,1)S(1)}, bf16[4,216,128]{2,1,0:T(8,128)(2,1)S(1)}, u32[]{:S(2)}, u32[]{:S(2)}) %collective-permute-start.8) | collective-permute-done | bytes 221216 | tf_op jit(solution)/shard_map/ppermute | solution.py:383
  33.4 2.3 %collective-permute-done.9.refs_2_ = bf16[4,216,128]{2,1,0:T(8,128)(2,1)S(1)} collective-permute-done((bf16[4,216,128]{2,1,0:T(8,128)(2,1)S(1)}, bf16[4,216,128]{2,1,0:T(8,128)(2,1)S(1)}, u32[]{:S(2)}, u32[]{:S(2)}) %collective-permute-start.9) | collective-permute-done | bytes 221216 | tf_op jit(solution)/shard_map/ppermute | solution.py:383
  35.8 1.1 %collective-permute-start.11 = (bf16[1,216,128]{2,1,0:T(8,128)(2,1)S(1)}, bf16[1,216,128]{2,1,0:T(8,128)(2,1)S(1)}, u32[]{:S(2)}, u32[]{:S(2)}) collective-permute-start(bf16[1,216,128]{2,1,0:T(8,128)(2,1)S(1)} %get-tuple-element.83), channel_id=1, source_target_pairs={{0,16},{1,5},{2,18},{3,7},{4,20},{5,1},{6,22},{7,3},{8,24},{9,13},... | collective-permute-start | bytes 165896 | tf_op jit(solution)/shard_map/ppermute | solution.py:383
  36.9 1.7 %collective-permute-start.12 = (bf16[1,216,128]{2,1,0:T(8,128)(2,1)S(1)}, bf16[1,216,128]{2,1,0:T(8,128)(2,1)S(1)}, u32[]{:S(2)}, u32[]{:S(2)}) collective-permute-start(bf16[1,216,128]{2,1,0:T(8,128)(2,1)S(1)} %get-tuple-element.84), channel_id=1, source_target_pairs={{0,24},{1,7},{2,26},{3,5},{4,28},{5,3},{6,30},{7,1},{8,16},{9,15},... | collective-permute-start | bytes 165896 | tf_op jit(solution)/shard_map/ppermute | solution.py:383
  38.6 0.7 %collective-permute-start.13 = (bf16[1,216,128]{2,1,0:T(8,128)(2,1)S(1)}, bf16[1,216,128]{2,1,0:T(8,128)(2,1)S(1)}, u32[]{:S(2)}, u32[]{:S(2)}) collective-permute-start(bf16[1,216,128]{2,1,0:T(8,128)(2,1)S(1)} %get-tuple-element.85), channel_id=1, source_target_pairs={{0,8},{1,3},{2,10},{3,1},{4,12},{5,7},{6,14},{7,5},{8,0},{9,11},{1... | collective-permute-start | bytes 165896 | tf_op jit(solution)/shard_map/ppermute | solution.py:383
  39.4 0.8 %copy.15 = bf16[128,576]{0,1:T(8,128)(2,1)} copy(bf16[128,576]{1,0:T(8,128)(2,1)S(1)} %add.61) | data formatting | bytes 294912
  40.2 1.2 %collective-permute-done.11.refs_0_ = bf16[1,216,128]{2,1,0:T(8,128)(2,1)S(1)} collective-permute-done((bf16[1,216,128]{2,1,0:T(8,128)(2,1)S(1)}, bf16[1,216,128]{2,1,0:T(8,128)(2,1)S(1)}, u32[]{:S(2)}, u32[]{:S(2)}) %collective-permute-start.11) | collective-permute-done | bytes 55328 | tf_op jit(solution)/shard_map/ppermute | solution.py:383
  41.4 1.6 %collective-permute-done.12.refs_1_ = bf16[1,216,128]{2,1,0:T(8,128)(2,1)S(1)} collective-permute-done((bf16[1,216,128]{2,1,0:T(8,128)(2,1)S(1)}, bf16[1,216,128]{2,1,0:T(8,128)(2,1)S(1)}, u32[]{:S(2)}, u32[]{:S(2)}) %collective-permute-start.12) | collective-permute-done | bytes 55328 | tf_op jit(solution)/shard_map/ppermute | solution.py:383
  43.0 0.4 collective-permute-done.13.refs_2_
  43.4 0.7 %finish_nodes.1 = bf16[1,48,576]{2,1,0:T(8,128)(2,1)} custom-call(f32[1,216,128]{2,1,0:T(8,128)S(1)} %get-tuple-element.82.keep_ref, bf16[1,216,128]{2,1,0:T(8,128)(2,1)S(1)} %collective-permute-done.11.refs_0_, bf16[1,216,128]{2,1,0:T(8,128)(2,1)S(1)} %collective-permute-done.12.refs_1_, bf16[1,216,128]{2,1,0:T(8,128)(2,1)S(1)} %collective-permute-done.13.refs_2_), custom_call_target="tpu_custom_call" | custom-call | tf_op jit(solution)/shard_map/finish_nodes/pallas_call | solution.py:358
  (25 shorter events, 1.4 us)
Async XLA Ops:
  0.6 10.6 %copy-start.1 = (bf16[1,48,576]{2,1,0:T(8,128)(2,1)S(1)}, bf16[1,48,576]{2,1,0:T(8,128)(2,1)}, u32[]{:S(2)}) copy-start(bf16[1,48,576]{2,1,0:T(8,128)(2,1)} %refs_0_.1) | copy-start | bytes 165892
  0.6 8.7 %collective-permute-start.1 = (bf16[1,48,576]{2,1,0:T(8,128)(2,1)}, bf16[1,48,576]{2,1,0:T(8,128)(2,1)S(1)}, u32[]{:S(2)}, u32[]{:S(2)}) collective-permute-start(bf16[1,48,576]{2,1,0:T(8,128)(2,1)} %refs_0_.1), channel_id=1, source_target_pairs={{0,16},{1,5},{2,18},{3,7},{4,20},{5,1},{6,22},{7,3},{8,24},{9,13},... | collective-permute-start | bytes 165896 | tf_op jit(solution)/shard_map/ppermute | solution.py:383
  4.8 6.3 %collective-permute-start = (bf16[1,48,576]{2,1,0:T(8,128)(2,1)}, bf16[1,48,576]{2,1,0:T(8,128)(2,1)S(1)}, u32[]{:S(2)}, u32[]{:S(2)}) collective-permute-start(bf16[1,48,576]{2,1,0:T(8,128)(2,1)} %refs_0_.1), channel_id=1, source_target_pairs={{0,24},{1,7},{2,26},{3,5},{4,28},{5,3},{6,30},{7,1},{8,16},{9,15},... | collective-permute-start | bytes 165896 | tf_op jit(solution)/shard_map/ppermute | solution.py:383
  6.1 5.1 %collective-permute-start.2 = (bf16[1,48,576]{2,1,0:T(8,128)(2,1)}, bf16[1,48,576]{2,1,0:T(8,128)(2,1)S(1)}, u32[]{:S(2)}, u32[]{:S(2)}) collective-permute-start(bf16[1,48,576]{2,1,0:T(8,128)(2,1)} %refs_0_.1), channel_id=1, source_target_pairs={{0,8},{1,3},{2,10},{3,1},{4,12},{5,7},{6,14},{7,5},{8,0},{9,11},{1... | collective-permute-start | bytes 165896 | tf_op jit(solution)/shard_map/ppermute | solution.py:383
  11.3 7.0 %collective-permute-start.5 = (bf16[4,216,128]{2,1,0:T(8,128)(2,1)S(1)}, bf16[4,216,128]{2,1,0:T(8,128)(2,1)S(1)}, u32[]{:S(2)}, u32[]{:S(2)}) collective-permute-start(bf16[4,216,128]{2,1,0:T(8,128)(2,1)S(1)} %pack_nodes.1), channel_id=1, source_target_pairs={{0,6},{1,25},{2,4},{3,27},{4,2},{5,29},{6,0},{7,31},{8,14},{9,17},... | collective-permute-start | bytes 663560 | tf_op jit(solution)/shard_map/ppermute | solution.py:383
  13.8 6.8 %collective-permute-start.4 = (bf16[4,216,128]{2,1,0:T(8,128)(2,1)S(1)}, bf16[4,216,128]{2,1,0:T(8,128)(2,1)S(1)}, u32[]{:S(2)}, u32[]{:S(2)}) collective-permute-start(bf16[4,216,128]{2,1,0:T(8,128)(2,1)S(1)} %pack_nodes.1), channel_id=1, source_target_pairs={{0,4},{1,17},{2,6},{3,19},{4,0},{5,21},{6,2},{7,23},{8,12},{9,25},... | collective-permute-start | bytes 663560 | tf_op jit(solution)/shard_map/ppermute | solution.py:383
  14.3 6.3 %collective-permute-start.3 = (bf16[4,216,128]{2,1,0:T(8,128)(2,1)S(1)}, bf16[4,216,128]{2,1,0:T(8,128)(2,1)S(1)}, u32[]{:S(2)}, u32[]{:S(2)}) collective-permute-start(bf16[4,216,128]{2,1,0:T(8,128)(2,1)S(1)} %pack_nodes.1), channel_id=1, source_target_pairs={{0,2},{1,9},{2,0},{3,11},{4,6},{5,13},{6,4},{7,15},{8,10},{9,1},{1... | collective-permute-start | bytes 663560 | tf_op jit(solution)/shard_map/ppermute | solution.py:383
  14.9 6.2 %copy-start.3 = (s32[2]{0:T(128)S(1)}, s32[2]{0:T(128)}, u32[]{:S(2)}) copy-start(s32[2]{0:T(128)} %param.11) | copy-start | bytes 28
  14.9 6.3 %copy-start.2 = (bf16[128,576]{0,1:T(8,128)(2,1)S(1)}, bf16[128,576]{0,1:T(8,128)(2,1)}, u32[]{:S(2)}) copy-start(bf16[128,576]{0,1:T(8,128)(2,1)} %param.7) | copy-start | bytes 442372
  14.9 6.4 %copy-start = (bf16[128,8,512]{2,1,0:T(8,128)(2,1)S(1)}, bf16[128,8,512]{2,1,0:T(8,128)(2,1)}, u32[]{:S(2)}) copy-start(bf16[128,8,512]{2,1,0:T(8,128)(2,1)} %param.9) | copy-start | bytes 3145732
  20.9 1.7 %collective-permute-start.6 = (bf16[6,216,128]{2,1,0:T(8,128)(2,1)S(1)}, bf16[6,216,128]{2,1,0:T(8,128)(2,1)S(1)}, u32[]{:S(2)}, u32[]{:S(2)}) collective-permute-start(bf16[6,216,128]{2,1,0:T(8,128)(2,1)S(1)} %select_nodes.1.part_ref), channel_id=1, source_target_pairs={{0,1},{1,0},{2,3},{3,2},{4,5},{5,4},{6,7},{7,6},{8,9},{9,8},{10,11... | collective-permute-start | bytes 995336 | tf_op jit(solution)/shard_map/ppermute | solution.py:386
  24.2 1.7 %collective-permute-start.7 = (bf16[6,216,128]{2,1,0:T(8,128)(2,1)S(1)}, bf16[6,216,128]{2,1,0:T(8,128)(2,1)S(1)}, u32[]{:S(2)}, u32[]{:S(2)}) collective-permute-start(bf16[6,216,128]{2,1,0:T(8,128)(2,1)S(1)} %get-tuple-element.58), channel_id=1, source_target_pairs={{0,1},{1,0},{2,3},{3,2},{4,5},{5,4},{6,7},{7,6},{8,9},{9,8},{10,11... | collective-permute-start | bytes 995336 | tf_op jit(solution)/shard_map/ppermute | solution.py:386
  26.4 7.0 %collective-permute-start.8 = (bf16[4,216,128]{2,1,0:T(8,128)(2,1)S(1)}, bf16[4,216,128]{2,1,0:T(8,128)(2,1)S(1)}, u32[]{:S(2)}, u32[]{:S(2)}) collective-permute-start(bf16[4,216,128]{2,1,0:T(8,128)(2,1)S(1)} %get-tuple-element.70), channel_id=1, source_target_pairs={{0,6},{1,25},{2,4},{3,27},{4,2},{5,29},{6,0},{7,31},{8,14},{9,17},... | collective-permute-start | bytes 663560 | tf_op jit(solution)/shard_map/ppermute | solution.py:383
  28.6 7.0 %collective-permute-start.9 = (bf16[4,216,128]{2,1,0:T(8,128)(2,1)S(1)}, bf16[4,216,128]{2,1,0:T(8,128)(2,1)S(1)}, u32[]{:S(2)}, u32[]{:S(2)}) collective-permute-start(bf16[4,216,128]{2,1,0:T(8,128)(2,1)S(1)} %get-tuple-element.71), channel_id=1, source_target_pairs={{0,4},{1,17},{2,6},{3,19},{4,0},{5,21},{6,2},{7,23},{8,12},{9,25},... | collective-permute-start | bytes 663560 | tf_op jit(solution)/shard_map/ppermute | solution.py:383
  29.4 6.2 %collective-permute-start.10 = (bf16[4,216,128]{2,1,0:T(8,128)(2,1)S(1)}, bf16[4,216,128]{2,1,0:T(8,128)(2,1)S(1)}, u32[]{:S(2)}, u32[]{:S(2)}) collective-permute-start(bf16[4,216,128]{2,1,0:T(8,128)(2,1)S(1)} %get-tuple-element.72), channel_id=1, source_target_pairs={{0,2},{1,9},{2,0},{3,11},{4,6},{5,13},{6,4},{7,15},{8,10},{9,1},{1... | collective-permute-start | bytes 663560 | tf_op jit(solution)/shard_map/ppermute | solution.py:383
  30.0 9.4 %collective-permute-start.14 = (bf16[128,576]{1,0:T(8,128)(2,1)S(1)}, bf16[128,576]{1,0:T(8,128)(2,1)S(1)}, u32[]{:S(2)}, u32[]{:S(2)}) collective-permute-start(bf16[128,576]{1,0:T(8,128)(2,1)S(1)} %get-tuple-element.86), channel_id=1, source_target_pairs={{0,1},{1,0},{2,3},{3,2},{4,5},{5,4},{6,7},{7,6},{8,9},{9,8},{10,11... | collective-permute-start | bytes 442376 | tf_op jit(solution)/shard_map/ppermute | solution.py:386
  35.8 5.6 %collective-permute-start.11 = (bf16[1,216,128]{2,1,0:T(8,128)(2,1)S(1)}, bf16[1,216,128]{2,1,0:T(8,128)(2,1)S(1)}, u32[]{:S(2)}, u32[]{:S(2)}) collective-permute-start(bf16[1,216,128]{2,1,0:T(8,128)(2,1)S(1)} %get-tuple-element.83), channel_id=1, source_target_pairs={{0,16},{1,5},{2,18},{3,7},{4,20},{5,1},{6,22},{7,3},{8,24},{9,13},... | collective-permute-start | bytes 165896 | tf_op jit(solution)/shard_map/ppermute | solution.py:383
  36.9 6.1 %collective-permute-start.12 = (bf16[1,216,128]{2,1,0:T(8,128)(2,1)S(1)}, bf16[1,216,128]{2,1,0:T(8,128)(2,1)S(1)}, u32[]{:S(2)}, u32[]{:S(2)}) collective-permute-start(bf16[1,216,128]{2,1,0:T(8,128)(2,1)S(1)} %get-tuple-element.84), channel_id=1, source_target_pairs={{0,24},{1,7},{2,26},{3,5},{4,28},{5,3},{6,30},{7,1},{8,16},{9,15},... | collective-permute-start | bytes 165896 | tf_op jit(solution)/shard_map/ppermute | solution.py:383
  38.6 4.7 %collective-permute-start.13 = (bf16[1,216,128]{2,1,0:T(8,128)(2,1)S(1)}, bf16[1,216,128]{2,1,0:T(8,128)(2,1)S(1)}, u32[]{:S(2)}, u32[]{:S(2)}) collective-permute-start(bf16[1,216,128]{2,1,0:T(8,128)(2,1)S(1)} %get-tuple-element.85), channel_id=1, source_target_pairs={{0,8},{1,3},{2,10},{3,1},{4,12},{5,7},{6,14},{7,5},{8,0},{9,11},{1... | collective-permute-start | bytes 165896 | tf_op jit(solution)/shard_map/ppermute | solution.py:383

commit v7 on v6

--- a/solution.py
+++ b/solution.py
@@ -398,8 +398,11 @@
     got, query, own = lax.optimization_barrier(([got[d] for d in order], query, leaf_latent))
     inner = pack([node_latent] + got, [0] + order)
     got = {d: step(inner, 1, d) for d in order}
-    table = jnp.concatenate([inner] + [got[d] for d in range(1, side)], axis=0)
-    mine = select(where, table)
+    line_up = sorted(range(1, side), key=lambda d: (d == side - 1, d == 1))
+    outer = where // side
+    spot = sum([jnp.where(outer == d, i + 1, 0) for i, d in enumerate(line_up)])
+    table = jnp.concatenate([inner] + [got[d] for d in line_up], axis=0)
+    mine = select(spot * side + where % side, table)
     parts = [swap(mine, d) for d in range(1, head_size)]
     grad = grad_out.reshape(rows * heads, LAT)
     slice_rows = node_latent.shape[1]
@@ -412,7 +415,7 @@
     sends, probs, own_grad = lax.optimization_barrier((sends, probs, own_grad))
     got = {d: step(sends[d], 1, d) for d in order}
     attention = outputs(probs, keys, near_probs, near_keys).reshape(rows, heads, LAT)
-    got, attention = lax.optimization_barrier(([sends[0]] + [got[d] for d in order], attention))
+    got, attention = lax.optimization_barrier(([sends[0]] + [got[d] for d in sorted(range(1, side), key=lambda d: (d != side - 1, d != 1))], attention))
     keep, *sends = merge(got)
     got = {d: step(sends[d - 1], 0, d) for d in order}
     node_grad = finish(keep, [got[d] for d in (*range(2, side), 1)], node_latent.shape)

time: 44.3 us -> 44 us (level)
  transfers between devices with their start and end apart: 15 -> 15, of which waited for: 12 -> 10; matrix products, arithmetic and copies ran while one was open for 9% -> 9% of each run, Pallas kernels for 8% -> 8%
where the time goes in v7:
time: 44 us; the launch traced here: 43.9 us
  starting transfers between devices  17 us (39%)
  waiting for transfers between devices  15.2 us (35%)
  Pallas kernels  6.71 us (15%)
  local copies, waits for them, and re-layouts  3.26 us (7%)
  other arithmetic  0.94 us (2%)
  between operations  0.74 us (2%)
    ppermute x12, starting transfers between devices, step(): return lax.ppermute(value, axes, pairs)  16.3 us
    ppermute x12, waiting for transfers between devices, step(): return lax.ppermute(value, axes, pairs)  14.3 us
    unnamed x10, local copies, waits for them, and re-layouts  3.02 us
    pallas_call x1, Pallas kernels, outputs(): pl.pallas_call(functools.partial(outputs_kernel, leaves), out_shape=jax.S...  1.72 us
    pallas_call x1, Pallas kernels, attend(): pl.pallas_call(functools.partial(attend_kernel, len(parts), leaves, slice...  1.61 us
    pallas_call x1, Pallas kernels, near_scores(): pl.pallas_call(functools.partial(near_kernel, leaves, heads, slice_rows),...  0.99 us
  transfers between devices with their start and end apart: 15, of which 10 were waited for; matrix products, arithmetic and copies ran while one was open for 9% of the time, Pallas kernels for 8%

profile of v7, /device:TPU:0, one launch (start us, length us, event | category | flops | bytes accessed | tf_op | source)
XLA Modules:
  0.0 43.9 jit_solution(12695237138658377113)
XLA Ops:
  0.6 4.1 %collective-permute-start.1 = (bf16[1,48,576]{2,1,0:T(8,128)(2,1)}, bf16[1,48,576]{2,1,0:T(8,128)(2,1)S(1)}, u32[]{:S(2)}, u32[]{:S(2)}) collective-permute-start(bf16[1,48,576]{2,1,0:T(8,128)(2,1)} %refs_0_.1), channel_id=1, source_target_pairs={{0,16},{1,5},{2,18},{3,7},{4,20},{5,1},{6,22},{7,3},{8,24},{9,13},... | collective-permute-start | bytes 165896 | tf_op jit(solution)/shard_map/ppermute | solution.py:383
  4.8 1.3 %collective-permute-start = (bf16[1,48,576]{2,1,0:T(8,128)(2,1)}, bf16[1,48,576]{2,1,0:T(8,128)(2,1)S(1)}, u32[]{:S(2)}, u32[]{:S(2)}) collective-permute-start(bf16[1,48,576]{2,1,0:T(8,128)(2,1)} %refs_0_.1), channel_id=1, source_target_pairs={{0,24},{1,7},{2,26},{3,5},{4,28},{5,3},{6,30},{7,1},{8,16},{9,15},... | collective-permute-start | bytes 165896 | tf_op jit(solution)/shard_map/ppermute | solution.py:383
  6.1 0.2 collective-permute-start.2
  6.4 0.7 %broadcast_xor_fusion = s32[2,3]{1,0:T(2,128)S(1)} fusion(s32[2,3]{1,0:T(2,128)} %param.10, s32[]{:T(128)S(6)} %axis_index.25), kind=kLoop, calls=%fused_computation.27 | loop fusion | flops 6 | bytes 52 | tf_op jit(solution)/shard_map/xor | solution.py:388
  7.1 2.2 %copy.13 = bf16[128,8,576]{2,1,0:T(8,128)(2,1)S(1)} copy(bf16[128,8,576]{0,2,1:T(8,128)(2,1)} %param.6) | data formatting | bytes 2359296 | tf_op args[0]
  9.3 1.8 %collective-permute-done.refs_1_ = bf16[1,48,576]{2,1,0:T(8,128)(2,1)S(1)} collective-permute-done((bf16[1,48,576]{2,1,0:T(8,128)(2,1)}, bf16[1,48,576]{2,1,0:T(8,128)(2,1)S(1)}, u32[]{:S(2)}, u32[]{:S(2)}) %collective-permute-start) | collective-permute-done | bytes 55328 | tf_op jit(solution)/shard_map/ppermute | solution.py:383
  11.3 2.5 %collective-permute-start.5 = (bf16[4,216,128]{2,1,0:T(8,128)(2,1)S(1)}, bf16[4,216,128]{2,1,0:T(8,128)(2,1)S(1)}, u32[]{:S(2)}, u32[]{:S(2)}) collective-permute-start(bf16[4,216,128]{2,1,0:T(8,128)(2,1)S(1)} %pack_nodes.1), channel_id=1, source_target_pairs={{0,6},{1,25},{2,4},{3,27},{4,2},{5,29},{6,0},{7,31},{8,14},{9,17},... | collective-permute-start | bytes 663560 | tf_op jit(solution)/shard_map/ppermute | solution.py:383
  13.8 0.5 %collective-permute-start.4 = (bf16[4,216,128]{2,1,0:T(8,128)(2,1)S(1)}, bf16[4,216,128]{2,1,0:T(8,128)(2,1)S(1)}, u32[]{:S(2)}, u32[]{:S(2)}) collective-permute-start(bf16[4,216,128]{2,1,0:T(8,128)(2,1)S(1)} %pack_nodes.1), channel_id=1, source_target_pairs={{0,2},{1,9},{2,0},{3,11},{4,6},{5,13},{6,4},{7,15},{8,10},{9,1},{1... | collective-permute-start | bytes 663560 | tf_op jit(solution)/shard_map/ppermute | solution.py:383
  14.3 0.5 %collective-permute-start.3 = (bf16[4,216,128]{2,1,0:T(8,128)(2,1)S(1)}, bf16[4,216,128]{2,1,0:T(8,128)(2,1)S(1)}, u32[]{:S(2)}, u32[]{:S(2)}) collective-permute-start(bf16[4,216,128]{2,1,0:T(8,128)(2,1)S(1)} %pack_nodes.1), channel_id=1, source_target_pairs={{0,4},{1,17},{2,6},{3,19},{4,0},{5,21},{6,2},{7,23},{8,12},{9,25},... | collective-permute-start | bytes 663560 | tf_op jit(solution)/shard_map/ppermute | solution.py:383
  14.9 3.3 %collective-permute-done.5 = bf16[4,216,128]{2,1,0:T(8,128)(2,1)S(1)} collective-permute-done((bf16[4,216,128]{2,1,0:T(8,128)(2,1)S(1)}, bf16[4,216,128]{2,1,0:T(8,128)(2,1)S(1)}, u32[]{:S(2)}, u32[]{:S(2)}) %collective-permute-start.5) | collective-permute-done | bytes 221216 | tf_op jit(solution)/shard_map/ppermute | solution.py:383
  18.2 2.4 %collective-permute-done.4 = bf16[4,216,128]{2,1,0:T(8,128)(2,1)S(1)} collective-permute-done((bf16[4,216,128]{2,1,0:T(8,128)(2,1)S(1)}, bf16[4,216,128]{2,1,0:T(8,128)(2,1)S(1)}, u32[]{:S(2)}, u32[]{:S(2)}) %collective-permute-start.4) | collective-permute-done | bytes 221216 | tf_op jit(solution)/shard_map/ppermute | solution.py:383
  20.9 0.2 collective-permute-start.6
  21.4 1.0 %near_scores.1 = (f32[2,208,512]{2,1,0:T(8,128)S(1)}, f32[2,208,512]{2,1,0:T(8,128)S(1)}, f32[2,1,512]{2,1,0:T(1,128)S(1)}, f32[2,1,512]{2,1,0:T(1,128)S(1)}, f3...) custom-call(bf16[6,216,128]{2,1,0:T(8,128)(2,1)S(1)} %select_nodes.1.part_ref, ...), custom_call_target="tpu_custom_call" | custom-call | flops 490733568 | bytes 4194304 | tf_op jit(solution)/shard_map/near_scores/pallas_call | solution.py:150
  22.6 1.6 %attend.1 = (bf16[6,216,128]{2,1,0:T(8,128)(2,1)S(1)}, f32[2,1,512]{2,1,0:T(1,128)S(1)}, f32[2,1,512]{2,1,0:T(1,128)S(1)}, bf16[2,144,512]{2,1,0:T(8,128)(2,1)S(1)}, bf16[2,144,576]{2,1,0:T(8,128)(2,1)S(1)}) custom-call(f32[2,1,512]{2,1,0:T(1,128)S(1)} %compare_convert_fusion.live_ref, bf16[1024,576]{1,0:T(8,128)(2,1)S(1)} %bitcast.4, ...), custom_call_target="tpu_custom_call" | custom-call | flops 679477248 | bytes 8388608 | tf_op jit(solution)/shard_map/attend/pallas_call | solution.py:207
  24.2 0.2 collective-permute-start.7
  24.4 0.8 %own_terms.1 = (f32[6,216,128]{2,1,0:T(8,128)S(1)}, bf16[128,576]{1,0:T(8,128)(2,1)S(1)}, bf16[2,208,512]{2,1,0:T(8,128)(2,1)S(1)}, bf16[4,216,128]{2,1,0:T(8,12...) custom-call(bf16[1024,576]{1,0:T(8,128)(2,1)S(1)} %bitcast.5, ...), custom_call_target="tpu_custom_call" | custom-call | flops 490733568 | bytes 4194304 | tf_op jit(solution)/shard_map/own_terms/pallas_call | solution.py:248
  25.2 0.6 %collective-permute-done.7.refs_1_ = bf16[6,216,128]{2,1,0:T(8,128)(2,1)S(1)} collective-permute-done((bf16[6,216,128]{2,1,0:T(8,128)(2,1)S(1)}, bf16[6,216,128]{2,1,0:T(8,128)(2,1)S(1)}, u32[]{:S(2)}, u32[]{:S(2)}) %collective-permute-start.7) | collective-permute-done | bytes 331808 | tf_op jit(solution)/shard_map/ppermute | solution.py:386
  25.9 0.5 %spread_terms.1 = (bf16[4,216,128]{2,1,0:T(8,128)(2,1)S(1)}, bf16[4,216,128]{2,1,0:T(8,128)(2,1)S(1)}, bf16[4,216,128]{2,1,0:T(8,128)(2,1)S(1)}, bf16[4,216,128]{2,1,0:T(8,128)(2,1)S(1)}) custom-call(s32[1,6]{1,0:T(1,128)S(1)} %get-tuple-element.91.where_ref, ...), custom_call_target="tpu_custom_call", output_to_operand_aliasing={{0}: (3, {}), {1}: (4, {}), {2}: (5, {}), {3}: (6, {})} | custom-call | tf_op jit(solution)/shard_map/spread_terms/pallas_call | solution.py:312
  26.4 2.5 %collective-permute-start.8 = (bf16[4,216,128]{2,1,0:T(8,128)(2,1)S(1)}, bf16[4,216,128]{2,1,0:T(8,128)(2,1)S(1)}, u32[]{:S(2)}, u32[]{:S(2)}) collective-permute-start(bf16[4,216,128]{2,1,0:T(8,128)(2,1)S(1)} %get-tuple-element.70), channel_id=1, source_target_pairs={{0,6},{1,25},{2,4},{3,27},{4,2},{5,29},{6,0},{7,31},{8,14},{9,17},... | collective-permute-start | bytes 663560 | tf_op jit(solution)/shard_map/ppermute | solution.py:383
  28.8 0.5 %collective-permute-start.9 = (bf16[4,216,128]{2,1,0:T(8,128)(2,1)S(1)}, bf16[4,216,128]{2,1,0:T(8,128)(2,1)S(1)}, u32[]{:S(2)}, u32[]{:S(2)}) collective-permute-start(bf16[4,216,128]{2,1,0:T(8,128)(2,1)S(1)} %get-tuple-element.71), channel_id=1, source_target_pairs={{0,2},{1,9},{2,0},{3,11},{4,6},{5,13},{6,4},{7,15},{8,10},{9,1},{1... | collective-permute-start | bytes 663560 | tf_op jit(solution)/shard_map/ppermute | solution.py:383
  29.4 0.6 %collective-permute-start.10 = (bf16[4,216,128]{2,1,0:T(8,128)(2,1)S(1)}, bf16[4,216,128]{2,1,0:T(8,128)(2,1)S(1)}, u32[]{:S(2)}, u32[]{:S(2)}) collective-permute-start(bf16[4,216,128]{2,1,0:T(8,128)(2,1)S(1)} %get-tuple-element.72), channel_id=1, source_target_pairs={{0,4},{1,17},{2,6},{3,19},{4,0},{5,21},{6,2},{7,23},{8,12},{9,25},... | collective-permute-start | bytes 663560 | tf_op jit(solution)/shard_map/ppermute | solution.py:383
  29.9 0.2 collective-permute-start.14
  30.2 1.7 %attend_outputs.1 = bf16[1024,512]{1,0:T(8,128)(2,1)} custom-call(bf16[2,144,512]{2,1,0:T(8,128)(2,1)S(1)} %get-tuple-element.73.probs_ref, bf16[2,144,576]{2,1,0:T(8,128)(2,1)S(1)} %get-tuple-element.74.keys_ref, bf16[2,208,512]{2,1,0:T(8,128)(2,1)S(1)} %get-tuple-element.75.near_probs_ref, bf16[2,208,576]{2,1,0:T(8,128)(2,1)S(1)} %get-tuple-element.76.near_keys_ref), custom_call_target="tpu_custom_call" | custom-call | flops 369098752 | bytes 4194304 | tf_op jit(solution)/shard_map/attend_outputs/pallas_call | solution.py:271
  31.9 1.4 %collective-permute-done.8.refs_1_ = bf16[4,216,128]{2,1,0:T(8,128)(2,1)S(1)} collective-permute-done((bf16[4,216,128]{2,1,0:T(8,128)(2,1)S(1)}, bf16[4,216,128]{2,1,0:T(8,128)(2,1)S(1)}, u32[]{:S(2)}, u32[]{:S(2)}) %collective-permute-start.8) | collective-permute-done | bytes 221216 | tf_op jit(solution)/shard_map/ppermute | solution.py:383
  33.3 2.3 %collective-permute-done.9.refs_2_ = bf16[4,216,128]{2,1,0:T(8,128)(2,1)S(1)} collective-permute-done((bf16[4,216,128]{2,1,0:T(8,128)(2,1)S(1)}, bf16[4,216,128]{2,1,0:T(8,128)(2,1)S(1)}, u32[]{:S(2)}, u32[]{:S(2)}) %collective-permute-start.9) | collective-permute-done | bytes 221216 | tf_op jit(solution)/shard_map/ppermute | solution.py:383
  35.8 1.4 %collective-permute-start.11 = (bf16[1,216,128]{2,1,0:T(8,128)(2,1)S(1)}, bf16[1,216,128]{2,1,0:T(8,128)(2,1)S(1)}, u32[]{:S(2)}, u32[]{:S(2)}) collective-permute-start(bf16[1,216,128]{2,1,0:T(8,128)(2,1)S(1)} %get-tuple-element.83), channel_id=1, source_target_pairs={{0,16},{1,5},{2,18},{3,7},{4,20},{5,1},{6,22},{7,3},{8,24},{9,13},... | collective-permute-start | bytes 165896 | tf_op jit(solution)/shard_map/ppermute | solution.py:383
  37.2 1.0 %collective-permute-start.12 = (bf16[1,216,128]{2,1,0:T(8,128)(2,1)S(1)}, bf16[1,216,128]{2,1,0:T(8,128)(2,1)S(1)}, u32[]{:S(2)}, u32[]{:S(2)}) collective-permute-start(bf16[1,216,128]{2,1,0:T(8,128)(2,1)S(1)} %get-tuple-element.84), channel_id=1, source_target_pairs={{0,24},{1,7},{2,26},{3,5},{4,28},{5,3},{6,30},{7,1},{8,16},{9,15},... | collective-permute-start | bytes 165896 | tf_op jit(solution)/shard_map/ppermute | solution.py:383
  38.2 1.1 %collective-permute-start.13 = (bf16[1,216,128]{2,1,0:T(8,128)(2,1)S(1)}, bf16[1,216,128]{2,1,0:T(8,128)(2,1)S(1)}, u32[]{:S(2)}, u32[]{:S(2)}) collective-permute-start(bf16[1,216,128]{2,1,0:T(8,128)(2,1)S(1)} %get-tuple-element.85), channel_id=1, source_target_pairs={{0,8},{1,3},{2,10},{3,1},{4,12},{5,7},{6,14},{7,5},{8,0},{9,11},{1... | collective-permute-start | bytes 165896 | tf_op jit(solution)/shard_map/ppermute | solution.py:383
  39.4 0.8 %copy.15 = bf16[128,576]{0,1:T(8,128)(2,1)} copy(bf16[128,576]{1,0:T(8,128)(2,1)S(1)} %add.127) | data formatting | bytes 294912
  40.2 0.7 %collective-permute-done.11.refs_0_ = bf16[1,216,128]{2,1,0:T(8,128)(2,1)S(1)} collective-permute-done((bf16[1,216,128]{2,1,0:T(8,128)(2,1)S(1)}, bf16[1,216,128]{2,1,0:T(8,128)(2,1)S(1)}, u32[]{:S(2)}, u32[]{:S(2)}) %collective-permute-start.11) | collective-permute-done | bytes 55328 | tf_op jit(solution)/shard_map/ppermute | solution.py:383
  40.9 2.2 %collective-permute-done.12.refs_1_ = bf16[1,216,128]{2,1,0:T(8,128)(2,1)S(1)} collective-permute-done((bf16[1,216,128]{2,1,0:T(8,128)(2,1)S(1)}, bf16[1,216,128]{2,1,0:T(8,128)(2,1)S(1)}, u32[]{:S(2)}, u32[]{:S(2)}) %collective-permute-start.12) | collective-permute-done | bytes 55328 | tf_op jit(solution)/shard_map/ppermute | solution.py:383
  43.2 0.7 %finish_nodes.1 = bf16[1,48,576]{2,1,0:T(8,128)(2,1)} custom-call(f32[1,216,128]{2,1,0:T(8,128)S(1)} %get-tuple-element.82.keep_ref, bf16[1,216,128]{2,1,0:T(8,128)(2,1)S(1)} %collective-permute-done.11.refs_0_, bf16[1,216,128]{2,1,0:T(8,128)(2,1)S(1)} %collective-permute-done.12.refs_1_, bf16[1,216,128]{2,1,0:T(8,128)(2,1)S(1)} %collective-permute-done.13.refs_2_), custom_call_target="tpu_custom_call" | custom-call | tf_op jit(solution)/shard_map/finish_nodes/pallas_call | solution.py:358
  (25 shorter events, 1.2 us)
Async XLA Ops:
  0.6 10.6 %copy-start.1 = (bf16[1,48,576]{2,1,0:T(8,128)(2,1)S(1)}, bf16[1,48,576]{2,1,0:T(8,128)(2,1)}, u32[]{:S(2)}) copy-start(bf16[1,48,576]{2,1,0:T(8,128)(2,1)} %refs_0_.1) | copy-start | bytes 165892
  0.6 8.7 %collective-permute-start.1 = (bf16[1,48,576]{2,1,0:T(8,128)(2,1)}, bf16[1,48,576]{2,1,0:T(8,128)(2,1)S(1)}, u32[]{:S(2)}, u32[]{:S(2)}) collective-permute-start(bf16[1,48,576]{2,1,0:T(8,128)(2,1)} %refs_0_.1), channel_id=1, source_target_pairs={{0,16},{1,5},{2,18},{3,7},{4,20},{5,1},{6,22},{7,3},{8,24},{9,13},... | collective-permute-start | bytes 165896 | tf_op jit(solution)/shard_map/ppermute | solution.py:383
  4.8 6.3 %collective-permute-start = (bf16[1,48,576]{2,1,0:T(8,128)(2,1)}, bf16[1,48,576]{2,1,0:T(8,128)(2,1)S(1)}, u32[]{:S(2)}, u32[]{:S(2)}) collective-permute-start(bf16[1,48,576]{2,1,0:T(8,128)(2,1)} %refs_0_.1), channel_id=1, source_target_pairs={{0,24},{1,7},{2,26},{3,5},{4,28},{5,3},{6,30},{7,1},{8,16},{9,15},... | collective-permute-start | bytes 165896 | tf_op jit(solution)/shard_map/ppermute | solution.py:383
  6.1 5.1 %collective-permute-start.2 = (bf16[1,48,576]{2,1,0:T(8,128)(2,1)}, bf16[1,48,576]{2,1,0:T(8,128)(2,1)S(1)}, u32[]{:S(2)}, u32[]{:S(2)}) collective-permute-start(bf16[1,48,576]{2,1,0:T(8,128)(2,1)} %refs_0_.1), channel_id=1, source_target_pairs={{0,8},{1,3},{2,10},{3,1},{4,12},{5,7},{6,14},{7,5},{8,0},{9,11},{1... | collective-permute-start | bytes 165896 | tf_op jit(solution)/shard_map/ppermute | solution.py:383
  11.3 6.9 %collective-permute-start.5 = (bf16[4,216,128]{2,1,0:T(8,128)(2,1)S(1)}, bf16[4,216,128]{2,1,0:T(8,128)(2,1)S(1)}, u32[]{:S(2)}, u32[]{:S(2)}) collective-permute-start(bf16[4,216,128]{2,1,0:T(8,128)(2,1)S(1)} %pack_nodes.1), channel_id=1, source_target_pairs={{0,6},{1,25},{2,4},{3,27},{4,2},{5,29},{6,0},{7,31},{8,14},{9,17},... | collective-permute-start | bytes 663560 | tf_op jit(solution)/shard_map/ppermute | solution.py:383
  13.8 6.8 %collective-permute-start.4 = (bf16[4,216,128]{2,1,0:T(8,128)(2,1)S(1)}, bf16[4,216,128]{2,1,0:T(8,128)(2,1)S(1)}, u32[]{:S(2)}, u32[]{:S(2)}) collective-permute-start(bf16[4,216,128]{2,1,0:T(8,128)(2,1)S(1)} %pack_nodes.1), channel_id=1, source_target_pairs={{0,2},{1,9},{2,0},{3,11},{4,6},{5,13},{6,4},{7,15},{8,10},{9,1},{1... | collective-permute-start | bytes 663560 | tf_op jit(solution)/shard_map/ppermute | solution.py:383
  14.3 6.3 %collective-permute-start.3 = (bf16[4,216,128]{2,1,0:T(8,128)(2,1)S(1)}, bf16[4,216,128]{2,1,0:T(8,128)(2,1)S(1)}, u32[]{:S(2)}, u32[]{:S(2)}) collective-permute-start(bf16[4,216,128]{2,1,0:T(8,128)(2,1)S(1)} %pack_nodes.1), channel_id=1, source_target_pairs={{0,4},{1,17},{2,6},{3,19},{4,0},{5,21},{6,2},{7,23},{8,12},{9,25},... | collective-permute-start | bytes 663560 | tf_op jit(solution)/shard_map/ppermute | solution.py:383
  14.9 6.2 %copy-start.3 = (s32[2]{0:T(128)S(1)}, s32[2]{0:T(128)}, u32[]{:S(2)}) copy-start(s32[2]{0:T(128)} %param.11) | copy-start | bytes 28
  14.9 6.3 %copy-start.2 = (bf16[128,576]{0,1:T(8,128)(2,1)S(1)}, bf16[128,576]{0,1:T(8,128)(2,1)}, u32[]{:S(2)}) copy-start(bf16[128,576]{0,1:T(8,128)(2,1)} %param.7) | copy-start | bytes 442372
  14.9 6.5 %copy-start = (bf16[128,8,512]{2,1,0:T(8,128)(2,1)S(1)}, bf16[128,8,512]{2,1,0:T(8,128)(2,1)}, u32[]{:S(2)}) copy-start(bf16[128,8,512]{2,1,0:T(8,128)(2,1)} %param.9) | copy-start | bytes 3145732
  20.9 1.7 %collective-permute-start.6 = (bf16[6,216,128]{2,1,0:T(8,128)(2,1)S(1)}, bf16[6,216,128]{2,1,0:T(8,128)(2,1)S(1)}, u32[]{:S(2)}, u32[]{:S(2)}) collective-permute-start(bf16[6,216,128]{2,1,0:T(8,128)(2,1)S(1)} %select_nodes.1.part_ref), channel_id=1, source_target_pairs={{0,1},{1,0},{2,3},{3,2},{4,5},{5,4},{6,7},{7,6},{8,9},{9,8},{10,11... | collective-permute-start | bytes 995336 | tf_op jit(solution)/shard_map/ppermute | solution.py:386
  24.2 1.7 %collective-permute-start.7 = (bf16[6,216,128]{2,1,0:T(8,128)(2,1)S(1)}, bf16[6,216,128]{2,1,0:T(8,128)(2,1)S(1)}, u32[]{:S(2)}, u32[]{:S(2)}) collective-permute-start(bf16[6,216,128]{2,1,0:T(8,128)(2,1)S(1)} %get-tuple-element.58), channel_id=1, source_target_pairs={{0,1},{1,0},{2,3},{3,2},{4,5},{5,4},{6,7},{7,6},{8,9},{9,8},{10,11... | collective-permute-start | bytes 995336 | tf_op jit(solution)/shard_map/ppermute | solution.py:386
  26.4 6.9 %collective-permute-start.8 = (bf16[4,216,128]{2,1,0:T(8,128)(2,1)S(1)}, bf16[4,216,128]{2,1,0:T(8,128)(2,1)S(1)}, u32[]{:S(2)}, u32[]{:S(2)}) collective-permute-start(bf16[4,216,128]{2,1,0:T(8,128)(2,1)S(1)} %get-tuple-element.70), channel_id=1, source_target_pairs={{0,6},{1,25},{2,4},{3,27},{4,2},{5,29},{6,0},{7,31},{8,14},{9,17},... | collective-permute-start | bytes 663560 | tf_op jit(solution)/shard_map/ppermute | solution.py:383
  28.8 6.8 %collective-permute-start.9 = (bf16[4,216,128]{2,1,0:T(8,128)(2,1)S(1)}, bf16[4,216,128]{2,1,0:T(8,128)(2,1)S(1)}, u32[]{:S(2)}, u32[]{:S(2)}) collective-permute-start(bf16[4,216,128]{2,1,0:T(8,128)(2,1)S(1)} %get-tuple-element.71), channel_id=1, source_target_pairs={{0,2},{1,9},{2,0},{3,11},{4,6},{5,13},{6,4},{7,15},{8,10},{9,1},{1... | collective-permute-start | bytes 663560 | tf_op jit(solution)/shard_map/ppermute | solution.py:383
  29.4 6.3 %collective-permute-start.10 = (bf16[4,216,128]{2,1,0:T(8,128)(2,1)S(1)}, bf16[4,216,128]{2,1,0:T(8,128)(2,1)S(1)}, u32[]{:S(2)}, u32[]{:S(2)}) collective-permute-start(bf16[4,216,128]{2,1,0:T(8,128)(2,1)S(1)} %get-tuple-element.72), channel_id=1, source_target_pairs={{0,4},{1,17},{2,6},{3,19},{4,0},{5,21},{6,2},{7,23},{8,12},{9,25},... | collective-permute-start | bytes 663560 | tf_op jit(solution)/shard_map/ppermute | solution.py:383
  29.9 9.4 %collective-permute-start.14 = (bf16[128,576]{1,0:T(8,128)(2,1)S(1)}, bf16[128,576]{1,0:T(8,128)(2,1)S(1)}, u32[]{:S(2)}, u32[]{:S(2)}) collective-permute-start(bf16[128,576]{1,0:T(8,128)(2,1)S(1)} %get-tuple-element.86), channel_id=1, source_target_pairs={{0,1},{1,0},{2,3},{3,2},{4,5},{5,4},{6,7},{7,6},{8,9},{9,8},{10,11... | collective-permute-start | bytes 442376 | tf_op jit(solution)/shard_map/ppermute | solution.py:386
  35.8 5.2 %collective-permute-start.11 = (bf16[1,216,128]{2,1,0:T(8,128)(2,1)S(1)}, bf16[1,216,128]{2,1,0:T(8,128)(2,1)S(1)}, u32[]{:S(2)}, u32[]{:S(2)}) collective-permute-start(bf16[1,216,128]{2,1,0:T(8,128)(2,1)S(1)} %get-tuple-element.83), channel_id=1, source_target_pairs={{0,16},{1,5},{2,18},{3,7},{4,20},{5,1},{6,22},{7,3},{8,24},{9,13},... | collective-permute-start | bytes 165896 | tf_op jit(solution)/shard_map/ppermute | solution.py:383
  37.2 6.0 %collective-permute-start.12 = (bf16[1,216,128]{2,1,0:T(8,128)(2,1)S(1)}, bf16[1,216,128]{2,1,0:T(8,128)(2,1)S(1)}, u32[]{:S(2)}, u32[]{:S(2)}) collective-permute-start(bf16[1,216,128]{2,1,0:T(8,128)(2,1)S(1)} %get-tuple-element.84), channel_id=1, source_target_pairs={{0,24},{1,7},{2,26},{3,5},{4,28},{5,3},{6,30},{7,1},{8,16},{9,15},... | collective-permute-start | bytes 165896 | tf_op jit(solution)/shard_map/ppermute | solution.py:383
  38.2 5.0 %collective-permute-start.13 = (bf16[1,216,128]{2,1,0:T(8,128)(2,1)S(1)}, bf16[1,216,128]{2,1,0:T(8,128)(2,1)S(1)}, u32[]{:S(2)}, u32[]{:S(2)}) collective-permute-start(bf16[1,216,128]{2,1,0:T(8,128)(2,1)S(1)} %get-tuple-element.85), channel_id=1, source_target_pairs={{0,8},{1,3},{2,10},{3,1},{4,12},{5,7},{6,14},{7,5},{8,0},{9,11},{1... | collective-permute-start | bytes 165896 | tf_op jit(solution)/shard_map/ppermute | solution.py:383
